TPU v7x, 768 devices: a whole 4x8x12 slice. The times are simulated.
768 devices in a mesh: rep: 32 (over x, y_hi, core), shard: 24 (over y_lo, z).
Axes of the slice: x: 4, y: 8 (y_hi: 4, y_lo: 2; y = y_hi * 2 + y_lo), z: 12, core: 2. Of those that a mesh axis runs over, the one named last changes fastest.
Arguments:
- tokens: bfloat16 [294912, 1536], P(('rep', 'shard')), may hold values from -16 to 16
- patch_mask: int32 [294912], P(('rep', 'shard')), may hold values 0 or 1
- mask_token: bfloat16 [1536], replicated, may hold values from -5 to 5
- student_w: float32 [1536, 768], P('shard'), may hold values from -0.15625 to 0.15625
- teacher_w: float32 [1536, 768], P('shard'), may hold values from -0.15625 to 0.15625
- first_moment: float32 [1536, 768], P('shard'), may hold values from -0.21875 to 0.21875
- second_moment: float32 [1536, 768], P('shard'), may hold values from 2e-05 to 0.0002
Outputs:
- teacher_feat: bfloat16 [294912, 768], P(('rep', 'shard'))
- student_new: float32 [1536, 768], P('shard')
- teacher_new: float32 [1536, 768], P('shard')
- first_new: float32 [1536, 768], P('shard')
- second_new: float32 [1536, 768], P('shard')
- step_direction: float32 [1536, 768], P('shard')
All inputs are finite; a program needn't handle non-finite values. No bound on the sum of `patch_mask` on one device may be relied on, other than what follows from the above.
Results may differ from a plain program's by a relative error of at most 0.0049.
Values may be sent and summed in bfloat16 or wider, within the bound.
No kernel may reach another device: no remote copies, remote signals or barrier semaphores. Data moves between devices by JAX's collectives and lax.ppermute only.
A program may use at most 32 MiB of HBM per device.

v0:
```python
import jax
import jax.numpy as jnp
from jax import lax
from jax.sharding import PartitionSpec as P

STEP = 100


beta_one = 0.9
beta_two = 0.999
adam_eps = 1e-08
learn_rate = 0.0002
decay_rate = 0.04
ema_keep = 0.994


def adamw_update(gradient, weights, teacher, moment_one, moment_two):
    first_new = beta_one * moment_one + (1.0 - beta_one) * gradient
    second_new = beta_two * moment_two + (1.0 - beta_two) * gradient * gradient
    fix_one = 1.0 - beta_one**STEP
    fix_two = 1.0 - beta_two**STEP
    direction = first_new / fix_one / (jnp.sqrt(second_new / fix_two) + adam_eps)
    student_new = weights - learn_rate * (direction + decay_rate * weights)
    teacher_new = ema_keep * teacher + (1.0 - ema_keep) * student_new
    return (student_new, teacher_new, first_new, second_new, direction)


def add_rows(inputs, shard_piece):
    return jnp.dot(inputs, shard_piece, preferred_element_type=jnp.float32)


def shards(tokens, patch_mask, mask_token, student_w, teacher_w, first_moment, second_moment):
    student_in = jnp.where(patch_mask[:, None] == 1, mask_token[None, :], tokens)
    student_half = student_w.astype(jnp.bfloat16)
    teacher_half = teacher_w.astype(jnp.bfloat16)
    teacher_out = add_rows(tokens, lax.all_gather(teacher_half, "shard", axis=0, tiled=True))
    student_out = add_rows(student_in, lax.all_gather(student_half, "shard", axis=0, tiled=True))
    teacher_feat = teacher_out.astype(jnp.bfloat16)
    difference = (student_out - teacher_feat.astype(jnp.float32)).astype(jnp.bfloat16)
    local_grad = lax.dot_general(
        student_in, difference, (((0,), (0,)), ((), ())), preferred_element_type=jnp.float32
    )
    shard_count = lax.axis_size("shard")
    replica_count = lax.axis_size("rep")
    row_total = float(tokens.shape[0] * shard_count * replica_count)
    shard_sum = lax.psum_scatter(local_grad, "shard", scatter_dimension=0, tiled=True)
    gradient = lax.psum(shard_sum, "rep") / row_total
    student_new, teacher_new, first_new, second_new, direction = adamw_update(
        gradient, student_w, teacher_w, first_moment, second_moment
    )
    return (teacher_feat, student_new, teacher_new, first_new, second_new, direction)


def solution(mesh):
    return jax.shard_map(
        shards,
        mesh=mesh,
        in_specs=(
            P(("rep", "shard"), None),
            P(("rep", "shard")),
            P(),
            P("shard", None),
            P("shard", None),
            P("shard", None),
            P("shard", None),
        ),
        out_specs=(
            P(("rep", "shard"), None),
            P("shard", None),
            P("shard", None),
            P("shard", None),
            P("shard", None),
            P("shard", None),
        ),
        check_vma=False,
    )
```

profile of v0, /device:TPU:1, one launch (start us, length us, event | category | flops | bytes accessed | tf_op | source)
XLA Modules:
  0.0 639.5 jit_solution(7458415331791210168)
XLA Ops:
  7.2 0.0 all-gather.3.cloned.1.call-start
  7.2 1.6 convert_element_type.15
  8.8 0.0 all-gather.3.cloned.1.call-update
  8.8 0.0 all-gather.5.cloned.1.call-start
  8.9 1.6 convert_element_type.17
  10.5 0.0 all-gather.5.cloned.1.call-update
  10.5 0.0 reduce-scatter.2.cloned.1.call-start
  10.5 0.7 broadcast_compare_fusion
  11.2 0.0 copy-start.4
  11.2 0.0 copy-start.5
  11.2 98.1 %all-gather.3.cloned.1.call-done = bf16[1536,768]{1,0:T(8,128)(2,1)} async-done(((bf16[64,768]{1,0:T(8,128)(2,1)}), bf16[1536,768]{1,0:T(8,128)(2,1)}) %all-gather.3.cloned.1.call-update) | async-done | bytes 2359312 | tf_op jit(solution)/shard_map/all_gather | solution.py:36
  109.3 3.1 convolution_convert_fusion
  112.4 0.0 copy-start.6
  112.4 101.4 %all-gather.5.cloned.1.call-done = bf16[1536,768]{1,0:T(8,128)(2,1)} async-done(((bf16[64,768]{1,0:T(8,128)(2,1)}), bf16[1536,768]{1,0:T(8,128)(2,1)}) %all-gather.5.cloned.1.call-update) | async-done | bytes 2359312 | tf_op jit(solution)/shard_map/all_gather | solution.py:37
  213.9 0.0 copy-done.4
  213.9 0.0 copy-done.5
  213.9 6.4 fusion.1
  220.2 0.0 copy-done.6
  220.2 0.0 copy-start
  220.2 0.0 copy-start.1
  220.3 0.0 copy-start.2
  220.3 0.0 copy-start.3
  220.3 0.0 reduce-scatter.2.cloned.1.call-update
  220.3 0.0 all-reduce.2.cloned.1.call-start
  220.3 114.7 %reduce-scatter.2.cloned.1.call-done = f32[64,768]{1,0:T(8,128)} async-done(((f32[1536,768]{1,0:T(8,128)}), f32[64,768]{1,0:T(8,128)}) %reduce-scatter.2.cloned.1.call-update) | async-done | bytes 196624 | tf_op jit(solution)/shard_map/reduce_scatter | solution.py:46
  335.0 0.0 all-reduce.2.cloned.1.call-update
  335.0 296.0 %all-reduce.2.cloned.1.call-done = f32[64,768]{1,0:T(8,128)} async-done(((f32[64,768]{1,0:T(8,128)}), f32[64,768]{1,0:T(8,128)}) %all-reduce.2.cloned.1.call-update) | async-done | bytes 196624 | tf_op jit(solution)/shard_map/psum | solution.py:47
  631.0 0.0 copy-done
  631.0 0.0 copy-done.1
  631.0 0.0 copy-done.2
  631.0 0.0 copy-done.3
  631.0 2.0 multiply_add_fusion
Async XLA Ops:
  7.2 102.1 %all-gather.3.cloned.1.call-start = ((), (), s32[]{:S(2)}) async-start(), calls=%async_computation.1 | async-start | bytes 2457600 | tf_op jit(solution)/shard_map/all_gather | solution.py:36
  8.8 205.1 %all-gather.5.cloned.1.call-start = ((), (), s32[]{:S(2)}) async-start(), calls=%async_computation.2 | async-start | bytes 2457600 | tf_op jit(solution)/shard_map/all_gather | solution.py:37
  10.5 324.5 %reduce-scatter.2.cloned.1.call-start = ((), (), s32[]{:S(2)}) async-start(), calls=%async_computation.3 | async-start | bytes 4915200 | tf_op jit(solution)/shard_map/reduce_scatter | solution.py:46
  11.2 202.7 %copy-start.4 = (bf16[384,1536]{1,0:T(8,128)(2,1)S(1)}, bf16[384,1536]{1,0:T(8,128)(2,1)}, u32[]{:S(2)}) copy-start(bf16[384,1536]{1,0:T(8,128)(2,1)} %param.7) | copy-start | bytes 3538948
  11.2 202.7 %copy-start.5 = (bf16[1536]{0:T(1024)(128)(2,1)S(1)}, bf16[1536]{0:T(1024)(128)(2,1)}, u32[]{:S(2)}) copy-start(bf16[1536]{0:T(1024)(128)(2,1)} %param.9) | copy-start | bytes 9220
  112.4 107.8 %copy-start.6 = (bf16[384,768]{1,0:T(8,128)(2,1)}, bf16[384,768]{1,0:T(8,128)(2,1)S(1)}, u32[]{:S(2)}) copy-start(bf16[384,768]{1,0:T(8,128)(2,1)S(1)} %convolution_convert_fusion) | copy-start | bytes 1769476
  220.2 410.8 %copy-start = (f32[64,768]{1,0:T(8,128)S(1)}, f32[64,768]{1,0:T(8,128)}, u32[]{:S(2)}) copy-start(f32[64,768]{1,0:T(8,128)} %param.11) | copy-start | bytes 589828
  220.2 410.8 %copy-start.1 = (f32[64,768]{1,0:T(8,128)S(1)}, f32[64,768]{1,0:T(8,128)}, u32[]{:S(2)}) copy-start(f32[64,768]{1,0:T(8,128)} %param.10) | copy-start | bytes 589828
  220.3 410.8 %copy-start.2 = (f32[64,768]{1,0:T(8,128)S(1)}, f32[64,768]{1,0:T(8,128)}, u32[]{:S(2)}) copy-start(f32[64,768]{1,0:T(8,128)} %param.12) | copy-start | bytes 589828
  220.3 410.8 %copy-start.3 = (f32[64,768]{1,0:T(8,128)S(1)}, f32[64,768]{1,0:T(8,128)}, u32[]{:S(2)}) copy-start(f32[64,768]{1,0:T(8,128)} %param.13) | copy-start | bytes 589828
  220.3 410.7 %all-reduce.2.cloned.1.call-start = ((), (), s32[]{:S(2)}) async-start(), calls=%async_computation.4 | async-start | bytes 393216 | tf_op jit(solution)/shard_map/psum | solution.py:47
Sparse Core Ops, SparseCore 0:
  10.9 98.3 all-gather.2
  112.3 101.5 all-gather.4
  220.4 114.5 reduce-scatter.1
  338.1 292.9 all-reduce.1
where the time goes:
time: 641 us; the launch traced here: 640 us
  waiting for transfers between devices  610 us (95%)
  between operations  13.8 us (2%)
  matrix products  9.47 us (1%)
    psum x1, waiting for transfers between devices, shards(): gradient = lax.psum(shard_sum, 'rep') / row_total  296 us
    reduce_scatter x1, waiting for transfers between devices, shards(): lax.psum_scatter(local_grad, 'shard', scatter_dimension=0, tiled=True)  115 us
    all_gather x1, waiting for transfers between devices, shards(): lax.all_gather(student_half, 'shard', axis=0, tiled=True)  101 us
    all_gather x1, waiting for transfers between devices, shards(): lax.all_gather(teacher_half, 'shard', axis=0, tiled=True)  98.1 us
  transfers between devices with their start and end apart: 4, of which 4 were waited for; matrix products, arithmetic and copies ran while one was open for 1% of the time, Pallas kernels for 0%

commit v1 on v0

v1 whole, which is shorter than its diff:
```python
import jax
import jax.numpy as jnp
from jax import lax
from jax.sharding import Mesh, PartitionSpec as P

STEP = 100


beta_one = 0.9
beta_two = 0.999
adam_eps = 1e-08
learn_rate = 0.0002
decay_rate = 0.04
ema_keep = 0.994

REP = ("x", "yh", "core")
SHARD = ("yl", "z")
SWAP = [(0, 1), (1, 0)]


def adamw_update(gradient, weights, teacher, moment_one, moment_two):
    first_new = beta_one * moment_one + (1.0 - beta_one) * gradient
    second_new = beta_two * moment_two + (1.0 - beta_two) * gradient * gradient
    fix_one = 1.0 - beta_one**STEP
    fix_two = 1.0 - beta_two**STEP
    direction = first_new / fix_one / (jnp.sqrt(second_new / fix_two) + adam_eps)
    student_new = weights - learn_rate * (direction + decay_rate * weights)
    teacher_new = ema_keep * teacher + (1.0 - ema_keep) * student_new
    return (student_new, teacher_new, first_new, second_new, direction)


def spread(piece, axes, members):
    copies = jnp.broadcast_to(piece[None], (members,) + piece.shape)
    return lax.all_to_all(copies, axes, 0, 0, tiled=True)


def exchange(pieces, axes):
    return lax.all_to_all(pieces, axes, 0, 0, tiled=True)


def join_halves(mine, theirs, core):
    return jnp.where(
        core == 0, jnp.concatenate([mine, theirs], 1), jnp.concatenate([theirs, mine], 1)
    )


def shards(tokens, patch_mask, mask_token, student_w, teacher_w, first_moment, second_moment):
    nx, nh, nl, nz = (lax.axis_size(a) for a in ("x", "yh", "yl", "z"))
    shard_count = nl * nz
    core = lax.axis_index("core")
    rows, width = student_w.shape
    half = width // 2
    piece_rows = rows // (nx * nh)
    row_total = float(tokens.shape[0] * shard_count * nx * nh * 2)

    place = (lax.axis_index(("x", "yh")) * piece_rows, core * half)
    cut = lambda w: lax.dynamic_slice(w, place, (piece_rows, half)).astype(jnp.bfloat16)
    piece = jnp.concatenate([cut(student_w), cut(teacher_w)], 1)
    gathered = spread(piece, SHARD, shard_count)
    gathered = lax.all_gather(gathered, "yh", axis=0)
    gathered = gathered.transpose(1, 0, 2, 3).reshape(shard_count, nh * piece_rows, width)
    gathered = spread(gathered, "x", nx)
    weights = gathered.transpose(1, 0, 2, 3).reshape(shard_count * rows, width)

    both = jnp.concatenate([tokens, lax.ppermute(tokens, "core", SWAP)], 0)
    masks = jnp.concatenate([patch_mask, lax.ppermute(patch_mask, "core", SWAP)], 0)
    student_in = jnp.where(masks[:, None] == 1, mask_token[None, :], both)
    teacher_half = jnp.dot(
        both, weights[:, half:], preferred_element_type=jnp.float32
    ).astype(jnp.bfloat16)
    student_out = jnp.dot(student_in, weights[:, :half], preferred_element_type=jnp.float32)
    difference = (student_out - teacher_half.astype(jnp.float32)).astype(jnp.bfloat16)
    local_grad = lax.dot_general(
        student_in, difference, (((0,), (0,)), ((), ())), preferred_element_type=jnp.float32
    )
    own = tokens.shape[0]
    teacher_feat = join_halves(
        teacher_half[:own], lax.ppermute(teacher_half[own:], "core", SWAP), core
    )

    grad = local_grad.astype(jnp.bfloat16).reshape(shard_count, nx, nh * piece_rows, half)
    grad = exchange(grad.transpose(1, 0, 2, 3), "x").astype(jnp.float32).sum(0)
    grad = grad.astype(jnp.bfloat16).reshape(nl, nz, nh, piece_rows, half)
    grad = grad.transpose(2, 0, 1, 3, 4).reshape(nh * nl, nz, piece_rows, half)
    grad = exchange(grad, ("yh", "yl")).astype(jnp.float32).sum(0)
    grad = exchange(grad.astype(jnp.bfloat16), "z").astype(jnp.float32).sum(0)
    grad = join_halves(grad, lax.ppermute(grad, "core", SWAP), core)
    gradient = spread(grad, ("x", "yh"), nx * nh).reshape(rows, width) / row_total
    student_new, teacher_new, first_new, second_new, direction = adamw_update(
        gradient, student_w, teacher_w, first_moment, second_moment
    )
    return (teacher_feat, student_new, teacher_new, first_new, second_new, direction)


def solution(mesh, sizes=(4, 4, 2, 2, 12)):
    fine = Mesh(mesh.devices.reshape(sizes), REP + SHARD)
    tok, row = P(REP + SHARD), P(SHARD, None)
    return jax.shard_map(
        shards,
        mesh=fine,
        in_specs=(P(REP + SHARD, None), tok, P(), row, row, row, row),
        out_specs=(P(REP + SHARD, None), row, row, row, row, row),
        check_vma=False,
    )
```

time: 641 us -> 162 us (0.25)
  waiting for transfers between devices: 610 us -> 34.5 us
  blocking collectives: 0 us -> 70.4 us
  starting transfers between devices: 0.16 us -> 34.9 us
  between operations: 13.8 us -> 0.92 us
  local copies, waits for them, and re-layouts: 0.03 us -> 9.58 us
    psum x1 -> x0, waiting for transfers between devices: 296 us -> none  [shards(): gradient = lax.psum(shard_sum, 'rep') / row_total]
    all_gather x2 -> x0, waiting for transfers between devices: 200 us -> none  [the longest x1 101 us: shards(): lax.all_gather(student_half, 'shard', axis=0, tiled=True)]
    reduce_scatter x1 -> x0, waiting for transfers between devices: 115 us -> none  [shards(): lax.psum_scatter(local_grad, 'shard', scatter_dimension=0, tiled=True)]
    all_to_all x0 -> x3, blocking collectives: none -> 53.1 us  [the longest x1 27.3 us: spread(): return lax.all_to_all(copies, axes, 0, 0, tiled=True)]
    all_to_all x0 -> x3, waiting for transfers between devices: none -> 34.5 us  [the longest x2 25 us: spread(): return lax.all_to_all(copies, axes, 0, 0, tiled=True)]
    ppermute x0 -> x4, starting transfers between devices: none -> 19.5 us  [the longest x1 9.51 us: shards(): grad = join_halves(grad, lax.ppermute(grad, 'core', SWAP), core)]
    all_gather x0 -> x1, blocking collectives: none -> 17.4 us  [shards(): gathered = lax.all_gather(gathered, 'yh', axis=0)]
    all_to_all x0 -> x3, starting transfers between devices: none -> 15.4 us  [the longest x1 7.71 us: exchange(): return lax.all_to_all(pieces, axes, 0, 0, tiled=True)]
  transfers between devices with their start and end apart: 4 -> 7, of which waited for: 4 -> 3; matrix products, arithmetic and copies ran while one was open for 1% -> 3% of each run, Pallas kernels for 0% -> 0%
where the time goes in v1:
time: 162 us; the launch traced here: 161 us
  blocking collectives  70.4 us (43%)
  starting transfers between devices  34.9 us (22%)
  waiting for transfers between devices  34.5 us (21%)
  local copies, waits for them, and re-layouts  9.58 us (6%)
  matrix products  8.51 us (5%)
  other arithmetic  2.4 us (1%)
    all_to_all x1, blocking collectives, spread(): return lax.all_to_all(copies, axes, 0, 0, tiled=True)  27.3 us
    all_to_all x2, blocking collectives, exchange(): return lax.all_to_all(pieces, axes, 0, 0, tiled=True)  25.8 us
    all_to_all x2, waiting for transfers between devices, spread(): return lax.all_to_all(copies, axes, 0, 0, tiled=True)  25 us
    all_gather x1, blocking collectives, shards(): gathered = lax.all_gather(gathered, 'yh', axis=0)  17.4 us
    ppermute x1, starting transfers between devices, shards(): grad = join_halves(grad, lax.ppermute(grad, 'core', SWAP), core)  9.51 us
    all_to_all x1, waiting for transfers between devices, exchange(): return lax.all_to_all(pieces, axes, 0, 0, tiled=True)  9.48 us
    all_to_all x1, starting transfers between devices, exchange(): return lax.all_to_all(pieces, axes, 0, 0, tiled=True)  7.71 us
    all_to_all x2, starting transfers between devices, spread(): return lax.all_to_all(copies, axes, 0, 0, tiled=True)  7.67 us
  transfers between devices with their start and end apart: 7, of which 3 were waited for; matrix products, arithmetic and copies ran while one was open for 3% of the time, Pallas kernels for 0%

profile of v1, /device:TPU:1, one launch (start us, length us, event | category | flops | bytes accessed | tf_op | source)
XLA Modules:
  0.0 161.3 jit_solution(16581844640445063191)
XLA Ops:
  0.6 0.8 dynamic_slice.10
  1.4 0.8 dynamic_slice.11
  2.3 27.3 %all_to_all.30 = bf16[24,4,768]{2,1,0:T(4,128)(2,1)S(1)} all-to-all(bf16[24,4,768]{2,1,0:T(4,128)(2,1)S(1)} %broadcast_in_dim.24), channel_id=1, replica_groups=mesh['x'=4,'yh'=4,'core'=2,'yl'=2,'z'=12] {'yl','z'}, dimensions={0} | all-to-all | bytes 294912 | tf_op jit(solution)/shard_map/all_to_all | solution.py:34
  29.6 17.4 %all-gather = bf16[96,4,768]{2,0,1:T(8,128)(2,1)S(1)} all-gather(bf16[24,4,768]{2,0,1:T(8,128)(2,1)S(1)} %copy.29), channel_id=2, replica_groups=mesh['x'=4,'yh'=4,'core'=2,'yl'=2,'z'=12] {'yh'}, dimensions={0}, use_global_device_ids=true | all-gather | bytes 737280 | tf_op jit(solution)/shard_map/all_gather | solution.py:60
  47.0 0.1 copy.31
  47.1 1.6 broadcast_in_dim.39
  48.7 4.1 %all-to-all-start.1 = ((bf16[4,24,16,768]{3,2,1,0:T(8,128)(2,1)}), bf16[4,24,16,768]{3,2,1,0:T(8,128)(2,1)S(1)}, u32[]{:S(2)}, u32[]{:S(2)}) async-start(bf16[4,24,16,768]{3,2,1,0:T(8,128)(2,1)} %broadcast_in_dim.39), calls=%async_computation.1 | async-start | bytes 4718592 | tf_op jit(solution)/shard_map/all_to_all | solution.py:34
  52.9 0.0 copy-done.1
  52.9 6.1 %collective-permute-start = (bf16[384,1536]{1,0:T(8,128)(2,1)S(1)}, bf16[384,1536]{1,0:T(8,128)(2,1)S(1)}, u32[]{:S(2)}, u32[]{:S(2)}) collective-permute-start(bf16[384,1536]{1,0:T(8,128)(2,1)S(1)} %copy-done.1), channel_id=1, source_target_pairs={{0,24},{24,0},{1,25},{25,1},{2,26},{26,2},{3,27},{27,3},{4,28},{28... | collective-permute-start | bytes 3538952 | tf_op jit(solution)/shard_map/ppermute | solution.py:65
  58.9 0.0 copy-done.6
  59.0 1.9 %collective-permute-start.2 = (s32[384]{0:T(512)S(1)}, s32[384]{0:T(512)S(1)}, u32[]{:S(2)}, u32[]{:S(2)}) collective-permute-start(s32[384]{0:T(512)S(1)} %copy-done.6), channel_id=1, source_target_pairs={{0,24},{24,0},{1,25},{25,1},{2,26},{26,2},{3,27},{27,3},{4,28},{28... | collective-permute-start | bytes 4616 | tf_op jit(solution)/shard_map/ppermute | solution.py:66
  60.9 1.1 constant_dynamic-update-slice_fusion.1
  62.0 0.0 collective-permute-done.2
  62.0 0.0 collective-permute-done
  62.0 1.1 constant_dynamic-update-slice_fusion
  63.1 14.8 %all-to-all-done.1 = bf16[4,24,16,768]{3,2,1,0:T(8,128)(2,1)S(1)} async-done(((bf16[4,24,16,768]{3,2,1,0:T(8,128)(2,1)}), bf16[4,24,16,768]{3,2,1,0:T(8,128)(2,1)S(1)}, u32[]{:S(2)}, u32[]{:S(2)}) %all-to-all-start.1) | async-done | bytes 2359328 | tf_op jit(solution)/shard_map/all_to_all | solution.py:34
  78.0 0.3 copy.32
  78.2 0.0 copy-start
  78.2 1.4 copy-done
  79.6 2.8 %convolution_convert_fusion.1 = bf16[768,384]{0,1:T(8,128)(2,1)S(1)} fusion(bf16[768,1536]{1,0:T(8,128)(2,1)} %constant_dynamic-update-slice_fusion, bf16[1536,768]{1,0:T(8,128)(2,1)S(1)} %bitcast.15), kind=kOutput, calls=%fused_computation.3 | convolution fusion | flops 906264576 | bytes 4128768 | tf_op jit(solution)/shard_map/dot_general | solution.py:68
  82.5 5.7 %convolution_convert_fusion = bf16[1536,384]{1,0:T(8,128)(2,1)S(1)} fusion(bf16[768,1536]{1,0:T(8,128)(2,1)} %constant_dynamic-update-slice_fusion, pred[768]{0:T(1024)(128)(4,1)S(1)} %add_compare_fusion, bf16[1536]{0:T(1024)(128)(2,1)S(1)} %copy-done.7, bf16[1536,768]{1,0:T(8,128)(2,1)} %bitcast.16, bf16[768,384]{0,1:T(8,128)(2,1)S(1)} %convolution_convert_fusion.1), kind=kOutput, calls=%fused_computation | convolution fusion | flops 1815773184 | bytes 7677952 | tf_op jit(solution)/shard_map/dot_general | solution.py:73
  88.2 0.1 copy.39
  88.3 13.7 %all_to_all.31 = bf16[4,24,16,384]{3,2,1,0:T(8,128)(2,1)S(1)} all-to-all(bf16[4,24,16,384]{3,2,1,0:T(8,128)(2,1)S(1)} %bitcast.14), channel_id=1, replica_groups=mesh['x'=4,'yh'=4,'core'=2,'yl'=2,'z'=12] {'x'}, dimensions={0} | all-to-all | bytes 2359296 | tf_op jit(solution)/shard_map/all_to_all | solution.py:38
  102.0 0.3 reduce_sum.33
  102.3 0.1 reshape.82
  102.4 0.1 copy.35
  102.5 12.1 %all_to_all.32 = bf16[8,12,4,384]{3,2,1,0:T(4,128)(2,1)S(1)} all-to-all(bf16[8,12,4,384]{3,2,1,0:T(4,128)(2,1)S(1)} %bitcast.21), channel_id=1, replica_groups=mesh['x'=4,'yh'=4,'core'=2,'yl'=2,'z'=12] {'yh','yl'}, dimensions={0} | all-to-all | bytes 589824 | tf_op jit(solution)/shard_map/all_to_all | solution.py:38
  114.6 0.7 reduce_sum.34
  115.3 7.7 %all-to-all-start.4 = ((bf16[12,4,384]{2,1,0:T(4,128)(2,1)}), bf16[12,4,384]{2,1,0:T(4,128)(2,1)S(1)}, u32[]{:S(2)}, u32[]{:S(2)}) async-start(bf16[12,4,384]{2,1,0:T(4,128)(2,1)} %reduce_sum.34), calls=%async_computation.4 | async-start | bytes 73728 | tf_op jit(solution)/shard_map/all_to_all | solution.py:38
  123.0 9.5 %all-to-all-done.4 = bf16[12,4,384]{2,1,0:T(4,128)(2,1)S(1)} async-done(((bf16[12,4,384]{2,1,0:T(4,128)(2,1)}), bf16[12,4,384]{2,1,0:T(4,128)(2,1)S(1)}, u32[]{:S(2)}, u32[]{:S(2)}) %all-to-all-start.4) | async-done | bytes 36896 | tf_op jit(solution)/shard_map/all_to_all | solution.py:38
  132.5 9.5 %collective-permute-start.3 = (f32[4,384]{1,0:T(4,128)S(1)}, f32[4,384]{1,0:T(4,128)S(1)}, u32[]{:S(2)}, u32[]{:S(2)}) collective-permute-start(f32[4,384]{1,0:T(4,128)S(1)} %convert_reduce_fusion), channel_id=1, source_target_pairs={{0,24},{24,0},{1,25},{25,1},{2,26},{26,2},{3,27},{27,3},{4,28},{28... | collective-permute-start | bytes 18440 | tf_op jit(solution)/shard_map/ppermute | solution.py:87
  142.1 0.1 fusion.5
  142.1 0.0 copy-start.2
  142.1 0.0 copy-start.3
  142.1 0.0 copy-start.4
  142.2 0.0 copy-start.5
  142.2 2.1 %collective-permute-start.1 = (bf16[384,384]{0,1:T(8,128)(2,1)S(1)}, bf16[384,384]{0,1:T(8,128)(2,1)S(1)}, u32[]{:S(2)}, u32[]{:S(2)}) collective-permute-start(bf16[384,384]{0,1:T(8,128)(2,1)S(1)} %get-tuple-element.42), channel_id=1, source_target_pairs={{0,24},{24,0},{1,25},{25,1},{2,26},{26,2},{3,27},{27,3},{4,28},{28... | collective-permute-start | bytes 884744 | tf_op jit(solution)/shard_map/ppermute | solution.py:78
  144.2 0.0 collective-permute-done.3
  144.3 0.7 broadcast_in_dim.42
  145.0 3.5 %all-to-all-start.5 = ((f32[16,4,768]{2,1,0:T(4,128)}), f32[16,4,768]{2,1,0:T(4,128)S(1)}, u32[]{:S(2)}, u32[]{:S(2)}) async-start(f32[16,4,768]{2,1,0:T(4,128)} %broadcast_in_dim.42), calls=%async_computation.5 | async-start | bytes 393216 | tf_op jit(solution)/shard_map/all_to_all | solution.py:34
  148.5 0.0 collective-permute-done.1
  148.5 0.2 maximum_select_fusion
  148.7 1.1 copy.36
  149.8 10.2 %all-to-all-done.5 = f32[16,4,768]{2,1,0:T(4,128)S(1)} async-done(((f32[16,4,768]{2,1,0:T(4,128)}), f32[16,4,768]{2,1,0:T(4,128)S(1)}, u32[]{:S(2)}, u32[]{:S(2)}) %all-to-all-start.5) | async-done | bytes 196640 | tf_op jit(solution)/shard_map/all_to_all | solution.py:34
  160.0 0.1 multiply_multiply_fusion
  160.1 0.1 mul.74
  160.1 0.1 mul.80
  160.3 1.0 multiply_add_fusion
  (15 shorter events, 0.2 us)
Async XLA Ops:
  48.7 4.2 %copy-start.1 = (bf16[384,1536]{1,0:T(8,128)(2,1)S(1)}, bf16[384,1536]{1,0:T(8,128)(2,1)}, u32[]{:S(2)}) copy-start(bf16[384,1536]{1,0:T(8,128)(2,1)} %param.7) | copy-start | bytes 3538948
  48.7 10.2 %copy-start.6 = (s32[384]{0:T(512)S(1)}, s32[384]{0:T(512)}, u32[]{:S(2)}) copy-start(s32[384]{0:T(512)} %param.8) | copy-start | bytes 4612
  48.7 29.2 %all-to-all-start.1 = ((bf16[4,24,16,768]{3,2,1,0:T(8,128)(2,1)}), bf16[4,24,16,768]{3,2,1,0:T(8,128)(2,1)S(1)}, u32[]{:S(2)}, u32[]{:S(2)}) async-start(bf16[4,24,16,768]{3,2,1,0:T(8,128)(2,1)} %broadcast_in_dim.39), calls=%async_computation.1 | async-start | bytes 4718592 | tf_op jit(solution)/shard_map/all_to_all | solution.py:34
  52.9 9.1 %collective-permute-start = (bf16[384,1536]{1,0:T(8,128)(2,1)S(1)}, bf16[384,1536]{1,0:T(8,128)(2,1)S(1)}, u32[]{:S(2)}, u32[]{:S(2)}) collective-permute-start(bf16[384,1536]{1,0:T(8,128)(2,1)S(1)} %copy-done.1), channel_id=1, source_target_pairs={{0,24},{24,0},{1,25},{25,1},{2,26},{26,2},{3,27},{27,3},{4,28},{28... | collective-permute-start | bytes 3538952 | tf_op jit(solution)/shard_map/ppermute | solution.py:65
  59.0 3.1 %collective-permute-start.2 = (s32[384]{0:T(512)S(1)}, s32[384]{0:T(512)S(1)}, u32[]{:S(2)}, u32[]{:S(2)}) collective-permute-start(s32[384]{0:T(512)S(1)} %copy-done.6), channel_id=1, source_target_pairs={{0,24},{24,0},{1,25},{25,1},{2,26},{26,2},{3,27},{27,3},{4,28},{28... | collective-permute-start | bytes 4616 | tf_op jit(solution)/shard_map/ppermute | solution.py:66
  78.2 1.4 copy-start
  79.6 2.8 %copy-start.7 = (bf16[1536]{0:T(1024)(128)(2,1)S(1)}, bf16[1536]{0:T(1024)(128)(2,1)}, u32[]{:S(2)}) copy-start(bf16[1536]{0:T(1024)(128)(2,1)} %param.9) | copy-start | bytes 9220
  115.3 17.2 %all-to-all-start.4 = ((bf16[12,4,384]{2,1,0:T(4,128)(2,1)}), bf16[12,4,384]{2,1,0:T(4,128)(2,1)S(1)}, u32[]{:S(2)}, u32[]{:S(2)}) async-start(bf16[12,4,384]{2,1,0:T(4,128)(2,1)} %reduce_sum.34), calls=%async_computation.4 | async-start | bytes 73728 | tf_op jit(solution)/shard_map/all_to_all | solution.py:38
  132.5 11.7 %collective-permute-start.3 = (f32[4,384]{1,0:T(4,128)S(1)}, f32[4,384]{1,0:T(4,128)S(1)}, u32[]{:S(2)}, u32[]{:S(2)}) collective-permute-start(f32[4,384]{1,0:T(4,128)S(1)} %convert_reduce_fusion), channel_id=1, source_target_pairs={{0,24},{24,0},{1,25},{25,1},{2,26},{26,2},{3,27},{27,3},{4,28},{28... | collective-permute-start | bytes 18440 | tf_op jit(solution)/shard_map/ppermute | solution.py:87
  142.1 18.1 %copy-start.2 = (f32[64,768]{1,0:T(8,128)S(1)}, f32[64,768]{1,0:T(8,128)}, u32[]{:S(2)}) copy-start(f32[64,768]{1,0:T(8,128)} %param.11) | copy-start | bytes 589828
  142.1 18.1 %copy-start.3 = (f32[64,768]{1,0:T(8,128)S(1)}, f32[64,768]{1,0:T(8,128)}, u32[]{:S(2)}) copy-start(f32[64,768]{1,0:T(8,128)} %param.10) | copy-start | bytes 589828
  142.1 18.1 %copy-start.4 = (f32[64,768]{1,0:T(8,128)S(1)}, f32[64,768]{1,0:T(8,128)}, u32[]{:S(2)}) copy-start(f32[64,768]{1,0:T(8,128)} %param.12) | copy-start | bytes 589828
  142.2 18.1 %copy-start.5 = (f32[64,768]{1,0:T(8,128)S(1)}, f32[64,768]{1,0:T(8,128)}, u32[]{:S(2)}) copy-start(f32[64,768]{1,0:T(8,128)} %param.13) | copy-start | bytes 589828
  142.2 6.3 %collective-permute-start.1 = (bf16[384,384]{0,1:T(8,128)(2,1)S(1)}, bf16[384,384]{0,1:T(8,128)(2,1)S(1)}, u32[]{:S(2)}, u32[]{:S(2)}) collective-permute-start(bf16[384,384]{0,1:T(8,128)(2,1)S(1)} %get-tuple-element.42), channel_id=1, source_target_pairs={{0,24},{24,0},{1,25},{25,1},{2,26},{26,2},{3,27},{27,3},{4,28},{28... | collective-permute-start | bytes 884744 | tf_op jit(solution)/shard_map/ppermute | solution.py:78
  145.0 15.0 %all-to-all-start.5 = ((f32[16,4,768]{2,1,0:T(4,128)}), f32[16,4,768]{2,1,0:T(4,128)S(1)}, u32[]{:S(2)}, u32[]{:S(2)}) async-start(f32[16,4,768]{2,1,0:T(4,128)} %broadcast_in_dim.42), calls=%async_computation.5 | async-start | bytes 393216 | tf_op jit(solution)/shard_map/all_to_all | solution.py:34

commit v2 on v1

--- a/solution.py
+++ b/solution.py
@@ -57,34 +57,42 @@
     cut = lambda w: lax.dynamic_slice(w, place, (piece_rows, half)).astype(jnp.bfloat16)
     piece = jnp.concatenate([cut(student_w), cut(teacher_w)], 1)
     gathered = spread(piece, SHARD, shard_count)
+
+    theirs = lax.ppermute(tokens, "core", SWAP)
+    their_mask = lax.ppermute(patch_mask, "core", SWAP)
+    gathered, theirs, their_mask = lax.optimization_barrier((gathered, theirs, their_mask))
+    both = jnp.concatenate([tokens, theirs], 0)
+    masks = jnp.concatenate([patch_mask, their_mask], 0)
+    student_in = jnp.where(masks[:, None] == 1, mask_token[None, :], both)
+
     gathered = lax.all_gather(gathered, "yh", axis=0)
     gathered = gathered.transpose(1, 0, 2, 3).reshape(shard_count, nh * piece_rows, width)
-    gathered = spread(gathered, "x", nx)
-    weights = gathered.transpose(1, 0, 2, 3).reshape(shard_count * rows, width)
+    gathered = spread(gathered, "x", nx).transpose(1, 0, 2, 3)
+    student_cols = gathered[..., :half].reshape(shard_count * rows, half)
+    teacher_cols = gathered[..., half:].reshape(shard_count * rows, half)
 
-    both = jnp.concatenate([tokens, lax.ppermute(tokens, "core", SWAP)], 0)
-    masks = jnp.concatenate([patch_mask, lax.ppermute(patch_mask, "core", SWAP)], 0)
-    student_in = jnp.where(masks[:, None] == 1, mask_token[None, :], both)
-    teacher_half = jnp.dot(
-        both, weights[:, half:], preferred_element_type=jnp.float32
-    ).astype(jnp.bfloat16)
-    student_out = jnp.dot(student_in, weights[:, :half], preferred_element_type=jnp.float32)
+    teacher_half = jnp.dot(both, teacher_cols, preferred_element_type=jnp.float32).astype(
+        jnp.bfloat16
+    )
+    student_out = jnp.dot(student_in, student_cols, preferred_element_type=jnp.float32)
     difference = (student_out - teacher_half.astype(jnp.float32)).astype(jnp.bfloat16)
     local_grad = lax.dot_general(
         student_in, difference, (((0,), (0,)), ((), ())), preferred_element_type=jnp.float32
     )
     own = tokens.shape[0]
-    teacher_feat = join_halves(
-        teacher_half[:own], lax.ppermute(teacher_half[own:], "core", SWAP), core
-    )
+    returned = lax.ppermute(teacher_half[own:], "core", SWAP)
 
     grad = local_grad.astype(jnp.bfloat16).reshape(shard_count, nx, nh * piece_rows, half)
     grad = exchange(grad.transpose(1, 0, 2, 3), "x").astype(jnp.float32).sum(0)
+    grad, returned = lax.optimization_barrier((grad, returned))
+    teacher_feat = join_halves(teacher_half[:own], returned, core)
     grad = grad.astype(jnp.bfloat16).reshape(nl, nz, nh, piece_rows, half)
     grad = grad.transpose(2, 0, 1, 3, 4).reshape(nh * nl, nz, piece_rows, half)
-    grad = exchange(grad, ("yh", "yl")).astype(jnp.float32).sum(0)
-    grad = exchange(grad.astype(jnp.bfloat16), "z").astype(jnp.float32).sum(0)
-    grad = join_halves(grad, lax.ppermute(grad, "core", SWAP), core)
+    grad = exchange(grad, ("yh", "yl")).astype(jnp.float32).sum(0).astype(jnp.bfloat16)
+    grad = jnp.broadcast_to(grad[None], (2,) + grad.shape).reshape(2 * nz, piece_rows, half)
+    grad = exchange(grad, ("core", "z")).astype(jnp.float32)
+    grad = grad.reshape(2, nz, piece_rows, half).sum(1)
+    grad = jnp.concatenate([grad[0], grad[1]], 1)
     gradient = spread(grad, ("x", "yh"), nx * nh).reshape(rows, width) / row_total
     student_new, teacher_new, first_new, second_new, direction = adamw_update(
         gradient, student_w, teacher_w, first_moment, second_moment

time: 162 us -> 162 us (level)
  blocking collectives: 70.4 us -> 55.8 us
  waiting for transfers between devices: 34.5 us -> 42.9 us
  starting transfers between devices: 34.9 us -> 40.6 us
    all_to_all x1 -> x0, blocking collectives: 27.3 us -> none  [spread(): return lax.all_to_all(copies, axes, 0, 0, tiled=True)]
    all_to_all x2 -> x3, waiting for transfers between devices: 25 us -> 39.1 us  [spread(): return lax.all_to_all(copies, axes, 0, 0, tiled=True)]
    all_to_all x2, blocking collectives: 25.8 us -> 39.2 us  [exchange(): return lax.all_to_all(pieces, axes, 0, 0, tiled=True)]
    all_to_all x2 -> x3, starting transfers between devices: 7.67 us -> 14.8 us  [spread(): return lax.all_to_all(copies, axes, 0, 0, tiled=True)]
    all_to_all x1, waiting for transfers between devices: 9.48 us -> 2.73 us  [exchange(): return lax.all_to_all(pieces, axes, 0, 0, tiled=True)]
    all_to_all x1, starting transfers between devices: 7.71 us -> 3.53 us  [exchange(): return lax.all_to_all(pieces, axes, 0, 0, tiled=True)]
    ppermute x4 -> x3, starting transfers between devices: 19.5 us -> 22.3 us  [the longest x1 12.4 us: shards(): theirs = lax.ppermute(tokens, 'core', SWAP)]
    unnamed x18 -> x20, local copies, waits for them, and re-layouts: 3.63 us -> 2.81 us
  transfers between devices with their start and end apart: 7 -> 7, of which waited for: 3 -> 5; matrix products, arithmetic and copies ran while one was open for 3% -> 4% of each run, Pallas kernels for 0% -> 0%
where the time goes in v2:
time: 162 us; the launch traced here: 161 us
  blocking collectives  55.8 us (34%)
  waiting for transfers between devices  42.9 us (26%)
  starting transfers between devices  40.6 us (25%)
  local copies, waits for them, and re-layouts  10.8 us (7%)
  matrix products  8.19 us (5%)
  other arithmetic  1.68 us (1%)
    all_to_all x2, blocking collectives, exchange(): return lax.all_to_all(pieces, axes, 0, 0, tiled=True)  39.2 us
    all_to_all x3, waiting for transfers between devices, spread(): return lax.all_to_all(copies, axes, 0, 0, tiled=True)  39.1 us
    all_gather x1, blocking collectives, shards(): gathered = lax.all_gather(gathered, 'yh', axis=0)  16.6 us
    all_to_all x3, starting transfers between devices, spread(): return lax.all_to_all(copies, axes, 0, 0, tiled=True)  14.8 us
    ppermute x1, starting transfers between devices, shards(): theirs = lax.ppermute(tokens, 'core', SWAP)  12.4 us
    ppermute x1, starting transfers between devices, shards(): returned = lax.ppermute(teacher_half[own:], 'core', SWAP)  7.69 us
    dot_general x1, matrix products, shards(): lax.dot_general(student_in, difference, (((0,), (0,)), ((), ())), preferr...  5.39 us
    all_to_all x1, starting transfers between devices, exchange(): return lax.all_to_all(pieces, axes, 0, 0, tiled=True)  3.53 us
  transfers between devices with their start and end apart: 7, of which 5 were waited for; matrix products, arithmetic and copies ran while one was open for 4% of the time, Pallas kernels for 0%

profile of v2, /device:TPU:1, one launch (start us, length us, event | category | flops | bytes accessed | tf_op | source)
XLA Modules:
  0.0 160.8 jit_solution(7121952230976493045)
XLA Ops:
  0.6 12.4 %collective-permute-start = (bf16[384,1536]{1,0:T(8,128)(2,1)}, bf16[384,1536]{1,0:T(8,128)(2,1)S(1)}, u32[]{:S(2)}, u32[]{:S(2)}) collective-permute-start(bf16[384,1536]{1,0:T(8,128)(2,1)} %param.7), channel_id=1, source_target_pairs={{0,24},{24,0},{1,25},{25,1},{2,26},{26,2},{3,27},{27,3},{4,28},{28... | collective-permute-start | bytes 3538952 | tf_op jit(solution)/shard_map/ppermute | solution.py:61
  13.0 0.8 dynamic_slice.10
  13.8 0.8 dynamic_slice.11
  14.6 0.7 broadcast_in_dim.26
  15.3 7.1 %all-to-all-start = ((bf16[24,4,768]{2,1,0:T(4,128)(2,1)}), bf16[24,4,768]{2,1,0:T(4,128)(2,1)S(1)}, u32[]{:S(2)}, u32[]{:S(2)}) async-start(bf16[24,4,768]{2,1,0:T(4,128)(2,1)} %broadcast_in_dim.26), calls=%async_computation | async-start | bytes 294912 | tf_op jit(solution)/shard_map/all_to_all | solution.py:34
  22.5 2.2 %collective-permute-start.1 = (s32[384]{0:T(512)}, s32[384]{0:T(512)S(1)}, u32[]{:S(2)}, u32[]{:S(2)}) collective-permute-start(s32[384]{0:T(512)} %param.8), channel_id=1, source_target_pairs={{0,24},{24,0},{1,25},{25,1},{2,26},{26,2},{3,27},{27,3},{4,28},{28... | collective-permute-start | bytes 4616 | tf_op jit(solution)/shard_map/ppermute | solution.py:62
  24.7 1.1 collective-permute-done.1
  25.7 7.9 %all-to-all-done = bf16[24,4,768]{2,1,0:T(4,128)(2,1)S(1)} async-done(((bf16[24,4,768]{2,1,0:T(4,128)(2,1)}), bf16[24,4,768]{2,1,0:T(4,128)(2,1)S(1)}, u32[]{:S(2)}, u32[]{:S(2)}) %all-to-all-start) | async-done | bytes 147488 | tf_op jit(solution)/shard_map/all_to_all | solution.py:34
  33.6 0.0 collective-permute-done
  33.6 16.6 %all-gather = bf16[96,4,768]{2,0,1:T(8,128)(2,1)S(1)} all-gather(bf16[24,4,768]{2,0,1:T(8,128)(2,1)S(1)} %copy.29), channel_id=2, replica_groups=mesh['x'=4,'yh'=4,'core'=2,'yl'=2,'z'=12] {'yh'}, dimensions={0}, use_global_device_ids=true | all-gather | bytes 737280 | tf_op jit(solution)/shard_map/all_gather | solution.py:68
  50.2 0.1 copy.31
  50.3 0.0 copy-done.1
  50.4 1.6 %broadcast_in_dim.28 = bf16[4,24,16,768]{3,2,1,0:T(8,128)(2,1)} broadcast(bf16[24,16,768]{2,1,0:T(8,128)(2,1)S(1)} %copy.31), dimensions={1,2,3} | broadcast | bytes 2949120 | tf_op jit(solution)/shard_map/broadcast_in_dim | solution.py:33
  52.0 4.1 %all-to-all-start.1 = ((bf16[4,24,16,768]{3,2,1,0:T(8,128)(2,1)}), bf16[4,24,16,768]{3,2,1,0:T(8,128)(2,1)S(1)}, u32[]{:S(2)}, u32[]{:S(2)}) async-start(bf16[4,24,16,768]{3,2,1,0:T(8,128)(2,1)} %broadcast_in_dim.28), calls=%async_computation.1 | async-start | bytes 4718592 | tf_op jit(solution)/shard_map/all_to_all | solution.py:34
  56.1 1.1 constant_dynamic-update-slice_fusion.1
  57.2 0.6 copy-done.2
  57.8 1.1 constant_dynamic-update-slice_fusion
  58.9 21.5 %all-to-all-done.1 = bf16[4,24,16,768]{3,2,1,0:T(8,128)(2,1)S(1)} async-done(((bf16[4,24,16,768]{3,2,1,0:T(8,128)(2,1)}), bf16[4,24,16,768]{3,2,1,0:T(8,128)(2,1)S(1)}, u32[]{:S(2)}, u32[]{:S(2)}) %all-to-all-start.1) | async-done | bytes 2359328 | tf_op jit(solution)/shard_map/all_to_all | solution.py:34
  80.4 0.3 copy.40
  80.7 0.3 fusion.1
  81.0 0.0 copy-start.8
  81.0 2.8 %convolution_convert_fusion.1 = bf16[768,384]{0,1:T(8,128)(2,1)S(1)} fusion(bf16[768,1536]{1,0:T(8,128)(2,1)} %constant_dynamic-update-slice_fusion, bf16[1536,384]{1,0:T(8,128)(2,1)S(1)} %bitcast.32), kind=kOutput, calls=%fused_computation.5 | convolution fusion | flops 906264576 | bytes 4128768 | tf_op jit(solution)/shard_map/dot_general | solution.py:74
  83.8 5.4 %convolution_convert_fusion = bf16[1536,384]{1,0:T(8,128)(2,1)S(1)} fusion(bf16[768,1536]{1,0:T(8,128)(2,1)} %constant_dynamic-update-slice_fusion, pred[768]{0:T(1024)(128)(4,1)S(1)} %add_compare_fusion, bf16[1536]{0:T(1024)(128)(2,1)S(1)} %copy-done.8, bf16[1536,384]{1,0:T(8,128)(2,1)S(1)} %bitcast.31, bf16[768,384]{0,1:T(8,128)(2,1)S(1)} %convolution_convert_fusion.1), kind=kOutput, calls=%fused_computation | convolution fusion | flops 1815773184 | bytes 5312256 | tf_op jit(solution)/shard_map/dot_general | solution.py:79
  89.2 1.1 copy.41
  90.4 3.5 %all-to-all-start.2 = ((bf16[4,24,16,384]{3,2,1,0:T(8,128)(2,1)}), bf16[4,24,16,384]{3,2,1,0:T(8,128)(2,1)S(1)}, u32[]{:S(2)}, u32[]{:S(2)}) async-start(bf16[4,24,16,384]{3,2,1,0:T(8,128)(2,1)} %bitcast.24), calls=%async_computation.2 | async-start | bytes 2359296 | tf_op jit(solution)/shard_map/all_to_all | solution.py:38
  93.9 0.1 fusion.2
  94.0 7.7 %collective-permute-start.2 = (bf16[384,384]{0,1:T(8,128)(2,1)S(1)}, bf16[384,384]{0,1:T(8,128)(2,1)S(1)}, u32[]{:S(2)}, u32[]{:S(2)}) collective-permute-start(bf16[384,384]{0,1:T(8,128)(2,1)S(1)} %get-tuple-element.54), channel_id=1, source_target_pairs={{0,24},{24,0},{1,25},{25,1},{2,26},{26,2},{3,27},{27,3},{4,28},{28... | collective-permute-start | bytes 884744 | tf_op jit(solution)/shard_map/ppermute | solution.py:83
  101.7 2.7 %all-to-all-done.2 = bf16[4,24,16,384]{3,2,1,0:T(8,128)(2,1)S(1)} async-done(((bf16[4,24,16,384]{3,2,1,0:T(8,128)(2,1)}), bf16[4,24,16,384]{3,2,1,0:T(8,128)(2,1)S(1)}, u32[]{:S(2)}, u32[]{:S(2)}) %all-to-all-start.2) | async-done | bytes 1179680 | tf_op jit(solution)/shard_map/all_to_all | solution.py:38
  104.4 0.2 convert_reduce_fusion
  104.5 0.0 collective-permute-done.2
  104.6 0.1 reshape.68
  104.6 0.1 copy.35
  104.7 14.9 %all_to_all.30 = bf16[8,12,4,384]{3,2,1,0:T(4,128)(2,1)S(1)} all-to-all(bf16[8,12,4,384]{3,2,1,0:T(4,128)(2,1)S(1)} %bitcast.30), channel_id=1, replica_groups=mesh['x'=4,'yh'=4,'core'=2,'yl'=2,'z'=12] {'yh','yl'}, dimensions={0} | all-to-all | bytes 589824 | tf_op jit(solution)/shard_map/all_to_all | solution.py:38
  119.7 0.1 reduce_sum.31
  119.8 24.3 %all_to_all.31 = bf16[24,4,384]{2,1,0:T(4,128)(2,1)S(1)} all-to-all(bf16[24,4,384]{2,1,0:T(4,128)(2,1)S(1)} %bitcast.33), channel_id=1, replica_groups=mesh['x'=4,'yh'=4,'core'=2,'yl'=2,'z'=12] {'core','z'}, dimensions={0} | all-to-all | bytes 147456 | tf_op jit(solution)/shard_map/all_to_all | solution.py:38
  144.2 0.7 broadcast_in_dim.49
  144.9 3.5 %all-to-all-start.5 = ((f32[16,4,768]{2,1,0:T(4,128)}), f32[16,4,768]{2,1,0:T(4,128)S(1)}, u32[]{:S(2)}, u32[]{:S(2)}) async-start(f32[16,4,768]{2,1,0:T(4,128)} %broadcast_in_dim.49), calls=%async_computation.5 | async-start | bytes 393216 | tf_op jit(solution)/shard_map/all_to_all | solution.py:34
  148.4 0.2 maximum_select_fusion
  148.6 0.0 copy-start.3
  148.6 0.0 copy-start.4
  148.6 0.0 copy-start.5
  148.7 0.0 copy-start.6
  148.7 1.1 copy.36
  149.8 9.7 %all-to-all-done.5 = f32[16,4,768]{2,1,0:T(4,128)S(1)} async-done(((f32[16,4,768]{2,1,0:T(4,128)}), f32[16,4,768]{2,1,0:T(4,128)S(1)}, u32[]{:S(2)}, u32[]{:S(2)}) %all-to-all-start.5) | async-done | bytes 196640 | tf_op jit(solution)/shard_map/all_to_all | solution.py:34
  159.5 0.1 multiply_multiply_fusion
  159.6 0.1 mul.74
  159.6 0.1 mul.80
  159.8 1.0 multiply_add_fusion
  (19 shorter events, 0.2 us)
Async XLA Ops:
  0.6 33.0 %collective-permute-start = (bf16[384,1536]{1,0:T(8,128)(2,1)}, bf16[384,1536]{1,0:T(8,128)(2,1)S(1)}, u32[]{:S(2)}, u32[]{:S(2)}) collective-permute-start(bf16[384,1536]{1,0:T(8,128)(2,1)} %param.7), channel_id=1, source_target_pairs={{0,24},{24,0},{1,25},{25,1},{2,26},{26,2},{3,27},{27,3},{4,28},{28... | collective-permute-start | bytes 3538952 | tf_op jit(solution)/shard_map/ppermute | solution.py:61
  15.3 18.3 %all-to-all-start = ((bf16[24,4,768]{2,1,0:T(4,128)(2,1)}), bf16[24,4,768]{2,1,0:T(4,128)(2,1)S(1)}, u32[]{:S(2)}, u32[]{:S(2)}) async-start(bf16[24,4,768]{2,1,0:T(4,128)(2,1)} %broadcast_in_dim.26), calls=%async_computation | async-start | bytes 294912 | tf_op jit(solution)/shard_map/all_to_all | solution.py:34
  22.5 3.3 %collective-permute-start.1 = (s32[384]{0:T(512)}, s32[384]{0:T(512)S(1)}, u32[]{:S(2)}, u32[]{:S(2)}) collective-permute-start(s32[384]{0:T(512)} %param.8), channel_id=1, source_target_pairs={{0,24},{24,0},{1,25},{25,1},{2,26},{26,2},{3,27},{27,3},{4,28},{28... | collective-permute-start | bytes 4616 | tf_op jit(solution)/shard_map/ppermute | solution.py:62
  33.6 16.7 %copy-start.1 = (bf16[384,1536]{1,0:T(8,128)(2,1)}, bf16[384,1536]{1,0:T(8,128)(2,1)S(1)}, u32[]{:S(2)}) copy-start(bf16[384,1536]{1,0:T(8,128)(2,1)S(1)} %collective-permute-done) | copy-start | bytes 3538948
  52.0 4.1 %copy-start = (bf16[384,1536]{1,0:T(8,128)(2,1)S(1)}, bf16[384,1536]{1,0:T(8,128)(2,1)}, u32[]{:S(2)}) copy-start(bf16[384,1536]{1,0:T(8,128)(2,1)} %param.7) | copy-start | bytes 3538948
  52.0 28.5 %all-to-all-start.1 = ((bf16[4,24,16,768]{3,2,1,0:T(8,128)(2,1)}), bf16[4,24,16,768]{3,2,1,0:T(8,128)(2,1)S(1)}, u32[]{:S(2)}, u32[]{:S(2)}) async-start(bf16[4,24,16,768]{3,2,1,0:T(8,128)(2,1)} %broadcast_in_dim.28), calls=%async_computation.1 | async-start | bytes 4718592 | tf_op jit(solution)/shard_map/all_to_all | solution.py:34
  56.1 1.1 copy-start.7
  56.1 1.7 %copy-start.2 = (bf16[384,1536]{1,0:T(8,128)(2,1)S(1)}, bf16[384,1536]{1,0:T(8,128)(2,1)}, u32[]{:S(2)}) copy-start(bf16[384,1536]{1,0:T(8,128)(2,1)} %copy-done.1) | copy-start | bytes 3538948
  81.0 2.8 %copy-start.8 = (bf16[1536]{0:T(1024)(128)(2,1)S(1)}, bf16[1536]{0:T(1024)(128)(2,1)}, u32[]{:S(2)}) copy-start(bf16[1536]{0:T(1024)(128)(2,1)} %param.9) | copy-start | bytes 9220
  90.4 14.0 %all-to-all-start.2 = ((bf16[4,24,16,384]{3,2,1,0:T(8,128)(2,1)}), bf16[4,24,16,384]{3,2,1,0:T(8,128)(2,1)S(1)}, u32[]{:S(2)}, u32[]{:S(2)}) async-start(bf16[4,24,16,384]{3,2,1,0:T(8,128)(2,1)} %bitcast.24), calls=%async_computation.2 | async-start | bytes 2359296 | tf_op jit(solution)/shard_map/all_to_all | solution.py:38
  94.0 10.6 %collective-permute-start.2 = (bf16[384,384]{0,1:T(8,128)(2,1)S(1)}, bf16[384,384]{0,1:T(8,128)(2,1)S(1)}, u32[]{:S(2)}, u32[]{:S(2)}) collective-permute-start(bf16[384,384]{0,1:T(8,128)(2,1)S(1)} %get-tuple-element.54), channel_id=1, source_target_pairs={{0,24},{24,0},{1,25},{25,1},{2,26},{26,2},{3,27},{27,3},{4,28},{28... | collective-permute-start | bytes 884744 | tf_op jit(solution)/shard_map/ppermute | solution.py:83
  144.9 14.6 %all-to-all-start.5 = ((f32[16,4,768]{2,1,0:T(4,128)}), f32[16,4,768]{2,1,0:T(4,128)S(1)}, u32[]{:S(2)}, u32[]{:S(2)}) async-start(f32[16,4,768]{2,1,0:T(4,128)} %broadcast_in_dim.49), calls=%async_computation.5 | async-start | bytes 393216 | tf_op jit(solution)/shard_map/all_to_all | solution.py:34
  148.6 11.1 %copy-start.3 = (f32[64,768]{1,0:T(8,128)S(1)}, f32[64,768]{1,0:T(8,128)}, u32[]{:S(2)}) copy-start(f32[64,768]{1,0:T(8,128)} %param.11) | copy-start | bytes 589828
  148.6 11.1 %copy-start.4 = (f32[64,768]{1,0:T(8,128)S(1)}, f32[64,768]{1,0:T(8,128)}, u32[]{:S(2)}) copy-start(f32[64,768]{1,0:T(8,128)} %param.10) | copy-start | bytes 589828
  148.6 11.1 %copy-start.5 = (f32[64,768]{1,0:T(8,128)S(1)}, f32[64,768]{1,0:T(8,128)}, u32[]{:S(2)}) copy-start(f32[64,768]{1,0:T(8,128)} %param.12) | copy-start | bytes 589828
  148.7 11.1 %copy-start.6 = (f32[64,768]{1,0:T(8,128)S(1)}, f32[64,768]{1,0:T(8,128)}, u32[]{:S(2)}) copy-start(f32[64,768]{1,0:T(8,128)} %param.13) | copy-start | bytes 589828

commit v3 on v1

v3 whole, which is shorter than its diff:
```python
import jax
import jax.numpy as jnp
from jax import lax
from jax.sharding import Mesh, PartitionSpec as P

STEP = 100


beta_one = 0.9
beta_two = 0.999
adam_eps = 1e-08
learn_rate = 0.0002
decay_rate = 0.04
ema_keep = 0.994

REP = ("x", "yh", "core")
SHARD = ("yl", "z")
SWAP = [(0, 1), (1, 0)]


def adamw_update(gradient, weights, teacher, moment_one, moment_two):
    first_new = beta_one * moment_one + (1.0 - beta_one) * gradient
    second_new = beta_two * moment_two + (1.0 - beta_two) * gradient * gradient
    fix_one = 1.0 - beta_one**STEP
    fix_two = 1.0 - beta_two**STEP
    direction = first_new / fix_one / (jnp.sqrt(second_new / fix_two) + adam_eps)
    student_new = weights - learn_rate * (direction + decay_rate * weights)
    teacher_new = ema_keep * teacher + (1.0 - ema_keep) * student_new
    return (student_new, teacher_new, first_new, second_new, direction)


def spread(piece, axes, members):
    copies = jnp.broadcast_to(piece[None], (members,) + piece.shape)
    return lax.all_to_all(copies, axes, 0, 0, tiled=True)


def exchange(pieces, axes):
    return lax.all_to_all(pieces, axes, 0, 0, tiled=True)


def halves_in_order(mine, theirs, index):
    return jnp.where(
        index == 0, jnp.concatenate([mine, theirs], 1), jnp.concatenate([theirs, mine], 1)
    )


def shards(tokens, patch_mask, mask_token, student_w, teacher_w, first_moment, second_moment):
    nx, nh, nl, nz = (lax.axis_size(a) for a in ("x", "yh", "yl", "z"))
    core, side = lax.axis_index("core"), lax.axis_index("yl")
    shard_count = nl * nz
    own, depth = tokens.shape
    rows, width = student_w.shape
    half, quarter = width // 2, width // 4
    part = rows // nx
    row_total = float(own * shard_count * nx * nh * 2)

    place = (lax.axis_index("x") * part, core * half)
    cut = lambda w: lax.dynamic_slice(w, place, (part, half)).astype(jnp.bfloat16)
    student_cut, teacher_cut = cut(student_w), cut(teacher_w)
    pieces = jnp.stack(
        [
            jnp.concatenate([student_cut[:, :quarter], teacher_cut[:, :quarter]], 1),
            jnp.concatenate([student_cut[:, quarter:], teacher_cut[:, quarter:]], 1),
        ]
    )
    pieces = jnp.broadcast_to(pieces[:, None], (nl, nz, part, half))
    gathered = exchange(pieces.reshape(shard_count, part, half), SHARD)

    beside = lax.ppermute(tokens, "yl", SWAP)
    beside_mask = lax.ppermute(patch_mask, "yl", SWAP)
    gathered, beside, beside_mask = lax.optimization_barrier((gathered, beside, beside_mask))
    gathered = spread(gathered, "x", nx).transpose(1, 0, 2, 3)
    weights = gathered.reshape(depth, half)

    pair = jnp.concatenate([tokens, beside], 0)
    pair_mask = jnp.concatenate([patch_mask, beside_mask], 0)
    shared = jnp.concatenate([pair, lax.ppermute(pair, "core", SWAP)], 0)
    masks = jnp.concatenate([pair_mask, lax.ppermute(pair_mask, "core", SWAP)], 0)
    masked = masks[:, None] == 1
    student_in = jnp.where(masked, mask_token[None, :], shared)

    product = jnp.dot(shared, weights, preferred_element_type=jnp.float32)
    mask_row = jnp.dot(mask_token[None], weights, preferred_element_type=jnp.float32)
    student_out = jnp.where(masked, mask_row[:, :quarter], product[:, :quarter])
    teacher_part = product[:, quarter:].astype(jnp.bfloat16)
    difference = (student_out - teacher_part.astype(jnp.float32)).astype(jnp.bfloat16)
    local_grad = lax.dot_general(
        student_in, difference, (((0,), (0,)), ((), ())), preferred_element_type=jnp.float32
    )

    grad = local_grad.astype(jnp.bfloat16).reshape(shard_count, nx, part, quarter)
    grad = exchange(grad.transpose(1, 0, 2, 3), "x").astype(jnp.float32).sum(0)

    teacher_part = teacher_part.reshape(2, 2, own, quarter)
    from_side = lax.ppermute(teacher_part[:, 1], "yl", SWAP)
    grad, from_side = lax.optimization_barrier((grad, from_side))
    mine = teacher_part[0, 0]
    to_core = jnp.stack([teacher_part[1, 0], from_side[1]])
    from_core = lax.ppermute(to_core, "core", SWAP)

    grad = exchange(grad.astype(jnp.bfloat16), SHARD).astype(jnp.float32)
    grad = grad.reshape(nl, nz, part, quarter).sum(1)
    grad, from_core = lax.optimization_barrier((grad, from_core))
    teacher_feat = halves_in_order(
        halves_in_order(mine, from_side[0], side),
        halves_in_order(from_core[0], from_core[1], side),
        core,
    )

    grad = jnp.concatenate([grad[0], grad[1]], 1).astype(jnp.bfloat16)
    grad = spread(grad, REP, nx * nh * 2).reshape(nx, nh, 2, part, half)
    grad = grad.astype(jnp.float32).sum(1).transpose(0, 2, 1, 3)
    gradient = grad.reshape(rows, width) / row_total
    student_new, teacher_new, first_new, second_new, direction = adamw_update(
        gradient, student_w, teacher_w, first_moment, second_moment
    )
    return (teacher_feat, student_new, teacher_new, first_new, second_new, direction)


def solution(mesh, sizes=(4, 4, 2, 2, 12)):
    fine = Mesh(mesh.devices.reshape(sizes), REP + SHARD)
    tok, row = P(REP + SHARD), P(SHARD, None)
    return jax.shard_map(
        shards,
        mesh=fine,
        in_specs=(P(REP + SHARD, None), tok, P(), row, row, row, row),
        out_specs=(P(REP + SHARD, None), row, row, row, row, row),
        check_vma=False,
    )
```

time: 162 us -> 150 us (0.926)
  blocking collectives: 70.4 us -> 0 us
  starting transfers between devices: 34.9 us -> 67.9 us
  waiting for transfers between devices: 34.5 us -> 51.5 us
  local copies, waits for them, and re-layouts: 9.58 us -> 16.5 us
  other arithmetic: 2.4 us -> 6.6 us
  matrix products: 8.51 us -> 6 us
    all_to_all x3 -> x0, blocking collectives: 53.1 us -> none  [the longest x1 27.3 us: spread(): return lax.all_to_all(copies, axes, 0, 0, tiled=True)]
    all_to_all x1 -> x3, starting transfers between devices: 7.71 us -> 29.3 us  [exchange(): return lax.all_to_all(pieces, axes, 0, 0, tiled=True)]
    all_gather x1 -> x0, blocking collectives: 17.4 us -> none  [shards(): gathered = lax.all_gather(gathered, 'yh', axis=0)]
    all_to_all x1 -> x3, waiting for transfers between devices: 9.48 us -> 22.4 us  [exchange(): return lax.all_to_all(pieces, axes, 0, 0, tiled=True)]
    all_to_all x2, starting transfers between devices: 7.67 us -> 16.9 us  [spread(): return lax.all_to_all(copies, axes, 0, 0, tiled=True)]
    dot_general x1, matrix products: 5.7 us -> 1.23 us  [shards(): lax.dot_general(student_in, difference, (((0,), (0,)), ((), ())), preferr...]
    ppermute x4 -> x6, waiting for transfers between devices: 0.03 us -> 4.46 us  [the longest x1 2.04 us: shards(): from_side = lax.ppermute(teacher_part[:, 1], 'yl', SWAP)]
    concatenate x1 -> x3, other arithmetic: 0.01 us -> 3 us  [the longest x1 2.92 us: shards(): pair = jnp.concatenate([tokens, beside], 0)]
  transfers between devices with their start and end apart: 7 -> 11, of which waited for: 3 -> 8; matrix products, arithmetic and copies ran while one was open for 3% -> 7% of each run, Pallas kernels for 0% -> 0%
where the time goes in v3:
time: 150 us
  starting transfers between devices  67.9 us (45%)
  waiting for transfers between devices  51.5 us (34%)
  local copies, waits for them, and re-layouts  16.5 us (11%)
  other arithmetic  6.6 us (4%)
  matrix products  6 us (4%)
    all_to_all x3, starting transfers between devices, exchange(): return lax.all_to_all(pieces, axes, 0, 0, tiled=True)  29.3 us
    all_to_all x2, waiting for transfers between devices, spread(): return lax.all_to_all(copies, axes, 0, 0, tiled=True)  24.7 us
    all_to_all x3, waiting for transfers between devices, exchange(): return lax.all_to_all(pieces, axes, 0, 0, tiled=True)  22.4 us
    all_to_all x2, starting transfers between devices, spread(): return lax.all_to_all(copies, axes, 0, 0, tiled=True)  16.9 us
    ppermute x1, starting transfers between devices, shards(): shared = jnp.concatenate([pair, lax.ppermute(pair, 'core', SWAP)], 0)  5.98 us
    unnamed x28, local copies, waits for them, and re-layouts  4.66 us
    dot_general x1, matrix products, shards(): product = jnp.dot(shared, weights, preferred_element_type=jnp.float32)  4.56 us
    ppermute x1, starting transfers between devices, shards(): from_core = lax.ppermute(to_core, 'core', SWAP)  4.2 us
  transfers between devices with their start and end apart: 11, of which 8 were waited for; matrix products, arithmetic and copies ran while one was open for 7% of the time, Pallas kernels for 0%

profile of v3, /device:TPU:1, one launch (start us, length us, event | category | flops | bytes accessed | tf_op | source)
XLA Modules:
  0.0 149.5 jit_solution(16283658395945874693)
XLA Ops:
  0.6 4.0 %collective-permute-start = (bf16[384,1536]{1,0:T(8,128)(2,1)}, bf16[384,1536]{1,0:T(8,128)(2,1)S(1)}, u32[]{:S(2)}, u32[]{:S(2)}) collective-permute-start(bf16[384,1536]{1,0:T(8,128)(2,1)} %param.7), channel_id=1, source_target_pairs={{0,12},{12,0},{1,13},{13,1},{2,14},{14,2},{3,15},{15,3},{4,16},{16... | collective-permute-start | bytes 3538952 | tf_op jit(solution)/shard_map/ppermute | solution.py:69
  4.7 0.7 dynamic_slice.11
  5.5 0.7 dynamic_slice.10
  6.4 0.7 broadcast_in_dim.55
  7.2 15.1 %all-to-all-start = ((bf16[24,16,384]{2,1,0:T(8,128)(2,1)}), bf16[24,16,384]{2,1,0:T(8,128)(2,1)S(1)}, u32[]{:S(2)}, u32[]{:S(2)}) async-start(bf16[24,16,384]{2,1,0:T(8,128)(2,1)} %bitcast.2), calls=%async_computation | async-start | bytes 589824 | tf_op jit(solution)/shard_map/all_to_all | solution.py:38
  22.3 3.2 %collective-permute-start.1 = (s32[384]{0:T(512)}, s32[384]{0:T(512)S(1)}, u32[]{:S(2)}, u32[]{:S(2)}) collective-permute-start(s32[384]{0:T(512)} %param.8), channel_id=1, source_target_pairs={{0,12},{12,0},{1,13},{13,1},{2,14},{14,2},{3,15},{15,3},{4,16},{16... | collective-permute-start | bytes 4616 | tf_op jit(solution)/shard_map/ppermute | solution.py:70
  25.5 1.6 %collective-permute-done.1 = s32[384]{0:T(512)S(1)} collective-permute-done((s32[384]{0:T(512)}, s32[384]{0:T(512)S(1)}, u32[]{:S(2)}, u32[]{:S(2)}) %collective-permute-start.1) | collective-permute-done | bytes 1568 | tf_op jit(solution)/shard_map/ppermute | solution.py:70
  27.1 9.5 %all-to-all-done = bf16[24,16,384]{2,1,0:T(8,128)(2,1)S(1)} async-done(((bf16[24,16,384]{2,1,0:T(8,128)(2,1)}), bf16[24,16,384]{2,1,0:T(8,128)(2,1)S(1)}, u32[]{:S(2)}, u32[]{:S(2)}) %all-to-all-start) | async-done | bytes 294944 | tf_op jit(solution)/shard_map/all_to_all | solution.py:38
  36.6 2.9 %pad_maximum_fusion = bf16[768,1536]{1,0:T(8,128)(2,1)} fusion(bf16[384,1536]{1,0:T(8,128)(2,1)S(1)} %collective-permute-done, bf16[384,1536]{1,0:T(8,128)(2,1)} %param.7), kind=kLoop, calls=%fused_computation.4 | loop fusion | flops 4718592 | bytes 4718592 | tf_op jit(solution)/shard_map/concatenate | solution.py:75
  39.5 6.0 %collective-permute-start.2 = (bf16[768,1536]{1,0:T(8,128)(2,1)}, bf16[768,1536]{1,0:T(8,128)(2,1)}, u32[]{:S(2)}, u32[]{:S(2)}) collective-permute-start(bf16[768,1536]{1,0:T(8,128)(2,1)} %pad_maximum_fusion), channel_id=1, source_target_pairs={{0,24},{24,0},{1,25},{25,1},{2,26},{26,2},{3,27},{27,3},{4,28},{28... | collective-permute-start | bytes 7077896 | tf_op jit(solution)/shard_map/ppermute | solution.py:77
  45.5 1.2 broadcast_in_dim.56
  46.7 4.1 %all-to-all-start.1 = ((bf16[4,24,16,384]{3,2,1,0:T(8,128)(2,1)}), bf16[4,24,16,384]{3,2,1,0:T(8,128)(2,1)S(1)}, u32[]{:S(2)}, u32[]{:S(2)}) async-start(bf16[4,24,16,384]{3,2,1,0:T(8,128)(2,1)} %broadcast_in_dim.56), calls=%async_computation.1 | async-start | bytes 2359296 | tf_op jit(solution)/shard_map/all_to_all | solution.py:34
  50.8 0.7 reshape.96
  51.6 2.2 %collective-permute-start.3 = (s32[768]{0:T(1024)S(1)}, s32[768]{0:T(1024)S(1)}, u32[]{:S(2)}, u32[]{:S(2)}) collective-permute-start(s32[768]{0:T(1024)S(1)} %pad_add_fusion), channel_id=1, source_target_pairs={{0,24},{24,0},{1,25},{25,1},{2,26},{26,2},{3,27},{27,3},{4,28},{28... | collective-permute-start | bytes 9224 | tf_op jit(solution)/shard_map/ppermute | solution.py:78
  53.9 0.8 collective-permute-done.3
  54.7 1.4 copy-done.1
  56.1 11.1 %all-to-all-done.1 = bf16[4,24,16,384]{3,2,1,0:T(8,128)(2,1)S(1)} async-done(((bf16[4,24,16,384]{3,2,1,0:T(8,128)(2,1)}), bf16[4,24,16,384]{3,2,1,0:T(8,128)(2,1)S(1)}, u32[]{:S(2)}, u32[]{:S(2)}) %all-to-all-start.1) | async-done | bytes 1179680 | tf_op jit(solution)/shard_map/all_to_all | solution.py:34
  67.1 0.2 copy.32
  67.3 0.2 fusion.9
  67.5 3.3 %constant_dynamic-update-slice_fusion = bf16[1536,1536]{1,0:T(8,128)(2,1)} fusion(bf16[1536,1536]{1,0:T(8,128)(2,1)} %copy-done.1, bf16[768,1536]{1,0:T(8,128)(2,1)} %collective-permute-done.2), kind=kLoop, calls=%fused_computation.39 | loop fusion | bytes 4718592 | tf_op jit(solution)/shard_map/concatenate | solution.py:77
  70.8 4.6 %fusion.18 = f32[1536,384]{0,1:T(8,128)S(1)} fusion(bf16[1536,1536]{1,0:T(8,128)(2,1)} %constant_dynamic-update-slice_fusion, bf16[1536,384]{1,0:T(8,128)(2,1)S(1)} %bitcast.47), kind=kOutput, calls=%fused_computation.48 | convolution fusion | flops 1811939328 | bytes 8257536 | tf_op jit(solution)/shard_map/dot_general | solution.py:82
  75.4 1.4 copy-done.7
  76.8 1.2 fusion.3
  78.0 0.3 copy.34
  78.3 1.0 copy.35
  79.3 3.5 %all-to-all-start.2 = ((bf16[4,24,16,192]{3,2,1,0:T(8,128)(2,1)}), bf16[4,24,16,192]{3,2,1,0:T(8,128)(2,1)S(1)}, u32[]{:S(2)}, u32[]{:S(2)}) async-start(bf16[4,24,16,192]{3,2,1,0:T(8,128)(2,1)} %copy.35), calls=%async_computation.2 | async-start | bytes 1572864 | tf_op jit(solution)/shard_map/all_to_all | solution.py:38
  82.8 1.3 slice.94
  84.1 0.1 reshape.89
  84.3 0.6 slice.76
  84.9 0.5 copy.41
  85.4 2.1 %collective-permute-start.4 = (bf16[2,384,192]{2,1,0:T(8,128)(2,1)S(1)}, bf16[2,384,192]{2,1,0:T(8,128)(2,1)S(1)}, u32[]{:S(2)}, u32[]{:S(2)}) collective-permute-start(bf16[2,384,192]{2,1,0:T(8,128)(2,1)S(1)} %bitcast.55), channel_id=1, source_target_pairs={{0,12},{12,0},{1,13},{13,1},{2,14},{14,2},{3,15},{15,3},{4,16},{16... | collective-permute-start | bytes 884744 | tf_op jit(solution)/shard_map/ppermute | solution.py:95
  87.6 0.4 fusion.14
  88.0 0.2 copy.42
  88.2 5.8 %all-to-all-done.2 = bf16[4,24,16,192]{3,2,1,0:T(8,128)(2,1)S(1)} async-done(((bf16[4,24,16,192]{3,2,1,0:T(8,128)(2,1)}), bf16[4,24,16,192]{3,2,1,0:T(8,128)(2,1)S(1)}, u32[]{:S(2)}, u32[]{:S(2)}) %all-to-all-start.2) | async-done | bytes 589856 | tf_op jit(solution)/shard_map/all_to_all | solution.py:38
  94.0 0.8 convert_reduce_fusion
  94.8 2.0 %collective-permute-done.4 = bf16[2,384,192]{2,1,0:T(8,128)(2,1)S(1)} collective-permute-done((bf16[2,384,192]{2,1,0:T(8,128)(2,1)S(1)}, bf16[2,384,192]{2,1,0:T(8,128)(2,1)S(1)}, u32[]{:S(2)}, u32[]{:S(2)}) %collective-permute-start.4) | collective-permute-done | bytes 294944 | tf_op jit(solution)/shard_map/ppermute | solution.py:95
  96.8 10.7 %all-to-all-start.3 = ((bf16[24,16,192]{2,1,0:T(8,128)(2,1)}), bf16[24,16,192]{2,1,0:T(8,128)(2,1)S(1)}, u32[]{:S(2)}, u32[]{:S(2)}) async-start(bf16[24,16,192]{2,1,0:T(8,128)(2,1)} %convert_reduce_fusion), calls=%async_computation.3 | async-start | bytes 393216 | tf_op jit(solution)/shard_map/all_to_all | solution.py:38
  107.7 4.2 %collective-permute-start.5 = (bf16[2,384,192]{2,1,0:T(8,128)(2,1)S(1)}, bf16[2,384,192]{2,1,0:T(8,128)(2,1)S(1)}, u32[]{:S(2)}, u32[]{:S(2)}) collective-permute-start(bf16[2,384,192]{2,1,0:T(8,128)(2,1)S(1)} %pad_maximum_fusion.1), channel_id=1, source_target_pairs={{0,24},{24,0},{1,25},{25,1},{2,26},{26,2},{3,27},{27,3},{4,28},{28... | collective-permute-start | bytes 884744 | tf_op jit(solution)/shard_map/ppermute | solution.py:99
  111.9 7.1 %all-to-all-done.3 = bf16[24,16,192]{2,1,0:T(8,128)(2,1)S(1)} async-done(((bf16[24,16,192]{2,1,0:T(8,128)(2,1)}), bf16[24,16,192]{2,1,0:T(8,128)(2,1)S(1)}, u32[]{:S(2)}, u32[]{:S(2)}) %all-to-all-start.3) | async-done | bytes 147488 | tf_op jit(solution)/shard_map/all_to_all | solution.py:38
  119.1 0.8 broadcast_in_dim.62
  119.9 12.8 %all-to-all-start.4 = ((bf16[32,16,384]{2,1,0:T(8,128)(2,1)}), bf16[32,16,384]{2,1,0:T(8,128)(2,1)S(1)}, u32[]{:S(2)}, u32[]{:S(2)}) async-start(bf16[32,16,384]{2,1,0:T(8,128)(2,1)} %broadcast_in_dim.62), calls=%async_computation.4 | async-start | bytes 786432 | tf_op jit(solution)/shard_map/all_to_all | solution.py:34
  132.7 0.2 copy.40
  132.9 0.3 maximum_select_fusion.1
  133.3 0.3 maximum_select_fusion.2
  133.5 1.0 maximum_select_fusion
  134.5 13.6 %all-to-all-done.4 = bf16[32,16,384]{2,1,0:T(8,128)(2,1)S(1)} async-done(((bf16[32,16,384]{2,1,0:T(8,128)(2,1)}), bf16[32,16,384]{2,1,0:T(8,128)(2,1)S(1)}, u32[]{:S(2)}, u32[]{:S(2)}) %all-to-all-start.4) | async-done | bytes 393248 | tf_op jit(solution)/shard_map/all_to_all | solution.py:34
  148.2 0.1 copy.38
  148.5 1.0 multiply_add_fusion
  (40 shorter events, 0.9 us)
Async XLA Ops:
  0.6 36.0 %collective-permute-start = (bf16[384,1536]{1,0:T(8,128)(2,1)}, bf16[384,1536]{1,0:T(8,128)(2,1)S(1)}, u32[]{:S(2)}, u32[]{:S(2)}) collective-permute-start(bf16[384,1536]{1,0:T(8,128)(2,1)} %param.7), channel_id=1, source_target_pairs={{0,12},{12,0},{1,13},{13,1},{2,14},{14,2},{3,15},{15,3},{4,16},{16... | collective-permute-start | bytes 3538952 | tf_op jit(solution)/shard_map/ppermute | solution.py:69
  7.2 29.4 %all-to-all-start = ((bf16[24,16,384]{2,1,0:T(8,128)(2,1)}), bf16[24,16,384]{2,1,0:T(8,128)(2,1)S(1)}, u32[]{:S(2)}, u32[]{:S(2)}) async-start(bf16[24,16,384]{2,1,0:T(8,128)(2,1)} %bitcast.2), calls=%async_computation | async-start | bytes 589824 | tf_op jit(solution)/shard_map/all_to_all | solution.py:38
  22.3 4.9 %collective-permute-start.1 = (s32[384]{0:T(512)}, s32[384]{0:T(512)S(1)}, u32[]{:S(2)}, u32[]{:S(2)}) collective-permute-start(s32[384]{0:T(512)} %param.8), channel_id=1, source_target_pairs={{0,12},{12,0},{1,13},{13,1},{2,14},{14,2},{3,15},{15,3},{4,16},{16... | collective-permute-start | bytes 4616 | tf_op jit(solution)/shard_map/ppermute | solution.py:70
  39.5 12.0 %copy-start = (bf16[384,1536]{1,0:T(8,128)(2,1)S(1)}, bf16[384,1536]{1,0:T(8,128)(2,1)}, u32[]{:S(2)}) copy-start(bf16[384,1536]{1,0:T(8,128)(2,1)} %param.7) | copy-start | bytes 3538948
  39.5 28.0 %collective-permute-start.2 = (bf16[768,1536]{1,0:T(8,128)(2,1)}, bf16[768,1536]{1,0:T(8,128)(2,1)}, u32[]{:S(2)}, u32[]{:S(2)}) collective-permute-start(bf16[768,1536]{1,0:T(8,128)(2,1)} %pad_maximum_fusion), channel_id=1, source_target_pairs={{0,24},{24,0},{1,25},{25,1},{2,26},{26,2},{3,27},{27,3},{4,28},{28... | collective-permute-start | bytes 7077896 | tf_op jit(solution)/shard_map/ppermute | solution.py:77
  46.7 4.9 %copy-start.8 = (s32[384]{0:T(512)S(1)}, s32[384]{0:T(512)}, u32[]{:S(2)}) copy-start(s32[384]{0:T(512)} %param.8) | copy-start | bytes 4612
  46.7 20.4 %all-to-all-start.1 = ((bf16[4,24,16,384]{3,2,1,0:T(8,128)(2,1)}), bf16[4,24,16,384]{3,2,1,0:T(8,128)(2,1)S(1)}, u32[]{:S(2)}, u32[]{:S(2)}) async-start(bf16[4,24,16,384]{3,2,1,0:T(8,128)(2,1)} %broadcast_in_dim.56), calls=%async_computation.1 | async-start | bytes 2359296 | tf_op jit(solution)/shard_map/all_to_all | solution.py:34
  51.6 3.1 %collective-permute-start.3 = (s32[768]{0:T(1024)S(1)}, s32[768]{0:T(1024)S(1)}, u32[]{:S(2)}, u32[]{:S(2)}) collective-permute-start(s32[768]{0:T(1024)S(1)} %pad_add_fusion), channel_id=1, source_target_pairs={{0,24},{24,0},{1,25},{25,1},{2,26},{26,2},{3,27},{27,3},{4,28},{28... | collective-permute-start | bytes 9224 | tf_op jit(solution)/shard_map/ppermute | solution.py:78
  53.9 2.1 %copy-start.1 = (bf16[1536,1536]{1,0:T(8,128)(2,1)}, bf16[1536,1536]{1,0:T(8,128)(2,1)S(1)}, u32[]{:S(2)}) copy-start(bf16[1536,1536]{1,0:T(8,128)(2,1)S(1)} %constant_dynamic-update-slice_fusion.1) | copy-start | bytes 14155780
  70.8 6.0 %copy-start.2 = (bf16[1536,1536]{1,0:T(8,128)(2,1)S(1)}, bf16[1536,1536]{1,0:T(8,128)(2,1)}, u32[]{:S(2)}) copy-start(bf16[1536,1536]{1,0:T(8,128)(2,1)} %constant_dynamic-update-slice_fusion) | copy-start | bytes 14155780
  70.8 6.0 %copy-start.9 = (bf16[1536]{0:T(1024)(128)(2,1)S(1)}, bf16[1536]{0:T(1024)(128)(2,1)}, u32[]{:S(2)}) copy-start(bf16[1536]{0:T(1024)(128)(2,1)} %param.9) | copy-start | bytes 9220
  75.4 1.4 copy-start.7
  79.3 14.7 %all-to-all-start.2 = ((bf16[4,24,16,192]{3,2,1,0:T(8,128)(2,1)}), bf16[4,24,16,192]{3,2,1,0:T(8,128)(2,1)S(1)}, u32[]{:S(2)}, u32[]{:S(2)}) async-start(bf16[4,24,16,192]{3,2,1,0:T(8,128)(2,1)} %copy.35), calls=%async_computation.2 | async-start | bytes 1572864 | tf_op jit(solution)/shard_map/all_to_all | solution.py:38
  85.4 11.4 %collective-permute-start.4 = (bf16[2,384,192]{2,1,0:T(8,128)(2,1)S(1)}, bf16[2,384,192]{2,1,0:T(8,128)(2,1)S(1)}, u32[]{:S(2)}, u32[]{:S(2)}) collective-permute-start(bf16[2,384,192]{2,1,0:T(8,128)(2,1)S(1)} %bitcast.55), channel_id=1, source_target_pairs={{0,12},{12,0},{1,13},{13,1},{2,14},{14,2},{3,15},{15,3},{4,16},{16... | collective-permute-start | bytes 884744 | tf_op jit(solution)/shard_map/ppermute | solution.py:95
  96.8 22.2 %all-to-all-start.3 = ((bf16[24,16,192]{2,1,0:T(8,128)(2,1)}), bf16[24,16,192]{2,1,0:T(8,128)(2,1)S(1)}, u32[]{:S(2)}, u32[]{:S(2)}) async-start(bf16[24,16,192]{2,1,0:T(8,128)(2,1)} %convert_reduce_fusion), calls=%async_computation.3 | async-start | bytes 393216 | tf_op jit(solution)/shard_map/all_to_all | solution.py:38
  107.7 11.4 %collective-permute-start.5 = (bf16[2,384,192]{2,1,0:T(8,128)(2,1)S(1)}, bf16[2,384,192]{2,1,0:T(8,128)(2,1)S(1)}, u32[]{:S(2)}, u32[]{:S(2)}) collective-permute-start(bf16[2,384,192]{2,1,0:T(8,128)(2,1)S(1)} %pad_maximum_fusion.1), channel_id=1, source_target_pairs={{0,24},{24,0},{1,25},{25,1},{2,26},{26,2},{3,27},{27,3},{4,28},{28... | collective-permute-start | bytes 884744 | tf_op jit(solution)/shard_map/ppermute | solution.py:99
  119.9 28.2 %all-to-all-start.4 = ((bf16[32,16,384]{2,1,0:T(8,128)(2,1)}), bf16[32,16,384]{2,1,0:T(8,128)(2,1)S(1)}, u32[]{:S(2)}, u32[]{:S(2)}) async-start(bf16[32,16,384]{2,1,0:T(8,128)(2,1)} %broadcast_in_dim.62), calls=%async_computation.4 | async-start | bytes 786432 | tf_op jit(solution)/shard_map/all_to_all | solution.py:34
  133.2 15.3 %copy-start.3 = (f32[64,768]{1,0:T(8,128)S(1)}, f32[64,768]{1,0:T(8,128)}, u32[]{:S(2)}) copy-start(f32[64,768]{1,0:T(8,128)} %param.11) | copy-start | bytes 589828
  133.2 15.3 %copy-start.4 = (f32[64,768]{1,0:T(8,128)S(1)}, f32[64,768]{1,0:T(8,128)}, u32[]{:S(2)}) copy-start(f32[64,768]{1,0:T(8,128)} %param.10) | copy-start | bytes 589828
  133.2 15.3 %copy-start.5 = (f32[64,768]{1,0:T(8,128)S(1)}, f32[64,768]{1,0:T(8,128)}, u32[]{:S(2)}) copy-start(f32[64,768]{1,0:T(8,128)} %param.12) | copy-start | bytes 589828
  133.3 15.3 %copy-start.6 = (f32[64,768]{1,0:T(8,128)S(1)}, f32[64,768]{1,0:T(8,128)}, u32[]{:S(2)}) copy-start(f32[64,768]{1,0:T(8,128)} %param.13) | copy-start | bytes 589828

commit v4 on v3

v4 whole, which is shorter than its diff:
```python
import jax
import jax.numpy as jnp
from jax import lax
from jax.experimental import pallas as pl
from jax.experimental.pallas import tpu as pltpu
from jax.sharding import Mesh, PartitionSpec as P


STEP = 100


beta_one = 0.9
beta_two = 0.999
adam_eps = 1e-08
learn_rate = 0.0002
decay_rate = 0.04
ema_keep = 0.994

REP = ("x", "yh", "core")
SHARD = ("yl", "z")
SWAP = [(0, 1), (1, 0)]


def adamw_update(gradient, weights, teacher, moment_one, moment_two):
    first_new = beta_one * moment_one + (1.0 - beta_one) * gradient
    second_new = beta_two * moment_two + (1.0 - beta_two) * gradient * gradient
    fix_one = 1.0 - beta_one**STEP
    fix_two = 1.0 - beta_two**STEP
    direction = first_new / fix_one / (jnp.sqrt(second_new / fix_two) + adam_eps)
    student_new = weights - learn_rate * (direction + decay_rate * weights)
    teacher_new = ema_keep * teacher + (1.0 - ema_keep) * student_new
    return (student_new, teacher_new, first_new, second_new, direction)


def spread(piece, axes, members):
    copies = jnp.broadcast_to(piece[None], (members,) + piece.shape)
    return lax.all_to_all(copies, axes, 0, 0, tiled=True)


def exchange(pieces, axes):
    return lax.all_to_all(pieces, axes, 0, 0, tiled=True)


def halves_in_order(mine, theirs, index):
    return jnp.where(
        index == 0, jnp.concatenate([mine, theirs], 1), jnp.concatenate([theirs, mine], 1)
    )


def products(
    t0, t1, t2, t3, mask_rows, weights, mask_token, features, gradient, blocks, total, sems
):
    own, quarter = features.shape[1:]
    copies = [
        pltpu.make_async_copy(t, blocks.at[j], sems.at[j]) for j, t in enumerate((t0, t1, t2, t3))
    ]
    for copy in copies:
        copy.start()
    by_rows = (((0,), (0,)), ((), ()))
    mask_out = jnp.dot(
        mask_token[...], weights[...], preferred_element_type=jnp.float32
    )[:1, :quarter]
    masked_sum = jnp.zeros((1, quarter), jnp.float32)
    for j, copy in enumerate(copies):
        copy.wait()
        block = blocks[j]
        product = jnp.dot(block, weights[...], preferred_element_type=jnp.float32)
        flags = jnp.broadcast_to(mask_rows[j], (128, own)).T[:, :1] == 1.0
        feature = product[:, quarter:].astype(jnp.bfloat16)
        features[j] = feature
        student = jnp.where(flags, mask_out, product[:, :quarter])
        difference = (student - feature.astype(jnp.float32)).astype(jnp.bfloat16)
        difference = difference.astype(jnp.float32)
        zero = jnp.zeros_like(difference)
        masked_sum += jnp.where(flags, difference, zero).sum(0, keepdims=True)
        kept = jnp.where(flags, zero, difference).astype(jnp.bfloat16)
        part = lax.dot_general(block, kept, by_rows, preferred_element_type=jnp.float32)
        if j == 0:
            total[...] = part
        else:
            total[...] += part
    coarse = masked_sum.astype(jnp.bfloat16).astype(jnp.float32)
    row = lax.broadcasted_iota(jnp.int32, (mask_token.shape[0], quarter), 0)
    terms = jnp.where(row == 0, coarse, jnp.where(row == 1, masked_sum - coarse, 0.0))
    part = lax.dot_general(
        mask_token[...], terms.astype(jnp.bfloat16), by_rows, preferred_element_type=jnp.float32
    )
    full = (total[...] + part).astype(jnp.bfloat16)
    nx, shard_count, rows, _ = gradient.shape
    full = full.reshape(shard_count, nx, rows, quarter)
    for x in range(nx):
        gradient[x] = full[:, x]


def step(tokens, patch_mask, mask_token, student_w, teacher_w, first_moment, second_moment):
    nx, nh, nl, nz = (lax.axis_size(a) for a in ("x", "yh", "yl", "z"))
    core, side = lax.axis_index("core"), lax.axis_index("yl")
    shard_count = nl * nz
    own, depth = tokens.shape
    rows, width = student_w.shape
    half, quarter = width // 2, width // 4
    part = rows // nx
    row_total = float(own * shard_count * nx * nh * 2)

    place = (lax.axis_index("x") * part, core * half)
    cut = lambda w: lax.dynamic_slice(w, place, (part, half)).astype(jnp.bfloat16)
    student_cut, teacher_cut = cut(student_w), cut(teacher_w)
    pieces = jnp.stack(
        [
            jnp.concatenate([student_cut[:, :quarter], teacher_cut[:, :quarter]], 1),
            jnp.concatenate([student_cut[:, quarter:], teacher_cut[:, quarter:]], 1),
        ]
    )
    pieces = jnp.broadcast_to(pieces[:, None], (nl, nz, part, half))
    gathered = exchange(pieces.reshape(shard_count, part, half), SHARD)
    across = lax.ppermute(tokens, "core", SWAP)
    beside = lax.ppermute(tokens, "yl", SWAP)
    gathered, across, beside = lax.optimization_barrier((gathered, across, beside))
    gathered = spread(gathered, "x", nx)
    weights = gathered.transpose(1, 0, 2, 3).reshape(depth, half)
    corner = lax.ppermute(beside, "core", SWAP)
    flags = patch_mask.astype(jnp.float32)
    flags = jnp.stack([flags, lax.ppermute(flags, "yl", SWAP)])
    flags = jnp.concatenate([flags, lax.ppermute(flags, "core", SWAP)])

    any_space = pl.BlockSpec(memory_space=pl.ANY)
    features, grad = pl.pallas_call(
        products,
        in_specs=[any_space] * 4 + [pl.BlockSpec(memory_space=pltpu.VMEM)] * 3,
        out_specs=[pl.BlockSpec(memory_space=pltpu.VMEM)] * 2,
        out_shape=[
            jax.ShapeDtypeStruct((4, own, quarter), jnp.bfloat16),
            jax.ShapeDtypeStruct((nx, shard_count, part, quarter), jnp.bfloat16),
        ],
        scratch_shapes=[
            pltpu.VMEM((4, own, depth), jnp.bfloat16),
            pltpu.VMEM((depth, quarter), jnp.float32),
            pltpu.SemaphoreType.DMA((4,)),
        ],
    )(
        tokens,
        beside,
        across,
        corner,
        flags[:, None, :],
        weights,
        jnp.broadcast_to(mask_token[None], (16, depth)),
    )

    grad = exchange(grad, "x")
    grad = grad.astype(jnp.float32).sum(0)
    from_side = lax.ppermute(features[1::2], "yl", SWAP)
    grad, from_side = lax.optimization_barrier((grad, from_side))
    grad = exchange(grad.astype(jnp.bfloat16), SHARD)
    from_core = lax.ppermute(jnp.stack([features[2], from_side[1]]), "core", SWAP)
    grad, from_core = lax.optimization_barrier((grad, from_core))
    grad = grad.astype(jnp.float32).reshape(nl, nz, part, quarter).sum(1)
    teacher_feat = halves_in_order(
        halves_in_order(features[0], from_side[0], side),
        halves_in_order(from_core[0], from_core[1], side),
        core,
    )

    grad = jnp.concatenate([grad[0], grad[1]], 1).astype(jnp.bfloat16)
    grad = spread(grad, REP, nx * nh * 2)
    grad = grad.reshape(nx, nh, 2, part, half)
    grad = grad.astype(jnp.float32).sum(1).transpose(0, 2, 1, 3)
    gradient = grad.reshape(rows, width) / row_total
    student_new, teacher_new, first_new, second_new, direction = adamw_update(
        gradient, student_w, teacher_w, first_moment, second_moment
    )
    return (teacher_feat, student_new, teacher_new, first_new, second_new, direction)


def solution(mesh, sizes=(4, 4, 2, 2, 12)):
    fine = Mesh(mesh.devices.reshape(sizes), REP + SHARD)
    tok, row = P(REP + SHARD), P(SHARD, None)
    return jax.shard_map(
        step,
        mesh=fine,
        in_specs=(P(REP + SHARD, None), tok, P(), row, row, row, row),
        out_specs=(P(REP + SHARD, None), row, row, row, row, row),
        check_vma=False,
    )
```

time: 150 us -> 149 us (level)
  blocking collectives: 0 us -> 29.1 us
  starting transfers between devices: 67.9 us -> 54.5 us
  Pallas kernels: 0 us -> 11.3 us
  waiting for transfers between devices: 51.5 us -> 41.7 us
  local copies, waits for them, and re-layouts: 16.5 us -> 7.28 us
  matrix products: 6 us -> 0 us
  other arithmetic: 6.6 us -> 3.69 us
    all_to_all x0 -> x1, blocking collectives: none -> 29.1 us  [exchange(): return lax.all_to_all(pieces, axes, 0, 0, tiled=True)]
    all_to_all x3 -> x2, starting transfers between devices: 29.3 us -> 10.7 us  [exchange(): return lax.all_to_all(pieces, axes, 0, 0, tiled=True)]
    pallas_call x0 -> x1, Pallas kernels: none -> 11.3 us  [step(): pl.pallas_call(products, in_specs=[any_space] * 4 + [pl.BlockSpec(memory_...]
    all_to_all x3 -> x2, waiting for transfers between devices: 22.4 us -> 15.3 us  [exchange(): return lax.all_to_all(pieces, axes, 0, 0, tiled=True)]
    ppermute x6 -> x7, starting transfers between devices: 21.7 us -> 27.9 us  [the longest x1 12.4 us: step(): across = lax.ppermute(tokens, 'core', SWAP)]
    dot_general x3 -> x0, matrix products: 6 us -> none  [the longest x1 4.56 us: shards(): product = jnp.dot(shared, weights, preferred_element_type=jnp.float32)]
    unnamed x28 -> x20, local copies, waits for them, and re-layouts: 4.66 us -> 0.93 us
    concatenate x2 -> x1, local copies, waits for them, and re-layouts: 3.27 us -> 0.01 us  [step(): grad = jnp.concatenate([grad[0], grad[1]], 1).astype(jnp.bfloat16)]
  transfers between devices with their start and end apart: 11 -> 11, of which waited for: 8 -> 7; matrix products, arithmetic and copies ran while one was open for 7% -> 5% of each run, Pallas kernels for 0% -> 0%
where the time goes in v4:
time: 149 us
  starting transfers between devices  54.5 us (37%)
  waiting for transfers between devices  41.7 us (28%)
  blocking collectives  29.1 us (20%)
  Pallas kernels  11.3 us (8%)
  local copies, waits for them, and re-layouts  7.28 us (5%)
  other arithmetic  3.69 us (2%)
    all_to_all x1, blocking collectives, exchange(): return lax.all_to_all(pieces, axes, 0, 0, tiled=True)  29.1 us
    all_to_all x2, waiting for transfers between devices, spread(): return lax.all_to_all(copies, axes, 0, 0, tiled=True)  21.6 us
    all_to_all x2, starting transfers between devices, spread(): return lax.all_to_all(copies, axes, 0, 0, tiled=True)  15.9 us
    all_to_all x2, waiting for transfers between devices, exchange(): return lax.all_to_all(pieces, axes, 0, 0, tiled=True)  15.3 us
    ppermute x1, starting transfers between devices, step(): across = lax.ppermute(tokens, 'core', SWAP)  12.4 us
    pallas_call x1, Pallas kernels, step(): pl.pallas_call(products, in_specs=[any_space] * 4 + [pl.BlockSpec(memory_...  11.3 us
    all_to_all x2, starting transfers between devices, exchange(): return lax.all_to_all(pieces, axes, 0, 0, tiled=True)  10.7 us
    ppermute x1, starting transfers between devices, step(): lax.ppermute(jnp.stack([features[2], from_side[1]]), 'core', SWAP)  4.2 us
  transfers between devices with their start and end apart: 11, of which 7 were waited for; matrix products, arithmetic and copies ran while one was open for 5% of the time, Pallas kernels for 0%

profile of v4, /device:TPU:1, one launch (start us, length us, event | category | flops | bytes accessed | tf_op | source)
XLA Modules:
  0.0 148.5 jit_solution(2252701746948862747)
XLA Ops:
  0.6 12.4 %collective-permute-start = (bf16[384,1536]{1,0:T(8,128)(2,1)}, bf16[384,1536]{1,0:T(8,128)(2,1)S(1)}, u32[]{:S(2)}, u32[]{:S(2)}) collective-permute-start(bf16[384,1536]{1,0:T(8,128)(2,1)} %t0.1), channel_id=1, source_target_pairs={{0,24},{24,0},{1,25},{25,1},{2,26},{26,2},{3,27},{27,3},{4,28},{28... | collective-permute-start | bytes 3538952 | tf_op jit(solution)/shard_map/ppermute | solution.py:116
  13.0 1.9 %collective-permute-start.1 = (bf16[384,1536]{1,0:T(8,128)(2,1)}, bf16[384,1536]{1,0:T(8,128)(2,1)S(1)}, u32[]{:S(2)}, u32[]{:S(2)}) collective-permute-start(bf16[384,1536]{1,0:T(8,128)(2,1)} %t0.1), channel_id=1, source_target_pairs={{0,12},{12,0},{1,13},{13,1},{2,14},{14,2},{3,15},{15,3},{4,16},{16... | collective-permute-start | bytes 3538952 | tf_op jit(solution)/shard_map/ppermute | solution.py:117
  15.0 0.7 dynamic_slice.11
  15.7 0.1 fusion
  15.8 0.7 dynamic_slice.10
  16.5 0.1 fusion.1
  16.6 0.1 maximum_bitcast_fusion
  16.7 29.1 %all_to_all.25 = bf16[24,16,384]{2,1,0:T(8,128)(2,1)S(1)} all-to-all(bf16[24,16,384]{2,1,0:T(8,128)(2,1)S(1)} %bitcast.35), channel_id=1, replica_groups=mesh['x'=4,'yh'=4,'core'=2,'yl'=2,'z'=12] {'yl','z'}, dimensions={0} | all-to-all | bytes 589824 | tf_op jit(solution)/shard_map/all_to_all | solution.py:41
  45.8 0.0 collective-permute-done.t2
  45.8 2.8 %collective-permute-start.2 = (bf16[384,1536]{1,0:T(8,128)(2,1)S(1)}, bf16[384,1536]{1,0:T(8,128)(2,1)}, u32[]{:S(2)}, u32[]{:S(2)}) collective-permute-start(bf16[384,1536]{1,0:T(8,128)(2,1)S(1)} %collective-permute-done.1.t1), channel_id=1, source_target_pairs={{0,24},{24,0},{1,25},{25,1},{2,26},{26,2},{3,27},{27,3},{4,28},{28... | collective-permute-start | bytes 3538952 | tf_op jit(solution)/shard_map/ppermute | solution.py:121
  48.6 1.1 broadcast_in_dim.12
  49.7 3.7 %all-to-all-start.1 = ((bf16[4,24,16,384]{3,2,1,0:T(8,128)(2,1)}), bf16[4,24,16,384]{3,2,1,0:T(8,128)(2,1)S(1)}, u32[]{:S(2)}, u32[]{:S(2)}) async-start(bf16[4,24,16,384]{3,2,1,0:T(8,128)(2,1)} %broadcast_in_dim.12), calls=%async_computation.1 | async-start | bytes 2359296 | tf_op jit(solution)/shard_map/all_to_all | solution.py:37
  53.4 1.9 %collective-permute-start.3 = (f32[384]{0:T(512)S(1)}, f32[384]{0:T(512)S(1)}, u32[]{:S(2)}, u32[]{:S(2)}) collective-permute-start(f32[384]{0:T(512)S(1)} %convert_element_type.29), channel_id=1, source_target_pairs={{0,12},{12,0},{1,13},{13,1},{2,14},{14,2},{3,15},{15,3},{4,16},{16... | collective-permute-start | bytes 4616 | tf_op jit(solution)/shard_map/ppermute | solution.py:123
  55.4 2.7 %collective-permute-done.3 = f32[384]{0:T(512)S(1)} collective-permute-done((f32[384]{0:T(512)S(1)}, f32[384]{0:T(512)S(1)}, u32[]{:S(2)}, u32[]{:S(2)}) %collective-permute-start.3) | collective-permute-done | bytes 1568 | tf_op jit(solution)/shard_map/ppermute | solution.py:123
  58.1 2.8 %collective-permute-start.4 = (f32[2,384]{1,0:T(2,128)S(1)}, f32[2,384]{1,0:T(2,128)S(1)}, u32[]{:S(2)}, u32[]{:S(2)}) collective-permute-start(f32[2,384]{1,0:T(2,128)S(1)} %pad_maximum_fusion.4), channel_id=1, source_target_pairs={{0,24},{24,0},{1,25},{25,1},{2,26},{26,2},{3,27},{27,3},{4,28},{28... | collective-permute-start | bytes 9224 | tf_op jit(solution)/shard_map/ppermute | solution.py:124
  60.9 0.8 collective-permute-done.4
  61.7 0.6 broadcast_in_dim.11.mask_rows
  62.3 7.7 %all-to-all-done.1 = bf16[4,24,16,384]{3,2,1,0:T(8,128)(2,1)S(1)} async-done(((bf16[4,24,16,384]{3,2,1,0:T(8,128)(2,1)}), bf16[4,24,16,384]{3,2,1,0:T(8,128)(2,1)S(1)}, u32[]{:S(2)}, u32[]{:S(2)}) %all-to-all-start.1) | async-done | bytes 1179680 | tf_op jit(solution)/shard_map/all_to_all | solution.py:37
  70.0 1.2 copy.15
  71.2 0.6 broadcast_in_dim.13.mask_token
  71.8 11.3 %shard_map.118 = (bf16[4,384,192]{2,1,0:T(8,128)(2,1)}, bf16[4,24,16,192]{3,2,1,0:T(8,128)(2,1)}) custom-call(bf16[384,1536]{1,0:T(8,128)(2,1)} %t0.1, bf16[384,1536]{1,0:T(8,128)(2,1)} %copy-done.1, bf16[384,1536]{1,0:T(8,128)(2,1)} %copy-done, bf16[384,1536]{1,0:T(8,128)(2,1)} %collective-permute-done.2.t3, f32[4,1,384]{2,1,0:T(1,128)} %broadcast_in_dim.11.mask_rows, ...), custom_call_target="tpu_custom_call" | custom-call | tf_op jit(solution)/shard_map/pallas_call | solution.py:127
  83.2 3.6 %all-to-all-start.2 = ((bf16[4,24,16,192]{3,2,1,0:T(8,128)(2,1)}), bf16[4,24,16,192]{3,2,1,0:T(8,128)(2,1)S(1)}, u32[]{:S(2)}, u32[]{:S(2)}) async-start(bf16[4,24,16,192]{3,2,1,0:T(8,128)(2,1)} %get-tuple-element.19), calls=%async_computation.2 | async-start | bytes 1572864 | tf_op jit(solution)/shard_map/all_to_all | solution.py:41
  86.9 1.9 %collective-permute-start.5 = (bf16[2,384,192]{2,1,0:T(8,128)(2,1)S(1)}, bf16[2,384,192]{2,1,0:T(8,128)(2,1)S(1)}, u32[]{:S(2)}, u32[]{:S(2)}) collective-permute-start(bf16[2,384,192]{2,1,0:T(8,128)(2,1)S(1)} %slice.46), channel_id=1, source_target_pairs={{0,12},{12,0},{1,13},{13,1},{2,14},{14,2},{3,15},{15,3},{4,16},{16... | collective-permute-start | bytes 884744 | tf_op jit(solution)/shard_map/ppermute | solution.py:152
  88.8 9.5 %all-to-all-done.2 = bf16[4,24,16,192]{3,2,1,0:T(8,128)(2,1)S(1)} async-done(((bf16[4,24,16,192]{3,2,1,0:T(8,128)(2,1)}), bf16[4,24,16,192]{3,2,1,0:T(8,128)(2,1)S(1)}, u32[]{:S(2)}, u32[]{:S(2)}) %all-to-all-start.2) | async-done | bytes 589856 | tf_op jit(solution)/shard_map/all_to_all | solution.py:41
  98.3 0.8 convert_reduce_fusion
  99.1 7.1 %all-to-all-start.3 = ((bf16[24,16,192]{2,1,0:T(8,128)(2,1)}), bf16[24,16,192]{2,1,0:T(8,128)(2,1)S(1)}, u32[]{:S(2)}, u32[]{:S(2)}) async-start(bf16[24,16,192]{2,1,0:T(8,128)(2,1)} %convert_reduce_fusion), calls=%async_computation.3 | async-start | bytes 393216 | tf_op jit(solution)/shard_map/all_to_all | solution.py:41
  106.2 0.1 pad_maximum_fusion
  106.3 4.2 %collective-permute-start.6 = (bf16[2,384,192]{2,1,0:T(8,128)(2,1)S(1)}, bf16[2,384,192]{2,1,0:T(8,128)(2,1)S(1)}, u32[]{:S(2)}, u32[]{:S(2)}) collective-permute-start(bf16[2,384,192]{2,1,0:T(8,128)(2,1)S(1)} %pad_maximum_fusion), channel_id=1, source_target_pairs={{0,24},{24,0},{1,25},{25,1},{2,26},{26,2},{3,27},{27,3},{4,28},{28... | collective-permute-start | bytes 884744 | tf_op jit(solution)/shard_map/ppermute | solution.py:155
  110.5 1.3 collective-permute-done.6
  111.9 5.8 %all-to-all-done.3 = bf16[24,16,192]{2,1,0:T(8,128)(2,1)S(1)} async-done(((bf16[24,16,192]{2,1,0:T(8,128)(2,1)}), bf16[24,16,192]{2,1,0:T(8,128)(2,1)S(1)}, u32[]{:S(2)}, u32[]{:S(2)}) %all-to-all-start.3) | async-done | bytes 147488 | tf_op jit(solution)/shard_map/all_to_all | solution.py:41
  117.7 0.1 pad_maximum_fusion.2
  117.8 0.8 broadcast_in_dim.14
  118.6 12.2 %all-to-all-start.4 = ((bf16[32,16,384]{2,1,0:T(8,128)(2,1)}), bf16[32,16,384]{2,1,0:T(8,128)(2,1)S(1)}, u32[]{:S(2)}, u32[]{:S(2)}) async-start(bf16[32,16,384]{2,1,0:T(8,128)(2,1)} %broadcast_in_dim.14), calls=%async_computation.4 | async-start | bytes 786432 | tf_op jit(solution)/shard_map/all_to_all | solution.py:37
  130.8 0.3 maximum_select_fusion.1
  131.1 0.3 maximum_select_fusion.2
  131.3 1.0 maximum_select_fusion
  132.3 13.9 %all-to-all-done.4 = bf16[32,16,384]{2,1,0:T(8,128)(2,1)S(1)} async-done(((bf16[32,16,384]{2,1,0:T(8,128)(2,1)}), bf16[32,16,384]{2,1,0:T(8,128)(2,1)S(1)}, u32[]{:S(2)}, u32[]{:S(2)}) %all-to-all-start.4) | async-done | bytes 393248 | tf_op jit(solution)/shard_map/all_to_all | solution.py:37
  146.3 0.0 copy-start.3
  146.3 0.0 copy-start.4
  146.3 0.0 copy-start.5
  146.3 0.0 copy-start.6
  146.4 0.1 copy.17
  146.5 0.1 copy.16
  146.6 0.6 copy-done.3
  147.2 0.1 copy-done.4
  147.3 0.1 copy-done.5
  147.4 0.1 copy-done.6
  147.5 1.0 multiply_add_fusion
  (30 shorter events, 0.4 us)
Async XLA Ops:
  0.6 45.2 %collective-permute-start = (bf16[384,1536]{1,0:T(8,128)(2,1)}, bf16[384,1536]{1,0:T(8,128)(2,1)S(1)}, u32[]{:S(2)}, u32[]{:S(2)}) collective-permute-start(bf16[384,1536]{1,0:T(8,128)(2,1)} %t0.1), channel_id=1, source_target_pairs={{0,24},{24,0},{1,25},{25,1},{2,26},{26,2},{3,27},{27,3},{4,28},{28... | collective-permute-start | bytes 3538952 | tf_op jit(solution)/shard_map/ppermute | solution.py:116
  13.0 32.8 %collective-permute-start.1 = (bf16[384,1536]{1,0:T(8,128)(2,1)}, bf16[384,1536]{1,0:T(8,128)(2,1)S(1)}, u32[]{:S(2)}, u32[]{:S(2)}) collective-permute-start(bf16[384,1536]{1,0:T(8,128)(2,1)} %t0.1), channel_id=1, source_target_pairs={{0,12},{12,0},{1,13},{13,1},{2,14},{14,2},{3,15},{15,3},{4,16},{16... | collective-permute-start | bytes 3538952 | tf_op jit(solution)/shard_map/ppermute | solution.py:117
  45.8 3.9 %copy-start = (bf16[384,1536]{1,0:T(8,128)(2,1)}, bf16[384,1536]{1,0:T(8,128)(2,1)S(1)}, u32[]{:S(2)}) copy-start(bf16[384,1536]{1,0:T(8,128)(2,1)S(1)} %collective-permute-done.t2) | copy-start | bytes 3538948
  45.8 3.9 %copy-start.1 = (bf16[384,1536]{1,0:T(8,128)(2,1)}, bf16[384,1536]{1,0:T(8,128)(2,1)S(1)}, u32[]{:S(2)}) copy-start(bf16[384,1536]{1,0:T(8,128)(2,1)S(1)} %collective-permute-done.1.t1) | copy-start | bytes 3538948
  45.8 25.4 %collective-permute-start.2 = (bf16[384,1536]{1,0:T(8,128)(2,1)S(1)}, bf16[384,1536]{1,0:T(8,128)(2,1)}, u32[]{:S(2)}, u32[]{:S(2)}) collective-permute-start(bf16[384,1536]{1,0:T(8,128)(2,1)S(1)} %collective-permute-done.1.t1), channel_id=1, source_target_pairs={{0,24},{24,0},{1,25},{25,1},{2,26},{26,2},{3,27},{27,3},{4,28},{28... | collective-permute-start | bytes 3538952 | tf_op jit(solution)/shard_map/ppermute | solution.py:121
  49.7 3.7 %copy-start.8 = (s32[384]{0:T(512)S(1)}, s32[384]{0:T(512)}, u32[]{:S(2)}) copy-start(s32[384]{0:T(512)} %param.8) | copy-start | bytes 4612
  49.7 20.2 %all-to-all-start.1 = ((bf16[4,24,16,384]{3,2,1,0:T(8,128)(2,1)}), bf16[4,24,16,384]{3,2,1,0:T(8,128)(2,1)S(1)}, u32[]{:S(2)}, u32[]{:S(2)}) async-start(bf16[4,24,16,384]{3,2,1,0:T(8,128)(2,1)} %broadcast_in_dim.12), calls=%async_computation.1 | async-start | bytes 2359296 | tf_op jit(solution)/shard_map/all_to_all | solution.py:37
  53.4 4.6 %collective-permute-start.3 = (f32[384]{0:T(512)S(1)}, f32[384]{0:T(512)S(1)}, u32[]{:S(2)}, u32[]{:S(2)}) collective-permute-start(f32[384]{0:T(512)S(1)} %convert_element_type.29), channel_id=1, source_target_pairs={{0,12},{12,0},{1,13},{13,1},{2,14},{14,2},{3,15},{15,3},{4,16},{16... | collective-permute-start | bytes 4616 | tf_op jit(solution)/shard_map/ppermute | solution.py:123
  58.1 3.6 %collective-permute-start.4 = (f32[2,384]{1,0:T(2,128)S(1)}, f32[2,384]{1,0:T(2,128)S(1)}, u32[]{:S(2)}, u32[]{:S(2)}) collective-permute-start(f32[2,384]{1,0:T(2,128)S(1)} %pad_maximum_fusion.4), channel_id=1, source_target_pairs={{0,24},{24,0},{1,25},{25,1},{2,26},{26,2},{3,27},{27,3},{4,28},{28... | collective-permute-start | bytes 9224 | tf_op jit(solution)/shard_map/ppermute | solution.py:124
  70.0 1.2 copy-start.7
  83.2 3.7 %copy-start.2 = (bf16[4,384,192]{2,1,0:T(8,128)(2,1)S(1)}, bf16[4,384,192]{2,1,0:T(8,128)(2,1)}, u32[]{:S(2)}) copy-start(bf16[4,384,192]{2,1,0:T(8,128)(2,1)} %get-tuple-element.18) | copy-start | bytes 1769476
  83.2 15.1 %all-to-all-start.2 = ((bf16[4,24,16,192]{3,2,1,0:T(8,128)(2,1)}), bf16[4,24,16,192]{3,2,1,0:T(8,128)(2,1)S(1)}, u32[]{:S(2)}, u32[]{:S(2)}) async-start(bf16[4,24,16,192]{3,2,1,0:T(8,128)(2,1)} %get-tuple-element.19), calls=%async_computation.2 | async-start | bytes 1572864 | tf_op jit(solution)/shard_map/all_to_all | solution.py:41
  86.9 12.2 %collective-permute-start.5 = (bf16[2,384,192]{2,1,0:T(8,128)(2,1)S(1)}, bf16[2,384,192]{2,1,0:T(8,128)(2,1)S(1)}, u32[]{:S(2)}, u32[]{:S(2)}) collective-permute-start(bf16[2,384,192]{2,1,0:T(8,128)(2,1)S(1)} %slice.46), channel_id=1, source_target_pairs={{0,12},{12,0},{1,13},{13,1},{2,14},{14,2},{3,15},{15,3},{4,16},{16... | collective-permute-start | bytes 884744 | tf_op jit(solution)/shard_map/ppermute | solution.py:152
  99.1 18.5 %all-to-all-start.3 = ((bf16[24,16,192]{2,1,0:T(8,128)(2,1)}), bf16[24,16,192]{2,1,0:T(8,128)(2,1)S(1)}, u32[]{:S(2)}, u32[]{:S(2)}) async-start(bf16[24,16,192]{2,1,0:T(8,128)(2,1)} %convert_reduce_fusion), calls=%async_computation.3 | async-start | bytes 393216 | tf_op jit(solution)/shard_map/all_to_all | solution.py:41
  106.3 5.5 %collective-permute-start.6 = (bf16[2,384,192]{2,1,0:T(8,128)(2,1)S(1)}, bf16[2,384,192]{2,1,0:T(8,128)(2,1)S(1)}, u32[]{:S(2)}, u32[]{:S(2)}) collective-permute-start(bf16[2,384,192]{2,1,0:T(8,128)(2,1)S(1)} %pad_maximum_fusion), channel_id=1, source_target_pairs={{0,24},{24,0},{1,25},{25,1},{2,26},{26,2},{3,27},{27,3},{4,28},{28... | collective-permute-start | bytes 884744 | tf_op jit(solution)/shard_map/ppermute | solution.py:155
  118.6 27.6 %all-to-all-start.4 = ((bf16[32,16,384]{2,1,0:T(8,128)(2,1)}), bf16[32,16,384]{2,1,0:T(8,128)(2,1)S(1)}, u32[]{:S(2)}, u32[]{:S(2)}) async-start(bf16[32,16,384]{2,1,0:T(8,128)(2,1)} %broadcast_in_dim.14), calls=%async_computation.4 | async-start | bytes 786432 | tf_op jit(solution)/shard_map/all_to_all | solution.py:37
  146.3 0.9 copy-start.3
  146.3 1.0 copy-start.4
  146.3 1.1 copy-start.5
  146.3 1.2 copy-start.6

commit v5 on v4

--- a/solution.py
+++ b/solution.py
@@ -48,23 +48,29 @@
 
 
 def products(
-    t0, t1, t2, t3, mask_rows, weights, mask_token, features, gradient, blocks, total, sems
+    t0, t1, t2, t3, gathered, mask_rows, mask_token, features, gradient, blocks, held, kept, sems
 ):
     own, quarter = features.shape[1:]
+    nx, shard_count, rows, _ = gradient.shape
+    loads = [
+        pltpu.make_async_copy(gathered.at[x], held.at[:, x], sems.at[x]) for x in range(nx)
+    ]
     copies = [
-        pltpu.make_async_copy(t, blocks.at[j], sems.at[j]) for j, t in enumerate((t0, t1, t2, t3))
+        pltpu.make_async_copy(t, blocks.at[pl.ds(j * own, own)], sems.at[nx + j])
+        for j, t in enumerate((t0, t1, t2, t3))
     ]
-    for copy in copies:
+    for copy in loads + copies:
         copy.start()
-    by_rows = (((0,), (0,)), ((), ()))
-    mask_out = jnp.dot(
-        mask_token[...], weights[...], preferred_element_type=jnp.float32
-    )[:1, :quarter]
+    for load in loads:
+        load.wait()
+    weights = held[...].reshape(nx * shard_count * rows, 2 * quarter)
+    mask_out = jnp.dot(mask_token[...], weights, preferred_element_type=jnp.float32)
+    mask_out = mask_out[:1, :quarter]
     masked_sum = jnp.zeros((1, quarter), jnp.float32)
     for j, copy in enumerate(copies):
         copy.wait()
-        block = blocks[j]
-        product = jnp.dot(block, weights[...], preferred_element_type=jnp.float32)
+        block = blocks[pl.ds(j * own, own)]
+        product = jnp.dot(block, weights, preferred_element_type=jnp.float32)
         flags = jnp.broadcast_to(mask_rows[j], (128, own)).T[:, :1] == 1.0
         feature = product[:, quarter:].astype(jnp.bfloat16)
         features[j] = feature
@@ -73,21 +79,17 @@
         difference = difference.astype(jnp.float32)
         zero = jnp.zeros_like(difference)
         masked_sum += jnp.where(flags, difference, zero).sum(0, keepdims=True)
-        kept = jnp.where(flags, zero, difference).astype(jnp.bfloat16)
-        part = lax.dot_general(block, kept, by_rows, preferred_element_type=jnp.float32)
-        if j == 0:
-            total[...] = part
-        else:
-            total[...] += part
+        kept[pl.ds(j * own, own)] = jnp.where(flags, zero, difference).astype(jnp.bfloat16)
     coarse = masked_sum.astype(jnp.bfloat16).astype(jnp.float32)
     row = lax.broadcasted_iota(jnp.int32, (mask_token.shape[0], quarter), 0)
     terms = jnp.where(row == 0, coarse, jnp.where(row == 1, masked_sum - coarse, 0.0))
-    part = lax.dot_general(
+    by_rows = (((0,), (0,)), ((), ()))
+    total = lax.dot_general(
+        blocks[...], kept[...], by_rows, preferred_element_type=jnp.float32
+    ) + lax.dot_general(
         mask_token[...], terms.astype(jnp.bfloat16), by_rows, preferred_element_type=jnp.float32
     )
-    full = (total[...] + part).astype(jnp.bfloat16)
-    nx, shard_count, rows, _ = gradient.shape
-    full = full.reshape(shard_count, nx, rows, quarter)
+    full = total.astype(jnp.bfloat16).reshape(shard_count, nx, rows, quarter)
     for x in range(nx):
         gradient[x] = full[:, x]
 
@@ -115,9 +117,9 @@
     gathered = exchange(pieces.reshape(shard_count, part, half), SHARD)
     across = lax.ppermute(tokens, "core", SWAP)
     beside = lax.ppermute(tokens, "yl", SWAP)
-    gathered, across, beside = lax.optimization_barrier((gathered, across, beside))
+    token_rows = jnp.broadcast_to(mask_token[None], (16, depth))
+    gathered, across, token_rows = lax.optimization_barrier((gathered, across, token_rows))
     gathered = spread(gathered, "x", nx)
-    weights = gathered.transpose(1, 0, 2, 3).reshape(depth, half)
     corner = lax.ppermute(beside, "core", SWAP)
     flags = patch_mask.astype(jnp.float32)
     flags = jnp.stack([flags, lax.ppermute(flags, "yl", SWAP)])
@@ -126,25 +128,26 @@
     any_space = pl.BlockSpec(memory_space=pl.ANY)
     features, grad = pl.pallas_call(
         products,
-        in_specs=[any_space] * 4 + [pl.BlockSpec(memory_space=pltpu.VMEM)] * 3,
+        in_specs=[any_space] * 5 + [pl.BlockSpec(memory_space=pltpu.VMEM)] * 2,
         out_specs=[pl.BlockSpec(memory_space=pltpu.VMEM)] * 2,
         out_shape=[
             jax.ShapeDtypeStruct((4, own, quarter), jnp.bfloat16),
             jax.ShapeDtypeStruct((nx, shard_count, part, quarter), jnp.bfloat16),
         ],
         scratch_shapes=[
-            pltpu.VMEM((4, own, depth), jnp.bfloat16),
-            pltpu.VMEM((depth, quarter), jnp.float32),
-            pltpu.SemaphoreType.DMA((4,)),
+            pltpu.VMEM((4 * own, depth), jnp.bfloat16),
+            pltpu.VMEM((shard_count, nx, part, half), jnp.bfloat16),
+            pltpu.VMEM((4 * own, quarter), jnp.bfloat16),
+            pltpu.SemaphoreType.DMA((nx + 4,)),
         ],
     )(
         tokens,
         beside,
         across,
         corner,
+        gathered,
         flags[:, None, :],
-        weights,
-        jnp.broadcast_to(mask_token[None], (16, depth)),
+        token_rows,
     )
 
     grad = exchange(grad, "x")
@@ -162,9 +165,10 @@
     )
 
     grad = jnp.concatenate([grad[0], grad[1]], 1).astype(jnp.bfloat16)
-    grad = spread(grad, REP, nx * nh * 2)
-    grad = grad.reshape(nx, nh, 2, part, half)
-    grad = grad.astype(jnp.float32).sum(1).transpose(0, 2, 1, 3)
+    grad = spread(grad, "yh", nh)
+    grad = grad.astype(jnp.float32).sum(0)
+    grad = spread(grad, ("x", "core"), nx * 2)
+    grad = grad.reshape(nx, 2, part, half).transpose(0, 2, 1, 3)
     gradient = grad.reshape(rows, width) / row_total
     student_new, teacher_new, first_new, second_new, direction = adamw_update(
         gradient, student_w, teacher_w, first_moment, second_moment

time: 149 us -> 144 us (0.966)
  starting transfers between devices: 54.5 us -> 88.8 us
  blocking collectives: 29.1 us -> 0 us
  waiting for transfers between devices: 41.7 us -> 33.3 us
  Pallas kernels: 11.3 us -> 8.64 us
    all_to_all x1 -> x0, blocking collectives: 29.1 us -> none  [exchange(): return lax.all_to_all(pieces, axes, 0, 0, tiled=True)]
    all_to_all x2 -> x3, starting transfers between devices: 10.7 us -> 30.6 us  [exchange(): return lax.all_to_all(pieces, axes, 0, 0, tiled=True)]
    all_to_all x2 -> x3, waiting for transfers between devices: 21.6 us -> 12 us  [spread(): return lax.all_to_all(copies, axes, 0, 0, tiled=True)]
    ppermute x1, starting transfers between devices: 2.78 us -> 9.02 us  [step(): corner = lax.ppermute(beside, 'core', SWAP)]
    ppermute x1, starting transfers between devices: 2.77 us -> 6.58 us  [step(): flags = jnp.concatenate([flags, lax.ppermute(flags, 'core', SWAP)])]
    all_to_all x2 -> x3, starting transfers between devices: 15.9 us -> 19.2 us  [spread(): return lax.all_to_all(copies, axes, 0, 0, tiled=True)]
    pallas_call x1, Pallas kernels: 11.3 us -> 8.64 us  [step(): pl.pallas_call(products, in_specs=[any_space] * 5 + [pl.BlockSpec(memory_...]
    all_to_all x2 -> x3, waiting for transfers between devices: 15.3 us -> 17.7 us  [exchange(): return lax.all_to_all(pieces, axes, 0, 0, tiled=True)]
  transfers between devices with their start and end apart: 11 -> 13, of which waited for: 7 -> 9; matrix products, arithmetic and copies ran while one was open for 5% -> 6% of each run, Pallas kernels for 0% -> 0%
where the time goes in v5:
time: 144 us; the launch traced here: 143 us
  starting transfers between devices  88.8 us (62%)
  waiting for transfers between devices  33.3 us (23%)
  Pallas kernels  8.64 us (6%)
  local copies, waits for them, and re-layouts  8.15 us (6%)
  other arithmetic  3.65 us (3%)
    all_to_all x3, starting transfers between devices, exchange(): return lax.all_to_all(pieces, axes, 0, 0, tiled=True)  30.6 us
    all_to_all x3, starting transfers between devices, spread(): return lax.all_to_all(copies, axes, 0, 0, tiled=True)  19.2 us
    all_to_all x3, waiting for transfers between devices, exchange(): return lax.all_to_all(pieces, axes, 0, 0, tiled=True)  17.7 us
    all_to_all x3, waiting for transfers between devices, spread(): return lax.all_to_all(copies, axes, 0, 0, tiled=True)  12 us
    ppermute x1, starting transfers between devices, step(): across = lax.ppermute(tokens, 'core', SWAP)  10.3 us
    ppermute x1, starting transfers between devices, step(): corner = lax.ppermute(beside, 'core', SWAP)  9.02 us
    pallas_call x1, Pallas kernels, step(): pl.pallas_call(products, in_specs=[any_space] * 5 + [pl.BlockSpec(memory_...  8.64 us
    ppermute x1, starting transfers between devices, step(): flags = jnp.concatenate([flags, lax.ppermute(flags, 'core', SWAP)])  6.58 us
  transfers between devices with their start and end apart: 13, of which 9 were waited for; matrix products, arithmetic and copies ran while one was open for 6% of the time, Pallas kernels for 0%

profile of v5, /device:TPU:1, one launch (start us, length us, event | category | flops | bytes accessed | tf_op | source)
XLA Modules:
  0.0 143.4 jit_solution(7210897077874816170)
XLA Ops:
  0.6 4.0 %collective-permute-start = (bf16[384,1536]{1,0:T(8,128)(2,1)}, bf16[384,1536]{1,0:T(8,128)(2,1)S(1)}, u32[]{:S(2)}, u32[]{:S(2)}) collective-permute-start(bf16[384,1536]{1,0:T(8,128)(2,1)} %t0.1), channel_id=1, source_target_pairs={{0,12},{12,0},{1,13},{13,1},{2,14},{14,2},{3,15},{15,3},{4,16},{16... | collective-permute-start | bytes 3538952 | tf_op jit(solution)/shard_map/ppermute | solution.py:119
  4.7 10.3 %collective-permute-start.1 = (bf16[384,1536]{1,0:T(8,128)(2,1)}, bf16[384,1536]{1,0:T(8,128)(2,1)S(1)}, u32[]{:S(2)}, u32[]{:S(2)}) collective-permute-start(bf16[384,1536]{1,0:T(8,128)(2,1)} %t0.1), channel_id=1, source_target_pairs={{0,24},{24,0},{1,25},{25,1},{2,26},{26,2},{3,27},{27,3},{4,28},{28... | collective-permute-start | bytes 3538952 | tf_op jit(solution)/shard_map/ppermute | solution.py:118
  15.0 0.7 dynamic_slice.11
  15.7 0.7 dynamic_slice.10
  16.5 0.1 fusion
  16.5 0.1 fusion.1
  16.6 0.1 maximum_bitcast_fusion
  16.7 0.7 broadcast_in_dim.12
  17.4 7.7 %all-to-all-start = ((bf16[24,16,384]{2,1,0:T(8,128)(2,1)}), bf16[24,16,384]{2,1,0:T(8,128)(2,1)S(1)}, u32[]{:S(2)}, u32[]{:S(2)}) async-start(bf16[24,16,384]{2,1,0:T(8,128)(2,1)} %bitcast.2), calls=%async_computation | async-start | bytes 589824 | tf_op jit(solution)/shard_map/all_to_all | solution.py:41
  25.1 0.0 collective-permute-done.t1
  25.1 9.0 %collective-permute-start.2 = (bf16[384,1536]{1,0:T(8,128)(2,1)S(1)}, bf16[384,1536]{1,0:T(8,128)(2,1)}, u32[]{:S(2)}, u32[]{:S(2)}) collective-permute-start(bf16[384,1536]{1,0:T(8,128)(2,1)S(1)} %collective-permute-done.t1), channel_id=1, source_target_pairs={{0,24},{24,0},{1,25},{25,1},{2,26},{26,2},{3,27},{27,3},{4,28},{28... | collective-permute-start | bytes 3538952 | tf_op jit(solution)/shard_map/ppermute | solution.py:123
  34.2 6.0 %all-to-all-done = bf16[24,16,384]{2,1,0:T(8,128)(2,1)S(1)} async-done(((bf16[24,16,384]{2,1,0:T(8,128)(2,1)}), bf16[24,16,384]{2,1,0:T(8,128)(2,1)S(1)}, u32[]{:S(2)}, u32[]{:S(2)}) %all-to-all-start) | async-done | bytes 294944 | tf_op jit(solution)/shard_map/all_to_all | solution.py:41
  40.2 0.0 collective-permute-done.1.t2
  40.2 1.3 broadcast_in_dim.13.mask_token
  41.5 1.1 broadcast_in_dim.14
  42.6 4.1 %all-to-all-start.1 = ((bf16[4,24,16,384]{3,2,1,0:T(8,128)(2,1)}), bf16[4,24,16,384]{3,2,1,0:T(8,128)(2,1)S(1)}, u32[]{:S(2)}, u32[]{:S(2)}) async-start(bf16[4,24,16,384]{3,2,1,0:T(8,128)(2,1)} %broadcast_in_dim.14), calls=%async_computation.1 | async-start | bytes 2359296 | tf_op jit(solution)/shard_map/all_to_all | solution.py:37
  46.8 2.6 %collective-permute-start.3 = (f32[384]{0:T(512)S(1)}, f32[384]{0:T(512)S(1)}, u32[]{:S(2)}, u32[]{:S(2)}) collective-permute-start(f32[384]{0:T(512)S(1)} %convert_element_type.26), channel_id=1, source_target_pairs={{0,12},{12,0},{1,13},{13,1},{2,14},{14,2},{3,15},{15,3},{4,16},{16... | collective-permute-start | bytes 4616 | tf_op jit(solution)/shard_map/ppermute | solution.py:125
  49.4 1.7 %collective-permute-done.3 = f32[384]{0:T(512)S(1)} collective-permute-done((f32[384]{0:T(512)S(1)}, f32[384]{0:T(512)S(1)}, u32[]{:S(2)}, u32[]{:S(2)}) %collective-permute-start.3) | collective-permute-done | bytes 1568 | tf_op jit(solution)/shard_map/ppermute | solution.py:125
  51.1 6.6 %collective-permute-start.4 = (f32[2,384]{1,0:T(2,128)S(1)}, f32[2,384]{1,0:T(2,128)S(1)}, u32[]{:S(2)}, u32[]{:S(2)}) collective-permute-start(f32[2,384]{1,0:T(2,128)S(1)} %pad_maximum_fusion.4), channel_id=1, source_target_pairs={{0,24},{24,0},{1,25},{25,1},{2,26},{26,2},{3,27},{27,3},{4,28},{28... | collective-permute-start | bytes 9224 | tf_op jit(solution)/shard_map/ppermute | solution.py:126
  57.7 0.8 collective-permute-done.4
  58.5 0.6 broadcast_in_dim.15.mask_rows
  59.1 0.4 all-to-all-done.1.gathered
  59.5 0.0 collective-permute-done.2.t3
  59.5 1.0 copy-done
  60.6 8.6 %shard_map.118 = (bf16[4,384,192]{2,1,0:T(8,128)(2,1)}, bf16[4,24,16,192]{3,2,1,0:T(8,128)(2,1)}) custom-call(bf16[384,1536]{1,0:T(8,128)(2,1)} %t0.1, bf16[384,1536]{1,0:T(8,128)(2,1)} %copy-done.1, bf16[384,1536]{1,0:T(8,128)(2,1)} %copy-done.2, bf16[384,1536]{1,0:T(8,128)(2,1)} %collective-permute-done.2.t3, bf16[4,24,16,384]{3,2,1,0:T(8,128)(2,1)} %copy-done, ...), custom_call_target="tpu_custom_call" | custom-call | tf_op jit(solution)/shard_map/pallas_call | solution.py:129
  69.2 4.2 %all-to-all-start.2 = ((bf16[4,24,16,192]{3,2,1,0:T(8,128)(2,1)}), bf16[4,24,16,192]{3,2,1,0:T(8,128)(2,1)S(1)}, u32[]{:S(2)}, u32[]{:S(2)}) async-start(bf16[4,24,16,192]{3,2,1,0:T(8,128)(2,1)} %get-tuple-element.19), calls=%async_computation.2 | async-start | bytes 1572864 | tf_op jit(solution)/shard_map/all_to_all | solution.py:41
  73.5 2.3 %collective-permute-start.5 = (bf16[2,384,192]{2,1,0:T(8,128)(2,1)S(1)}, bf16[2,384,192]{2,1,0:T(8,128)(2,1)S(1)}, u32[]{:S(2)}, u32[]{:S(2)}) collective-permute-start(bf16[2,384,192]{2,1,0:T(8,128)(2,1)S(1)} %slice.46), channel_id=1, source_target_pairs={{0,12},{12,0},{1,13},{13,1},{2,14},{14,2},{3,15},{15,3},{4,16},{16... | collective-permute-start | bytes 884744 | tf_op jit(solution)/shard_map/ppermute | solution.py:155
  75.9 5.9 %all-to-all-done.2 = bf16[4,24,16,192]{3,2,1,0:T(8,128)(2,1)S(1)} async-done(((bf16[4,24,16,192]{3,2,1,0:T(8,128)(2,1)}), bf16[4,24,16,192]{3,2,1,0:T(8,128)(2,1)S(1)}, u32[]{:S(2)}, u32[]{:S(2)}) %all-to-all-start.2) | async-done | bytes 589856 | tf_op jit(solution)/shard_map/all_to_all | solution.py:41
  81.8 0.8 convert_reduce_fusion
  82.6 0.0 collective-permute-done.5
  82.6 18.7 %all-to-all-start.3 = ((bf16[24,16,192]{2,1,0:T(8,128)(2,1)}), bf16[24,16,192]{2,1,0:T(8,128)(2,1)S(1)}, u32[]{:S(2)}, u32[]{:S(2)}) async-start(bf16[24,16,192]{2,1,0:T(8,128)(2,1)} %convert_reduce_fusion), calls=%async_computation.3 | async-start | bytes 393216 | tf_op jit(solution)/shard_map/all_to_all | solution.py:41
  101.3 0.1 pad_maximum_fusion
  101.4 4.2 %collective-permute-start.6 = (bf16[2,384,192]{2,1,0:T(8,128)(2,1)S(1)}, bf16[2,384,192]{2,1,0:T(8,128)(2,1)S(1)}, u32[]{:S(2)}, u32[]{:S(2)}) collective-permute-start(bf16[2,384,192]{2,1,0:T(8,128)(2,1)S(1)} %pad_maximum_fusion), channel_id=1, source_target_pairs={{0,24},{24,0},{1,25},{25,1},{2,26},{26,2},{3,27},{27,3},{4,28},{28... | collective-permute-start | bytes 884744 | tf_op jit(solution)/shard_map/ppermute | solution.py:158
  105.6 0.3 maximum_select_fusion.1
  105.9 1.1 collective-permute-done.6
  106.9 5.8 %all-to-all-done.3 = bf16[24,16,192]{2,1,0:T(8,128)(2,1)S(1)} async-done(((bf16[24,16,192]{2,1,0:T(8,128)(2,1)}), bf16[24,16,192]{2,1,0:T(8,128)(2,1)S(1)}, u32[]{:S(2)}, u32[]{:S(2)}) %all-to-all-start.3) | async-done | bytes 147488 | tf_op jit(solution)/shard_map/all_to_all | solution.py:41
  112.8 0.1 pad_maximum_fusion.2
  112.9 0.6 broadcast_in_dim.16
  113.5 5.9 %all-to-all-start.4 = ((bf16[4,16,384]{2,1,0:T(8,128)(2,1)}), bf16[4,16,384]{2,1,0:T(8,128)(2,1)S(1)}, u32[]{:S(2)}, u32[]{:S(2)}) async-start(bf16[4,16,384]{2,1,0:T(8,128)(2,1)} %broadcast_in_dim.16), calls=%async_computation.4 | async-start | bytes 98304 | tf_op jit(solution)/shard_map/all_to_all | solution.py:37
  119.5 6.9 %all-to-all-done.4 = bf16[4,16,384]{2,1,0:T(8,128)(2,1)S(1)} async-done(((bf16[4,16,384]{2,1,0:T(8,128)(2,1)}), bf16[4,16,384]{2,1,0:T(8,128)(2,1)S(1)}, u32[]{:S(2)}, u32[]{:S(2)}) %all-to-all-start.4) | async-done | bytes 49184 | tf_op jit(solution)/shard_map/all_to_all | solution.py:37
  126.4 0.7 broadcast_in_dim.17
  127.1 9.1 %all-to-all-start.5 = ((f32[8,16,384]{2,1,0:T(8,128)}), f32[8,16,384]{2,1,0:T(8,128)S(1)}, u32[]{:S(2)}, u32[]{:S(2)}) async-start(f32[8,16,384]{2,1,0:T(8,128)} %broadcast_in_dim.17), calls=%async_computation.5 | async-start | bytes 393216 | tf_op jit(solution)/shard_map/all_to_all | solution.py:37
  136.2 0.3 maximum_select_fusion.2
  136.4 0.9 maximum_select_fusion
  137.4 4.6 %all-to-all-done.5 = f32[8,16,384]{2,1,0:T(8,128)S(1)} async-done(((f32[8,16,384]{2,1,0:T(8,128)}), f32[8,16,384]{2,1,0:T(8,128)S(1)}, u32[]{:S(2)}, u32[]{:S(2)}) %all-to-all-start.5) | async-done | bytes 196640 | tf_op jit(solution)/shard_map/all_to_all | solution.py:37
  142.1 0.1 copy.16
  142.2 0.1 copy.15
  142.4 1.0 multiply_add_fusion
  (33 shorter events, 0.3 us)
Async XLA Ops:
  0.6 24.5 %collective-permute-start = (bf16[384,1536]{1,0:T(8,128)(2,1)}, bf16[384,1536]{1,0:T(8,128)(2,1)S(1)}, u32[]{:S(2)}, u32[]{:S(2)}) collective-permute-start(bf16[384,1536]{1,0:T(8,128)(2,1)} %t0.1), channel_id=1, source_target_pairs={{0,12},{12,0},{1,13},{13,1},{2,14},{14,2},{3,15},{15,3},{4,16},{16... | collective-permute-start | bytes 3538952 | tf_op jit(solution)/shard_map/ppermute | solution.py:119
  4.7 35.5 %collective-permute-start.1 = (bf16[384,1536]{1,0:T(8,128)(2,1)}, bf16[384,1536]{1,0:T(8,128)(2,1)S(1)}, u32[]{:S(2)}, u32[]{:S(2)}) collective-permute-start(bf16[384,1536]{1,0:T(8,128)(2,1)} %t0.1), channel_id=1, source_target_pairs={{0,24},{24,0},{1,25},{25,1},{2,26},{26,2},{3,27},{27,3},{4,28},{28... | collective-permute-start | bytes 3538952 | tf_op jit(solution)/shard_map/ppermute | solution.py:118
  17.4 22.7 %all-to-all-start = ((bf16[24,16,384]{2,1,0:T(8,128)(2,1)}), bf16[24,16,384]{2,1,0:T(8,128)(2,1)S(1)}, u32[]{:S(2)}, u32[]{:S(2)}) async-start(bf16[24,16,384]{2,1,0:T(8,128)(2,1)} %bitcast.2), calls=%async_computation | async-start | bytes 589824 | tf_op jit(solution)/shard_map/all_to_all | solution.py:41
  25.1 17.5 %copy-start.1 = (bf16[384,1536]{1,0:T(8,128)(2,1)}, bf16[384,1536]{1,0:T(8,128)(2,1)S(1)}, u32[]{:S(2)}) copy-start(bf16[384,1536]{1,0:T(8,128)(2,1)S(1)} %collective-permute-done.t1) | copy-start | bytes 3538948
  25.1 34.4 %collective-permute-start.2 = (bf16[384,1536]{1,0:T(8,128)(2,1)S(1)}, bf16[384,1536]{1,0:T(8,128)(2,1)}, u32[]{:S(2)}, u32[]{:S(2)}) collective-permute-start(bf16[384,1536]{1,0:T(8,128)(2,1)S(1)} %collective-permute-done.t1), channel_id=1, source_target_pairs={{0,24},{24,0},{1,25},{25,1},{2,26},{26,2},{3,27},{27,3},{4,28},{28... | collective-permute-start | bytes 3538952 | tf_op jit(solution)/shard_map/ppermute | solution.py:123
  40.2 2.5 %copy-start.2 = (bf16[384,1536]{1,0:T(8,128)(2,1)}, bf16[384,1536]{1,0:T(8,128)(2,1)S(1)}, u32[]{:S(2)}) copy-start(bf16[384,1536]{1,0:T(8,128)(2,1)S(1)} %collective-permute-done.1.t2) | copy-start | bytes 3538948
  42.6 4.2 %copy-start.8 = (s32[384]{0:T(512)S(1)}, s32[384]{0:T(512)}, u32[]{:S(2)}) copy-start(s32[384]{0:T(512)} %param.8) | copy-start | bytes 4612
  42.6 16.9 %all-to-all-start.1 = ((bf16[4,24,16,384]{3,2,1,0:T(8,128)(2,1)}), bf16[4,24,16,384]{3,2,1,0:T(8,128)(2,1)S(1)}, u32[]{:S(2)}, u32[]{:S(2)}) async-start(bf16[4,24,16,384]{3,2,1,0:T(8,128)(2,1)} %broadcast_in_dim.14), calls=%async_computation.1 | async-start | bytes 2359296 | tf_op jit(solution)/shard_map/all_to_all | solution.py:37
  46.8 4.3 %collective-permute-start.3 = (f32[384]{0:T(512)S(1)}, f32[384]{0:T(512)S(1)}, u32[]{:S(2)}, u32[]{:S(2)}) collective-permute-start(f32[384]{0:T(512)S(1)} %convert_element_type.26), channel_id=1, source_target_pairs={{0,12},{12,0},{1,13},{13,1},{2,14},{14,2},{3,15},{15,3},{4,16},{16... | collective-permute-start | bytes 4616 | tf_op jit(solution)/shard_map/ppermute | solution.py:125
  51.1 7.4 %collective-permute-start.4 = (f32[2,384]{1,0:T(2,128)S(1)}, f32[2,384]{1,0:T(2,128)S(1)}, u32[]{:S(2)}, u32[]{:S(2)}) collective-permute-start(f32[2,384]{1,0:T(2,128)S(1)} %pad_maximum_fusion.4), channel_id=1, source_target_pairs={{0,24},{24,0},{1,25},{25,1},{2,26},{26,2},{3,27},{27,3},{4,28},{28... | collective-permute-start | bytes 9224 | tf_op jit(solution)/shard_map/ppermute | solution.py:126
  59.5 1.0 copy-start
  69.2 4.2 %copy-start.3 = (bf16[4,384,192]{2,1,0:T(8,128)(2,1)S(1)}, bf16[4,384,192]{2,1,0:T(8,128)(2,1)}, u32[]{:S(2)}) copy-start(bf16[4,384,192]{2,1,0:T(8,128)(2,1)} %get-tuple-element.18) | copy-start | bytes 1769476
  69.2 12.6 %all-to-all-start.2 = ((bf16[4,24,16,192]{3,2,1,0:T(8,128)(2,1)}), bf16[4,24,16,192]{3,2,1,0:T(8,128)(2,1)S(1)}, u32[]{:S(2)}, u32[]{:S(2)}) async-start(bf16[4,24,16,192]{3,2,1,0:T(8,128)(2,1)} %get-tuple-element.19), calls=%async_computation.2 | async-start | bytes 1572864 | tf_op jit(solution)/shard_map/all_to_all | solution.py:41
  73.5 9.1 %collective-permute-start.5 = (bf16[2,384,192]{2,1,0:T(8,128)(2,1)S(1)}, bf16[2,384,192]{2,1,0:T(8,128)(2,1)S(1)}, u32[]{:S(2)}, u32[]{:S(2)}) collective-permute-start(bf16[2,384,192]{2,1,0:T(8,128)(2,1)S(1)} %slice.46), channel_id=1, source_target_pairs={{0,12},{12,0},{1,13},{13,1},{2,14},{14,2},{3,15},{15,3},{4,16},{16... | collective-permute-start | bytes 884744 | tf_op jit(solution)/shard_map/ppermute | solution.py:155
  82.6 30.1 %all-to-all-start.3 = ((bf16[24,16,192]{2,1,0:T(8,128)(2,1)}), bf16[24,16,192]{2,1,0:T(8,128)(2,1)S(1)}, u32[]{:S(2)}, u32[]{:S(2)}) async-start(bf16[24,16,192]{2,1,0:T(8,128)(2,1)} %convert_reduce_fusion), calls=%async_computation.3 | async-start | bytes 393216 | tf_op jit(solution)/shard_map/all_to_all | solution.py:41
  101.4 5.5 %collective-permute-start.6 = (bf16[2,384,192]{2,1,0:T(8,128)(2,1)S(1)}, bf16[2,384,192]{2,1,0:T(8,128)(2,1)S(1)}, u32[]{:S(2)}, u32[]{:S(2)}) collective-permute-start(bf16[2,384,192]{2,1,0:T(8,128)(2,1)S(1)} %pad_maximum_fusion), channel_id=1, source_target_pairs={{0,24},{24,0},{1,25},{25,1},{2,26},{26,2},{3,27},{27,3},{4,28},{28... | collective-permute-start | bytes 884744 | tf_op jit(solution)/shard_map/ppermute | solution.py:158
  113.5 12.8 %all-to-all-start.4 = ((bf16[4,16,384]{2,1,0:T(8,128)(2,1)}), bf16[4,16,384]{2,1,0:T(8,128)(2,1)S(1)}, u32[]{:S(2)}, u32[]{:S(2)}) async-start(bf16[4,16,384]{2,1,0:T(8,128)(2,1)} %broadcast_in_dim.16), calls=%async_computation.4 | async-start | bytes 98304 | tf_op jit(solution)/shard_map/all_to_all | solution.py:37
  127.1 15.0 %all-to-all-start.5 = ((f32[8,16,384]{2,1,0:T(8,128)}), f32[8,16,384]{2,1,0:T(8,128)S(1)}, u32[]{:S(2)}, u32[]{:S(2)}) async-start(f32[8,16,384]{2,1,0:T(8,128)} %broadcast_in_dim.17), calls=%async_computation.5 | async-start | bytes 393216 | tf_op jit(solution)/shard_map/all_to_all | solution.py:37
  137.4 5.0 %copy-start.4 = (f32[64,768]{1,0:T(8,128)S(1)}, f32[64,768]{1,0:T(8,128)}, u32[]{:S(2)}) copy-start(f32[64,768]{1,0:T(8,128)} %param.11) | copy-start | bytes 589828
  137.4 5.0 %copy-start.5 = (f32[64,768]{1,0:T(8,128)S(1)}, f32[64,768]{1,0:T(8,128)}, u32[]{:S(2)}) copy-start(f32[64,768]{1,0:T(8,128)} %param.10) | copy-start | bytes 589828
  137.4 5.0 %copy-start.6 = (f32[64,768]{1,0:T(8,128)S(1)}, f32[64,768]{1,0:T(8,128)}, u32[]{:S(2)}) copy-start(f32[64,768]{1,0:T(8,128)} %param.12) | copy-start | bytes 589828
  137.4 5.0 %copy-start.7 = (f32[64,768]{1,0:T(8,128)S(1)}, f32[64,768]{1,0:T(8,128)}, u32[]{:S(2)}) copy-start(f32[64,768]{1,0:T(8,128)} %param.13) | copy-start | bytes 589828

commit v6 on v5

--- a/solution.py
+++ b/solution.py
@@ -61,10 +61,12 @@
     ]
     for copy in loads + copies:
         copy.start()
+    token_rows = jnp.broadcast_to(mask_token[...].astype(jnp.float32), (16, mask_token.shape[1]))
+    token_rows = token_rows.astype(jnp.bfloat16)
     for load in loads:
         load.wait()
     weights = held[...].reshape(nx * shard_count * rows, 2 * quarter)
-    mask_out = jnp.dot(mask_token[...], weights, preferred_element_type=jnp.float32)
+    mask_out = jnp.dot(token_rows, weights, preferred_element_type=jnp.float32)
     mask_out = mask_out[:1, :quarter]
     masked_sum = jnp.zeros((1, quarter), jnp.float32)
     for j, copy in enumerate(copies):
@@ -81,13 +83,13 @@
         masked_sum += jnp.where(flags, difference, zero).sum(0, keepdims=True)
         kept[pl.ds(j * own, own)] = jnp.where(flags, zero, difference).astype(jnp.bfloat16)
     coarse = masked_sum.astype(jnp.bfloat16).astype(jnp.float32)
-    row = lax.broadcasted_iota(jnp.int32, (mask_token.shape[0], quarter), 0)
+    row = lax.broadcasted_iota(jnp.int32, (token_rows.shape[0], quarter), 0)
     terms = jnp.where(row == 0, coarse, jnp.where(row == 1, masked_sum - coarse, 0.0))
     by_rows = (((0,), (0,)), ((), ()))
     total = lax.dot_general(
         blocks[...], kept[...], by_rows, preferred_element_type=jnp.float32
     ) + lax.dot_general(
-        mask_token[...], terms.astype(jnp.bfloat16), by_rows, preferred_element_type=jnp.float32
+        token_rows, terms.astype(jnp.bfloat16), by_rows, preferred_element_type=jnp.float32
     )
     full = total.astype(jnp.bfloat16).reshape(shard_count, nx, rows, quarter)
     for x in range(nx):
@@ -117,13 +119,12 @@
     gathered = exchange(pieces.reshape(shard_count, part, half), SHARD)
     across = lax.ppermute(tokens, "core", SWAP)
     beside = lax.ppermute(tokens, "yl", SWAP)
-    token_rows = jnp.broadcast_to(mask_token[None], (16, depth))
-    gathered, across, token_rows = lax.optimization_barrier((gathered, across, token_rows))
+    pair = patch_mask.astype(jnp.float32)
+    pair = jnp.stack([pair, lax.ppermute(pair, "core", SWAP)])
+    gathered, across, pair = lax.optimization_barrier((gathered, across, pair))
     gathered = spread(gathered, "x", nx)
     corner = lax.ppermute(beside, "core", SWAP)
-    flags = patch_mask.astype(jnp.float32)
-    flags = jnp.stack([flags, lax.ppermute(flags, "yl", SWAP)])
-    flags = jnp.concatenate([flags, lax.ppermute(flags, "core", SWAP)])
+    flags = jnp.stack([pair, lax.ppermute(pair, "yl", SWAP)], 1).reshape(4, 1, own)
 
     any_space = pl.BlockSpec(memory_space=pl.ANY)
     features, grad = pl.pallas_call(
@@ -146,8 +147,8 @@
         across,
         corner,
         gathered,
-        flags[:, None, :],
-        token_rows,
+        flags,
+        mask_token[None],
     )
 
     grad = exchange(grad, "x")

time: 144 us -> 147 us (1.021)
  waiting for transfers between devices: 33.3 us -> 35.9 us
    all_to_all x3, waiting for transfers between devices: 12 us -> 19.3 us  [spread(): return lax.all_to_all(copies, axes, 0, 0, tiled=True)]
    ppermute x2, starting transfers between devices: 9.18 us -> 4.5 us  [the longest x1 2.59 us: step(): lax.ppermute(pair, 'yl', SWAP)]
    all_to_all x3, waiting for transfers between devices: 17.7 us -> 13.2 us  [exchange(): return lax.all_to_all(pieces, axes, 0, 0, tiled=True)]
    all_to_all x3, starting transfers between devices: 30.6 us -> 34 us  [exchange(): return lax.all_to_all(pieces, axes, 0, 0, tiled=True)]
where the time goes in v6:
time: 147 us; the launch traced here: 146 us
  starting transfers between devices  88.2 us (60%)
  waiting for transfers between devices  35.9 us (24%)
  Pallas kernels  8.54 us (6%)
  local copies, waits for them, and re-layouts  7.76 us (5%)
  other arithmetic  4.33 us (3%)
    all_to_all x3, starting transfers between devices, exchange(): return lax.all_to_all(pieces, axes, 0, 0, tiled=True)  34 us
    all_to_all x3, waiting for transfers between devices, spread(): return lax.all_to_all(copies, axes, 0, 0, tiled=True)  19.3 us
    all_to_all x3, starting transfers between devices, spread(): return lax.all_to_all(copies, axes, 0, 0, tiled=True)  19.1 us
    all_to_all x3, waiting for transfers between devices, exchange(): return lax.all_to_all(pieces, axes, 0, 0, tiled=True)  13.2 us
    ppermute x1, starting transfers between devices, step(): across = lax.ppermute(tokens, 'core', SWAP)  10.3 us
    ppermute x1, starting transfers between devices, step(): corner = lax.ppermute(beside, 'core', SWAP)  9.02 us
    pallas_call x1, Pallas kernels, step(): pl.pallas_call(products, in_specs=[any_space] * 5 + [pl.BlockSpec(memory_...  8.54 us
    ppermute x1, starting transfers between devices, step(): lax.ppermute(jnp.stack([features[2], from_side[1]]), 'core', SWAP)  4.35 us
  transfers between devices with their start and end apart: 13, of which 9 were waited for; matrix products, arithmetic and copies ran while one was open for 6% of the time, Pallas kernels for 0%

profile of v6, /device:TPU:1, one launch (start us, length us, event | category | flops | bytes accessed | tf_op | source)
XLA Modules:
  0.0 145.6 jit_solution(8382346205407762656)
XLA Ops:
  0.6 4.0 %collective-permute-start = (bf16[384,1536]{1,0:T(8,128)(2,1)}, bf16[384,1536]{1,0:T(8,128)(2,1)S(1)}, u32[]{:S(2)}, u32[]{:S(2)}) collective-permute-start(bf16[384,1536]{1,0:T(8,128)(2,1)} %t0.1), channel_id=1, source_target_pairs={{0,12},{12,0},{1,13},{13,1},{2,14},{14,2},{3,15},{15,3},{4,16},{16... | collective-permute-start | bytes 3538952 | tf_op jit(solution)/shard_map/ppermute | solution.py:121
  4.7 10.3 %collective-permute-start.1 = (bf16[384,1536]{1,0:T(8,128)(2,1)}, bf16[384,1536]{1,0:T(8,128)(2,1)S(1)}, u32[]{:S(2)}, u32[]{:S(2)}) collective-permute-start(bf16[384,1536]{1,0:T(8,128)(2,1)} %t0.1), channel_id=1, source_target_pairs={{0,24},{24,0},{1,25},{25,1},{2,26},{26,2},{3,27},{27,3},{4,28},{28... | collective-permute-start | bytes 3538952 | tf_op jit(solution)/shard_map/ppermute | solution.py:120
  15.0 0.7 dynamic_slice.11
  15.7 0.7 dynamic_slice.10
  16.5 0.1 fusion
  16.5 0.1 fusion.1
  16.6 0.1 maximum_bitcast_fusion
  16.7 0.7 broadcast_in_dim.10
  17.4 7.7 %all-to-all-start = ((bf16[24,16,384]{2,1,0:T(8,128)(2,1)}), bf16[24,16,384]{2,1,0:T(8,128)(2,1)S(1)}, u32[]{:S(2)}, u32[]{:S(2)}) async-start(bf16[24,16,384]{2,1,0:T(8,128)(2,1)} %bitcast.2), calls=%async_computation | async-start | bytes 589824 | tf_op jit(solution)/shard_map/all_to_all | solution.py:41
  25.1 0.0 collective-permute-done.t1
  25.1 9.0 %collective-permute-start.3 = (bf16[384,1536]{1,0:T(8,128)(2,1)S(1)}, bf16[384,1536]{1,0:T(8,128)(2,1)}, u32[]{:S(2)}, u32[]{:S(2)}) collective-permute-start(bf16[384,1536]{1,0:T(8,128)(2,1)S(1)} %collective-permute-done.t1), channel_id=1, source_target_pairs={{0,24},{24,0},{1,25},{25,1},{2,26},{26,2},{3,27},{27,3},{4,28},{28... | collective-permute-start | bytes 3538952 | tf_op jit(solution)/shard_map/ppermute | solution.py:126
  34.2 0.7 convert_element_type.26
  34.9 1.9 %collective-permute-start.2 = (f32[384]{0:T(512)S(1)}, f32[384]{0:T(512)S(1)}, u32[]{:S(2)}, u32[]{:S(2)}) collective-permute-start(f32[384]{0:T(512)S(1)} %convert_element_type.26), channel_id=1, source_target_pairs={{0,24},{24,0},{1,25},{25,1},{2,26},{26,2},{3,27},{27,3},{4,28},{28... | collective-permute-start | bytes 4616 | tf_op jit(solution)/shard_map/ppermute | solution.py:123
  36.8 1.1 collective-permute-done.2
  37.9 2.2 %all-to-all-done = bf16[24,16,384]{2,1,0:T(8,128)(2,1)S(1)} async-done(((bf16[24,16,384]{2,1,0:T(8,128)(2,1)}), bf16[24,16,384]{2,1,0:T(8,128)(2,1)S(1)}, u32[]{:S(2)}, u32[]{:S(2)}) %all-to-all-start) | async-done | bytes 294944 | tf_op jit(solution)/shard_map/all_to_all | solution.py:41
  40.2 1.2 broadcast_in_dim.11
  41.4 0.2 copy-done.2
  41.6 4.0 %all-to-all-start.1 = ((bf16[4,24,16,384]{3,2,1,0:T(8,128)(2,1)}), bf16[4,24,16,384]{3,2,1,0:T(8,128)(2,1)S(1)}, u32[]{:S(2)}, u32[]{:S(2)}) async-start(bf16[4,24,16,384]{3,2,1,0:T(8,128)(2,1)} %broadcast_in_dim.11), calls=%async_computation.1 | async-start | bytes 2359296 | tf_op jit(solution)/shard_map/all_to_all | solution.py:37
  45.6 2.6 %collective-permute-start.4 = (f32[2,384]{1,0:T(2,128)S(1)}, f32[2,384]{1,0:T(2,128)S(1)}, u32[]{:S(2)}, u32[]{:S(2)}) collective-permute-start(f32[2,384]{1,0:T(2,128)S(1)} %pad_maximum_fusion.4), channel_id=1, source_target_pairs={{0,12},{12,0},{1,13},{13,1},{2,14},{14,2},{3,15},{15,3},{4,16},{16... | collective-permute-start | bytes 9224 | tf_op jit(solution)/shard_map/ppermute | solution.py:127
  48.2 0.6 broadcast_in_dim.12.mask_token
  48.8 1.1 collective-permute-done.4
  50.0 0.6 reshape.61.mask_rows
  50.6 7.8 %all-to-all-done.1.gathered = bf16[4,24,16,384]{3,2,1,0:T(8,128)(2,1)S(1)} async-done(((bf16[4,24,16,384]{3,2,1,0:T(8,128)(2,1)}), bf16[4,24,16,384]{3,2,1,0:T(8,128)(2,1)S(1)}, u32[]{:S(2)}, u32[]{:S(2)}) %all-to-all-start.1) | async-done | bytes 1179680 | tf_op jit(solution)/shard_map/all_to_all | solution.py:37
  58.4 0.0 collective-permute-done.3.t3
  58.4 1.0 copy-done
  59.4 8.5 %shard_map.118 = (bf16[4,384,192]{2,1,0:T(8,128)(2,1)}, bf16[4,24,16,192]{3,2,1,0:T(8,128)(2,1)}) custom-call(bf16[384,1536]{1,0:T(8,128)(2,1)} %t0.1, bf16[384,1536]{1,0:T(8,128)(2,1)} %copy-done.1, bf16[384,1536]{1,0:T(8,128)(2,1)} %copy-done.2, bf16[384,1536]{1,0:T(8,128)(2,1)} %collective-permute-done.3.t3, bf16[4,24,16,384]{3,2,1,0:T(8,128)(2,1)} %copy-done, ...), custom_call_target="tpu_custom_call" | custom-call | tf_op jit(solution)/shard_map/pallas_call | solution.py:130
  68.0 3.6 %all-to-all-start.2 = ((bf16[4,24,16,192]{3,2,1,0:T(8,128)(2,1)}), bf16[4,24,16,192]{3,2,1,0:T(8,128)(2,1)S(1)}, u32[]{:S(2)}, u32[]{:S(2)}) async-start(bf16[4,24,16,192]{3,2,1,0:T(8,128)(2,1)} %get-tuple-element.19), calls=%async_computation.2 | async-start | bytes 1572864 | tf_op jit(solution)/shard_map/all_to_all | solution.py:41
  71.7 2.9 %collective-permute-start.5 = (bf16[2,384,192]{2,1,0:T(8,128)(2,1)S(1)}, bf16[2,384,192]{2,1,0:T(8,128)(2,1)S(1)}, u32[]{:S(2)}, u32[]{:S(2)}) collective-permute-start(bf16[2,384,192]{2,1,0:T(8,128)(2,1)S(1)} %slice.46), channel_id=1, source_target_pairs={{0,12},{12,0},{1,13},{13,1},{2,14},{14,2},{3,15},{15,3},{4,16},{16... | collective-permute-start | bytes 884744 | tf_op jit(solution)/shard_map/ppermute | solution.py:156
  74.6 5.3 %all-to-all-done.2 = bf16[4,24,16,192]{3,2,1,0:T(8,128)(2,1)S(1)} async-done(((bf16[4,24,16,192]{3,2,1,0:T(8,128)(2,1)}), bf16[4,24,16,192]{3,2,1,0:T(8,128)(2,1)S(1)}, u32[]{:S(2)}, u32[]{:S(2)}) %all-to-all-start.2) | async-done | bytes 589856 | tf_op jit(solution)/shard_map/all_to_all | solution.py:41
  79.9 0.8 convert_reduce_fusion
  80.7 22.7 %all-to-all-start.3 = ((bf16[24,16,192]{2,1,0:T(8,128)(2,1)}), bf16[24,16,192]{2,1,0:T(8,128)(2,1)S(1)}, u32[]{:S(2)}, u32[]{:S(2)}) async-start(bf16[24,16,192]{2,1,0:T(8,128)(2,1)} %convert_reduce_fusion), calls=%async_computation.3 | async-start | bytes 393216 | tf_op jit(solution)/shard_map/all_to_all | solution.py:41
  103.5 0.1 pad_maximum_fusion
  103.6 4.3 %collective-permute-start.6 = (bf16[2,384,192]{2,1,0:T(8,128)(2,1)S(1)}, bf16[2,384,192]{2,1,0:T(8,128)(2,1)S(1)}, u32[]{:S(2)}, u32[]{:S(2)}) collective-permute-start(bf16[2,384,192]{2,1,0:T(8,128)(2,1)S(1)} %pad_maximum_fusion), channel_id=1, source_target_pairs={{0,24},{24,0},{1,25},{25,1},{2,26},{26,2},{3,27},{27,3},{4,28},{28... | collective-permute-start | bytes 884744 | tf_op jit(solution)/shard_map/ppermute | solution.py:159
  107.9 0.3 maximum_select_fusion.1
  108.2 1.1 collective-permute-done.6
  109.3 5.6 %all-to-all-done.3 = bf16[24,16,192]{2,1,0:T(8,128)(2,1)S(1)} async-done(((bf16[24,16,192]{2,1,0:T(8,128)(2,1)}), bf16[24,16,192]{2,1,0:T(8,128)(2,1)S(1)}, u32[]{:S(2)}, u32[]{:S(2)}) %all-to-all-start.3) | async-done | bytes 147488 | tf_op jit(solution)/shard_map/all_to_all | solution.py:41
  115.0 0.1 pad_maximum_fusion.2
  115.0 0.6 broadcast_in_dim.13
  115.7 5.9 %all-to-all-start.4 = ((bf16[4,16,384]{2,1,0:T(8,128)(2,1)}), bf16[4,16,384]{2,1,0:T(8,128)(2,1)S(1)}, u32[]{:S(2)}, u32[]{:S(2)}) async-start(bf16[4,16,384]{2,1,0:T(8,128)(2,1)} %broadcast_in_dim.13), calls=%async_computation.4 | async-start | bytes 98304 | tf_op jit(solution)/shard_map/all_to_all | solution.py:37
  121.6 6.9 %all-to-all-done.4 = bf16[4,16,384]{2,1,0:T(8,128)(2,1)S(1)} async-done(((bf16[4,16,384]{2,1,0:T(8,128)(2,1)}), bf16[4,16,384]{2,1,0:T(8,128)(2,1)S(1)}, u32[]{:S(2)}, u32[]{:S(2)}) %all-to-all-start.4) | async-done | bytes 49184 | tf_op jit(solution)/shard_map/all_to_all | solution.py:37
  128.5 0.7 broadcast_in_dim.14
  129.2 9.2 %all-to-all-start.5 = ((f32[8,16,384]{2,1,0:T(8,128)}), f32[8,16,384]{2,1,0:T(8,128)S(1)}, u32[]{:S(2)}, u32[]{:S(2)}) async-start(f32[8,16,384]{2,1,0:T(8,128)} %broadcast_in_dim.14), calls=%async_computation.5 | async-start | bytes 393216 | tf_op jit(solution)/shard_map/all_to_all | solution.py:37
  138.4 0.3 maximum_select_fusion.2
  138.7 0.9 maximum_select_fusion
  139.6 4.6 %all-to-all-done.5 = f32[8,16,384]{2,1,0:T(8,128)S(1)} async-done(((f32[8,16,384]{2,1,0:T(8,128)}), f32[8,16,384]{2,1,0:T(8,128)S(1)}, u32[]{:S(2)}, u32[]{:S(2)}) %all-to-all-start.5) | async-done | bytes 196640 | tf_op jit(solution)/shard_map/all_to_all | solution.py:37
  144.3 0.1 copy.20
  144.4 0.1 copy.19
  144.6 1.0 multiply_add_fusion
  (35 shorter events, 0.3 us)
Async XLA Ops:
  0.6 24.5 %collective-permute-start = (bf16[384,1536]{1,0:T(8,128)(2,1)}, bf16[384,1536]{1,0:T(8,128)(2,1)S(1)}, u32[]{:S(2)}, u32[]{:S(2)}) collective-permute-start(bf16[384,1536]{1,0:T(8,128)(2,1)} %t0.1), channel_id=1, source_target_pairs={{0,12},{12,0},{1,13},{13,1},{2,14},{14,2},{3,15},{15,3},{4,16},{16... | collective-permute-start | bytes 3538952 | tf_op jit(solution)/shard_map/ppermute | solution.py:121
  4.7 35.5 %collective-permute-start.1 = (bf16[384,1536]{1,0:T(8,128)(2,1)}, bf16[384,1536]{1,0:T(8,128)(2,1)S(1)}, u32[]{:S(2)}, u32[]{:S(2)}) collective-permute-start(bf16[384,1536]{1,0:T(8,128)(2,1)} %t0.1), channel_id=1, source_target_pairs={{0,24},{24,0},{1,25},{25,1},{2,26},{26,2},{3,27},{27,3},{4,28},{28... | collective-permute-start | bytes 3538952 | tf_op jit(solution)/shard_map/ppermute | solution.py:120
  17.4 22.7 %all-to-all-start = ((bf16[24,16,384]{2,1,0:T(8,128)(2,1)}), bf16[24,16,384]{2,1,0:T(8,128)(2,1)S(1)}, u32[]{:S(2)}, u32[]{:S(2)}) async-start(bf16[24,16,384]{2,1,0:T(8,128)(2,1)} %bitcast.2), calls=%async_computation | async-start | bytes 589824 | tf_op jit(solution)/shard_map/all_to_all | solution.py:41
  25.1 16.3 %copy-start.1 = (bf16[384,1536]{1,0:T(8,128)(2,1)}, bf16[384,1536]{1,0:T(8,128)(2,1)S(1)}, u32[]{:S(2)}) copy-start(bf16[384,1536]{1,0:T(8,128)(2,1)S(1)} %collective-permute-done.t1) | copy-start | bytes 3538948
  25.1 33.3 %collective-permute-start.3 = (bf16[384,1536]{1,0:T(8,128)(2,1)S(1)}, bf16[384,1536]{1,0:T(8,128)(2,1)}, u32[]{:S(2)}, u32[]{:S(2)}) collective-permute-start(bf16[384,1536]{1,0:T(8,128)(2,1)S(1)} %collective-permute-done.t1), channel_id=1, source_target_pairs={{0,24},{24,0},{1,25},{25,1},{2,26},{26,2},{3,27},{27,3},{4,28},{28... | collective-permute-start | bytes 3538952 | tf_op jit(solution)/shard_map/ppermute | solution.py:126
  34.9 3.0 %collective-permute-start.2 = (f32[384]{0:T(512)S(1)}, f32[384]{0:T(512)S(1)}, u32[]{:S(2)}, u32[]{:S(2)}) collective-permute-start(f32[384]{0:T(512)S(1)} %convert_element_type.26), channel_id=1, source_target_pairs={{0,24},{24,0},{1,25},{25,1},{2,26},{26,2},{3,27},{27,3},{4,28},{28... | collective-permute-start | bytes 4616 | tf_op jit(solution)/shard_map/ppermute | solution.py:123
  40.2 1.4 copy-start.2
  41.4 6.8 %copy-start.8 = (bf16[1536]{0:T(1024)(128)(2,1)S(1)}, bf16[1536]{0:T(1024)(128)(2,1)}, u32[]{:S(2)}) copy-start(bf16[1536]{0:T(1024)(128)(2,1)} %param.9) | copy-start | bytes 9220
  41.6 16.8 %all-to-all-start.1 = ((bf16[4,24,16,384]{3,2,1,0:T(8,128)(2,1)}), bf16[4,24,16,384]{3,2,1,0:T(8,128)(2,1)S(1)}, u32[]{:S(2)}, u32[]{:S(2)}) async-start(bf16[4,24,16,384]{3,2,1,0:T(8,128)(2,1)} %broadcast_in_dim.11), calls=%async_computation.1 | async-start | bytes 2359296 | tf_op jit(solution)/shard_map/all_to_all | solution.py:37
  45.6 4.3 %collective-permute-start.4 = (f32[2,384]{1,0:T(2,128)S(1)}, f32[2,384]{1,0:T(2,128)S(1)}, u32[]{:S(2)}, u32[]{:S(2)}) collective-permute-start(f32[2,384]{1,0:T(2,128)S(1)} %pad_maximum_fusion.4), channel_id=1, source_target_pairs={{0,12},{12,0},{1,13},{13,1},{2,14},{14,2},{3,15},{15,3},{4,16},{16... | collective-permute-start | bytes 9224 | tf_op jit(solution)/shard_map/ppermute | solution.py:127
  58.4 1.0 copy-start
  68.0 3.7 %copy-start.3 = (bf16[4,384,192]{2,1,0:T(8,128)(2,1)S(1)}, bf16[4,384,192]{2,1,0:T(8,128)(2,1)}, u32[]{:S(2)}) copy-start(bf16[4,384,192]{2,1,0:T(8,128)(2,1)} %get-tuple-element.18) | copy-start | bytes 1769476
  68.0 11.9 %all-to-all-start.2 = ((bf16[4,24,16,192]{3,2,1,0:T(8,128)(2,1)}), bf16[4,24,16,192]{3,2,1,0:T(8,128)(2,1)S(1)}, u32[]{:S(2)}, u32[]{:S(2)}) async-start(bf16[4,24,16,192]{3,2,1,0:T(8,128)(2,1)} %get-tuple-element.19), calls=%async_computation.2 | async-start | bytes 1572864 | tf_op jit(solution)/shard_map/all_to_all | solution.py:41
  71.7 9.1 %collective-permute-start.5 = (bf16[2,384,192]{2,1,0:T(8,128)(2,1)S(1)}, bf16[2,384,192]{2,1,0:T(8,128)(2,1)S(1)}, u32[]{:S(2)}, u32[]{:S(2)}) collective-permute-start(bf16[2,384,192]{2,1,0:T(8,128)(2,1)S(1)} %slice.46), channel_id=1, source_target_pairs={{0,12},{12,0},{1,13},{13,1},{2,14},{14,2},{3,15},{15,3},{4,16},{16... | collective-permute-start | bytes 884744 | tf_op jit(solution)/shard_map/ppermute | solution.py:156
  80.7 34.2 %all-to-all-start.3 = ((bf16[24,16,192]{2,1,0:T(8,128)(2,1)}), bf16[24,16,192]{2,1,0:T(8,128)(2,1)S(1)}, u32[]{:S(2)}, u32[]{:S(2)}) async-start(bf16[24,16,192]{2,1,0:T(8,128)(2,1)} %convert_reduce_fusion), calls=%async_computation.3 | async-start | bytes 393216 | tf_op jit(solution)/shard_map/all_to_all | solution.py:41
  103.6 5.7 %collective-permute-start.6 = (bf16[2,384,192]{2,1,0:T(8,128)(2,1)S(1)}, bf16[2,384,192]{2,1,0:T(8,128)(2,1)S(1)}, u32[]{:S(2)}, u32[]{:S(2)}) collective-permute-start(bf16[2,384,192]{2,1,0:T(8,128)(2,1)S(1)} %pad_maximum_fusion), channel_id=1, source_target_pairs={{0,24},{24,0},{1,25},{25,1},{2,26},{26,2},{3,27},{27,3},{4,28},{28... | collective-permute-start | bytes 884744 | tf_op jit(solution)/shard_map/ppermute | solution.py:159
  115.7 12.8 %all-to-all-start.4 = ((bf16[4,16,384]{2,1,0:T(8,128)(2,1)}), bf16[4,16,384]{2,1,0:T(8,128)(2,1)S(1)}, u32[]{:S(2)}, u32[]{:S(2)}) async-start(bf16[4,16,384]{2,1,0:T(8,128)(2,1)} %broadcast_in_dim.13), calls=%async_computation.4 | async-start | bytes 98304 | tf_op jit(solution)/shard_map/all_to_all | solution.py:37
  129.2 15.0 %all-to-all-start.5 = ((f32[8,16,384]{2,1,0:T(8,128)}), f32[8,16,384]{2,1,0:T(8,128)S(1)}, u32[]{:S(2)}, u32[]{:S(2)}) async-start(f32[8,16,384]{2,1,0:T(8,128)} %broadcast_in_dim.14), calls=%async_computation.5 | async-start | bytes 393216 | tf_op jit(solution)/shard_map/all_to_all | solution.py:37
  139.6 5.0 %copy-start.4 = (f32[64,768]{1,0:T(8,128)S(1)}, f32[64,768]{1,0:T(8,128)}, u32[]{:S(2)}) copy-start(f32[64,768]{1,0:T(8,128)} %param.11) | copy-start | bytes 589828
  139.6 5.0 %copy-start.5 = (f32[64,768]{1,0:T(8,128)S(1)}, f32[64,768]{1,0:T(8,128)}, u32[]{:S(2)}) copy-start(f32[64,768]{1,0:T(8,128)} %param.10) | copy-start | bytes 589828
  139.6 5.0 %copy-start.6 = (f32[64,768]{1,0:T(8,128)S(1)}, f32[64,768]{1,0:T(8,128)}, u32[]{:S(2)}) copy-start(f32[64,768]{1,0:T(8,128)} %param.12) | copy-start | bytes 589828
  139.6 5.0 %copy-start.7 = (f32[64,768]{1,0:T(8,128)S(1)}, f32[64,768]{1,0:T(8,128)}, u32[]{:S(2)}) copy-start(f32[64,768]{1,0:T(8,128)} %param.13) | copy-start | bytes 589828

commit v7 on v6

--- a/solution.py
+++ b/solution.py
@@ -51,7 +51,7 @@
     t0, t1, t2, t3, gathered, mask_rows, mask_token, features, gradient, blocks, held, kept, sems
 ):
     own, quarter = features.shape[1:]
-    nx, shard_count, rows, _ = gradient.shape
+    nx, shard_count, rows, _ = gathered.shape
     loads = [
         pltpu.make_async_copy(gathered.at[x], held.at[:, x], sems.at[x]) for x in range(nx)
     ]
@@ -91,9 +91,10 @@
     ) + lax.dot_general(
         token_rows, terms.astype(jnp.bfloat16), by_rows, preferred_element_type=jnp.float32
     )
-    full = total.astype(jnp.bfloat16).reshape(shard_count, nx, rows, quarter)
+    full = total.reshape(shard_count, nx, rows, quarter)
     for x in range(nx):
-        gradient[x] = full[:, x]
+        paired = jnp.concatenate([full[:, x, : rows // 2], full[:, x, rows // 2 :]], 2)
+        gradient[x] = paired.astype(jnp.bfloat16)
 
 
 def step(tokens, patch_mask, mask_token, student_w, teacher_w, first_moment, second_moment):
@@ -133,7 +134,7 @@
         out_specs=[pl.BlockSpec(memory_space=pltpu.VMEM)] * 2,
         out_shape=[
             jax.ShapeDtypeStruct((4, own, quarter), jnp.bfloat16),
-            jax.ShapeDtypeStruct((nx, shard_count, part, quarter), jnp.bfloat16),
+            jax.ShapeDtypeStruct((nx, shard_count, part // 2, half), jnp.bfloat16),
         ],
         scratch_shapes=[
             pltpu.VMEM((4 * own, depth), jnp.bfloat16),
@@ -154,11 +155,11 @@
     grad = exchange(grad, "x")
     grad = grad.astype(jnp.float32).sum(0)
     from_side = lax.ppermute(features[1::2], "yl", SWAP)
-    grad, from_side = lax.optimization_barrier((grad, from_side))
     grad = exchange(grad.astype(jnp.bfloat16), SHARD)
     from_core = lax.ppermute(jnp.stack([features[2], from_side[1]]), "core", SWAP)
     grad, from_core = lax.optimization_barrier((grad, from_core))
-    grad = grad.astype(jnp.float32).reshape(nl, nz, part, quarter).sum(1)
+    grad = grad.astype(jnp.float32).reshape(nl, nz, part // 2, half).sum(1)
+    grad = jnp.concatenate([grad[..., :quarter], grad[..., quarter:]], 1)
     teacher_feat = halves_in_order(
         halves_in_order(features[0], from_side[0], side),
         halves_in_order(from_core[0], from_core[1], side),

time: 147 us -> 143 us (0.973)
  waiting for transfers between devices: 35.9 us -> 33.7 us
  starting transfers between devices: 88.2 us -> 86.6 us
    all_to_all x3, waiting for transfers between devices: 13.2 us -> 11 us  [exchange(): return lax.all_to_all(pieces, axes, 0, 0, tiled=True)]
where the time goes in v7:
time: 143 us; the launch traced here: 142 us
  starting transfers between devices  86.6 us (61%)
  waiting for transfers between devices  33.7 us (24%)
  Pallas kernels  8.53 us (6%)
  local copies, waits for them, and re-layouts  7.81 us (5%)
  other arithmetic  4.29 us (3%)
    all_to_all x3, starting transfers between devices, exchange(): return lax.all_to_all(pieces, axes, 0, 0, tiled=True)  32.6 us
    all_to_all x3, waiting for transfers between devices, spread(): return lax.all_to_all(copies, axes, 0, 0, tiled=True)  19.4 us
    all_to_all x3, starting transfers between devices, spread(): return lax.all_to_all(copies, axes, 0, 0, tiled=True)  18.6 us
    all_to_all x3, waiting for transfers between devices, exchange(): return lax.all_to_all(pieces, axes, 0, 0, tiled=True)  11 us
    ppermute x1, starting transfers between devices, step(): across = lax.ppermute(tokens, 'core', SWAP)  10.3 us
    ppermute x1, starting transfers between devices, step(): corner = lax.ppermute(beside, 'core', SWAP)  9.02 us
    pallas_call x1, Pallas kernels, step(): pl.pallas_call(products, in_specs=[any_space] * 5 + [pl.BlockSpec(memory_...  8.53 us
    ppermute x1, starting transfers between devices, step(): lax.ppermute(jnp.stack([features[2], from_side[1]]), 'core', SWAP)  4.64 us
  transfers between devices with their start and end apart: 13, of which 9 were waited for; matrix products, arithmetic and copies ran while one was open for 6% of the time, Pallas kernels for 0%

profile of v7, /device:TPU:1, one launch (start us, length us, event | category | flops | bytes accessed | tf_op | source)
XLA Modules:
  0.0 141.9 jit_solution(12285447672375636520)
XLA Ops:
  0.6 4.0 %collective-permute-start = (bf16[384,1536]{1,0:T(8,128)(2,1)}, bf16[384,1536]{1,0:T(8,128)(2,1)S(1)}, u32[]{:S(2)}, u32[]{:S(2)}) collective-permute-start(bf16[384,1536]{1,0:T(8,128)(2,1)} %t0.1), channel_id=1, source_target_pairs={{0,12},{12,0},{1,13},{13,1},{2,14},{14,2},{3,15},{15,3},{4,16},{16... | collective-permute-start | bytes 3538952 | tf_op jit(solution)/shard_map/ppermute | solution.py:122
  4.7 10.3 %collective-permute-start.1 = (bf16[384,1536]{1,0:T(8,128)(2,1)}, bf16[384,1536]{1,0:T(8,128)(2,1)S(1)}, u32[]{:S(2)}, u32[]{:S(2)}) collective-permute-start(bf16[384,1536]{1,0:T(8,128)(2,1)} %t0.1), channel_id=1, source_target_pairs={{0,24},{24,0},{1,25},{25,1},{2,26},{26,2},{3,27},{27,3},{4,28},{28... | collective-permute-start | bytes 3538952 | tf_op jit(solution)/shard_map/ppermute | solution.py:121
  15.0 0.7 dynamic_slice.11
  15.7 0.7 dynamic_slice.10
  16.5 0.1 fusion.1
  16.5 0.1 fusion.2
  16.6 0.1 maximum_bitcast_fusion
  16.7 0.7 broadcast_in_dim.10
  17.4 7.7 %all-to-all-start = ((bf16[24,16,384]{2,1,0:T(8,128)(2,1)}), bf16[24,16,384]{2,1,0:T(8,128)(2,1)S(1)}, u32[]{:S(2)}, u32[]{:S(2)}) async-start(bf16[24,16,384]{2,1,0:T(8,128)(2,1)} %bitcast.2), calls=%async_computation | async-start | bytes 589824 | tf_op jit(solution)/shard_map/all_to_all | solution.py:41
  25.1 0.0 collective-permute-done.t1
  25.1 9.0 %collective-permute-start.3 = (bf16[384,1536]{1,0:T(8,128)(2,1)S(1)}, bf16[384,1536]{1,0:T(8,128)(2,1)}, u32[]{:S(2)}, u32[]{:S(2)}) collective-permute-start(bf16[384,1536]{1,0:T(8,128)(2,1)S(1)} %collective-permute-done.t1), channel_id=1, source_target_pairs={{0,24},{24,0},{1,25},{25,1},{2,26},{26,2},{3,27},{27,3},{4,28},{28... | collective-permute-start | bytes 3538952 | tf_op jit(solution)/shard_map/ppermute | solution.py:127
  34.2 0.7 convert_element_type.22
  34.9 1.9 %collective-permute-start.2 = (f32[384]{0:T(512)S(1)}, f32[384]{0:T(512)S(1)}, u32[]{:S(2)}, u32[]{:S(2)}) collective-permute-start(f32[384]{0:T(512)S(1)} %convert_element_type.22), channel_id=1, source_target_pairs={{0,24},{24,0},{1,25},{25,1},{2,26},{26,2},{3,27},{27,3},{4,28},{28... | collective-permute-start | bytes 4616 | tf_op jit(solution)/shard_map/ppermute | solution.py:124
  36.8 1.1 collective-permute-done.2
  37.9 2.2 %all-to-all-done = bf16[24,16,384]{2,1,0:T(8,128)(2,1)S(1)} async-done(((bf16[24,16,384]{2,1,0:T(8,128)(2,1)}), bf16[24,16,384]{2,1,0:T(8,128)(2,1)S(1)}, u32[]{:S(2)}, u32[]{:S(2)}) %all-to-all-start) | async-done | bytes 294944 | tf_op jit(solution)/shard_map/all_to_all | solution.py:41
  40.2 1.2 broadcast_in_dim.11
  41.4 0.2 copy-done.2
  41.6 4.0 %all-to-all-start.1 = ((bf16[4,24,16,384]{3,2,1,0:T(8,128)(2,1)}), bf16[4,24,16,384]{3,2,1,0:T(8,128)(2,1)S(1)}, u32[]{:S(2)}, u32[]{:S(2)}) async-start(bf16[4,24,16,384]{3,2,1,0:T(8,128)(2,1)} %broadcast_in_dim.11), calls=%async_computation.1 | async-start | bytes 2359296 | tf_op jit(solution)/shard_map/all_to_all | solution.py:37
  45.6 2.6 %collective-permute-start.4 = (f32[2,384]{1,0:T(2,128)S(1)}, f32[2,384]{1,0:T(2,128)S(1)}, u32[]{:S(2)}, u32[]{:S(2)}) collective-permute-start(f32[2,384]{1,0:T(2,128)S(1)} %pad_maximum_fusion.4), channel_id=1, source_target_pairs={{0,12},{12,0},{1,13},{13,1},{2,14},{14,2},{3,15},{15,3},{4,16},{16... | collective-permute-start | bytes 9224 | tf_op jit(solution)/shard_map/ppermute | solution.py:128
  48.2 0.6 broadcast_in_dim.12.mask_token
  48.8 1.1 collective-permute-done.4
  49.9 0.6 reshape.61.mask_rows
  50.6 7.8 %all-to-all-done.1.gathered = bf16[4,24,16,384]{3,2,1,0:T(8,128)(2,1)S(1)} async-done(((bf16[4,24,16,384]{3,2,1,0:T(8,128)(2,1)}), bf16[4,24,16,384]{3,2,1,0:T(8,128)(2,1)S(1)}, u32[]{:S(2)}, u32[]{:S(2)}) %all-to-all-start.1) | async-done | bytes 1179680 | tf_op jit(solution)/shard_map/all_to_all | solution.py:37
  58.4 1.0 copy-done
  59.4 8.5 %shard_map.118 = (bf16[4,384,192]{2,1,0:T(8,128)(2,1)}, bf16[4,24,8,384]{3,2,1,0:T(8,128)(2,1)}) custom-call(bf16[384,1536]{1,0:T(8,128)(2,1)} %t0.1, bf16[384,1536]{1,0:T(8,128)(2,1)} %copy-done.1, bf16[384,1536]{1,0:T(8,128)(2,1)} %copy-done.2, bf16[384,1536]{1,0:T(8,128)(2,1)} %collective-permute-done.3.t3, bf16[4,24,16,384]{3,2,1,0:T(8,128)(2,1)} %copy-done, ...), custom_call_target="tpu_custom_call" | custom-call | tf_op jit(solution)/shard_map/pallas_call | solution.py:131
  67.9 3.6 %all-to-all-start.2 = ((bf16[4,24,8,384]{3,2,1,0:T(8,128)(2,1)}), bf16[4,24,8,384]{3,2,1,0:T(8,128)(2,1)S(1)}, u32[]{:S(2)}, u32[]{:S(2)}) async-start(bf16[4,24,8,384]{3,2,1,0:T(8,128)(2,1)} %get-tuple-element.17), calls=%async_computation.2 | async-start | bytes 1179648 | tf_op jit(solution)/shard_map/all_to_all | solution.py:41
  71.6 2.9 %collective-permute-start.5 = (bf16[2,384,192]{2,1,0:T(8,128)(2,1)S(1)}, bf16[2,384,192]{2,1,0:T(8,128)(2,1)S(1)}, u32[]{:S(2)}, u32[]{:S(2)}) collective-permute-start(bf16[2,384,192]{2,1,0:T(8,128)(2,1)S(1)} %slice.52), channel_id=1, source_target_pairs={{0,12},{12,0},{1,13},{13,1},{2,14},{14,2},{3,15},{15,3},{4,16},{16... | collective-permute-start | bytes 884744 | tf_op jit(solution)/shard_map/ppermute | solution.py:157
  74.6 4.3 %all-to-all-done.2 = bf16[4,24,8,384]{3,2,1,0:T(8,128)(2,1)S(1)} async-done(((bf16[4,24,8,384]{3,2,1,0:T(8,128)(2,1)}), bf16[4,24,8,384]{3,2,1,0:T(8,128)(2,1)S(1)}, u32[]{:S(2)}, u32[]{:S(2)}) %all-to-all-start.2) | async-done | bytes 589856 | tf_op jit(solution)/shard_map/all_to_all | solution.py:41
  78.8 0.8 reduce_sum.30
  79.6 21.4 %all-to-all-start.3 = ((bf16[24,8,384]{2,1,0:T(8,128)(2,1)}), bf16[24,8,384]{2,1,0:T(8,128)(2,1)S(1)}, u32[]{:S(2)}, u32[]{:S(2)}) async-start(bf16[24,8,384]{2,1,0:T(8,128)(2,1)} %reduce_sum.30), calls=%async_computation.3 | async-start | bytes 294912 | tf_op jit(solution)/shard_map/all_to_all | solution.py:41
  101.0 0.1 pad_maximum_fusion
  101.1 4.6 %collective-permute-start.6 = (bf16[2,384,192]{2,1,0:T(8,128)(2,1)S(1)}, bf16[2,384,192]{2,1,0:T(8,128)(2,1)S(1)}, u32[]{:S(2)}, u32[]{:S(2)}) collective-permute-start(bf16[2,384,192]{2,1,0:T(8,128)(2,1)S(1)} %pad_maximum_fusion), channel_id=1, source_target_pairs={{0,24},{24,0},{1,25},{25,1},{2,26},{26,2},{3,27},{27,3},{4,28},{28... | collective-permute-start | bytes 884744 | tf_op jit(solution)/shard_map/ppermute | solution.py:159
  105.7 0.3 maximum_select_fusion.1
  106.0 1.1 collective-permute-done.6
  107.1 4.5 %all-to-all-done.3 = bf16[24,8,384]{2,1,0:T(8,128)(2,1)S(1)} async-done(((bf16[24,8,384]{2,1,0:T(8,128)(2,1)}), bf16[24,8,384]{2,1,0:T(8,128)(2,1)S(1)}, u32[]{:S(2)}, u32[]{:S(2)}) %all-to-all-start.3) | async-done | bytes 147488 | tf_op jit(solution)/shard_map/all_to_all | solution.py:41
  111.6 0.1 fusion
  111.7 0.1 pad_maximum_fusion.2
  111.7 0.6 broadcast_in_dim.13
  112.4 5.9 %all-to-all-start.4 = ((bf16[4,16,384]{2,1,0:T(8,128)(2,1)}), bf16[4,16,384]{2,1,0:T(8,128)(2,1)S(1)}, u32[]{:S(2)}, u32[]{:S(2)}) async-start(bf16[4,16,384]{2,1,0:T(8,128)(2,1)} %broadcast_in_dim.13), calls=%async_computation.4 | async-start | bytes 98304 | tf_op jit(solution)/shard_map/all_to_all | solution.py:37
  118.3 6.9 %all-to-all-done.4 = bf16[4,16,384]{2,1,0:T(8,128)(2,1)S(1)} async-done(((bf16[4,16,384]{2,1,0:T(8,128)(2,1)}), bf16[4,16,384]{2,1,0:T(8,128)(2,1)S(1)}, u32[]{:S(2)}, u32[]{:S(2)}) %all-to-all-start.4) | async-done | bytes 49184 | tf_op jit(solution)/shard_map/all_to_all | solution.py:37
  125.2 0.7 broadcast_in_dim.14
  125.9 8.7 %all-to-all-start.5 = ((f32[8,16,384]{2,1,0:T(8,128)}), f32[8,16,384]{2,1,0:T(8,128)S(1)}, u32[]{:S(2)}, u32[]{:S(2)}) async-start(f32[8,16,384]{2,1,0:T(8,128)} %broadcast_in_dim.14), calls=%async_computation.5 | async-start | bytes 393216 | tf_op jit(solution)/shard_map/all_to_all | solution.py:37
  134.6 0.3 maximum_select_fusion.2
  134.9 0.9 maximum_select_fusion
  135.8 4.7 %all-to-all-done.5 = f32[8,16,384]{2,1,0:T(8,128)S(1)} async-done(((f32[8,16,384]{2,1,0:T(8,128)}), f32[8,16,384]{2,1,0:T(8,128)S(1)}, u32[]{:S(2)}, u32[]{:S(2)}) %all-to-all-start.5) | async-done | bytes 196640 | tf_op jit(solution)/shard_map/all_to_all | solution.py:37
  140.5 0.1 copy.20
  140.7 0.1 copy.19
  140.8 1.0 multiply_add_fusion
  (37 shorter events, 0.3 us)
Async XLA Ops:
  0.6 24.5 %collective-permute-start = (bf16[384,1536]{1,0:T(8,128)(2,1)}, bf16[384,1536]{1,0:T(8,128)(2,1)S(1)}, u32[]{:S(2)}, u32[]{:S(2)}) collective-permute-start(bf16[384,1536]{1,0:T(8,128)(2,1)} %t0.1), channel_id=1, source_target_pairs={{0,12},{12,0},{1,13},{13,1},{2,14},{14,2},{3,15},{15,3},{4,16},{16... | collective-permute-start | bytes 3538952 | tf_op jit(solution)/shard_map/ppermute | solution.py:122
  4.7 35.5 %collective-permute-start.1 = (bf16[384,1536]{1,0:T(8,128)(2,1)}, bf16[384,1536]{1,0:T(8,128)(2,1)S(1)}, u32[]{:S(2)}, u32[]{:S(2)}) collective-permute-start(bf16[384,1536]{1,0:T(8,128)(2,1)} %t0.1), channel_id=1, source_target_pairs={{0,24},{24,0},{1,25},{25,1},{2,26},{26,2},{3,27},{27,3},{4,28},{28... | collective-permute-start | bytes 3538952 | tf_op jit(solution)/shard_map/ppermute | solution.py:121
  17.4 22.7 %all-to-all-start = ((bf16[24,16,384]{2,1,0:T(8,128)(2,1)}), bf16[24,16,384]{2,1,0:T(8,128)(2,1)S(1)}, u32[]{:S(2)}, u32[]{:S(2)}) async-start(bf16[24,16,384]{2,1,0:T(8,128)(2,1)} %bitcast.2), calls=%async_computation | async-start | bytes 589824 | tf_op jit(solution)/shard_map/all_to_all | solution.py:41
  25.1 16.3 %copy-start.1 = (bf16[384,1536]{1,0:T(8,128)(2,1)}, bf16[384,1536]{1,0:T(8,128)(2,1)S(1)}, u32[]{:S(2)}) copy-start(bf16[384,1536]{1,0:T(8,128)(2,1)S(1)} %collective-permute-done.t1) | copy-start | bytes 3538948
  25.1 33.2 %collective-permute-start.3 = (bf16[384,1536]{1,0:T(8,128)(2,1)S(1)}, bf16[384,1536]{1,0:T(8,128)(2,1)}, u32[]{:S(2)}, u32[]{:S(2)}) collective-permute-start(bf16[384,1536]{1,0:T(8,128)(2,1)S(1)} %collective-permute-done.t1), channel_id=1, source_target_pairs={{0,24},{24,0},{1,25},{25,1},{2,26},{26,2},{3,27},{27,3},{4,28},{28... | collective-permute-start | bytes 3538952 | tf_op jit(solution)/shard_map/ppermute | solution.py:127
  34.9 3.0 %collective-permute-start.2 = (f32[384]{0:T(512)S(1)}, f32[384]{0:T(512)S(1)}, u32[]{:S(2)}, u32[]{:S(2)}) collective-permute-start(f32[384]{0:T(512)S(1)} %convert_element_type.22), channel_id=1, source_target_pairs={{0,24},{24,0},{1,25},{25,1},{2,26},{26,2},{3,27},{27,3},{4,28},{28... | collective-permute-start | bytes 4616 | tf_op jit(solution)/shard_map/ppermute | solution.py:124
  40.2 1.4 %copy-start.2 = (bf16[384,1536]{1,0:T(8,128)(2,1)}, bf16[384,1536]{1,0:T(8,128)(2,1)S(1)}, u32[]{:S(2)}) copy-start(bf16[384,1536]{1,0:T(8,128)(2,1)S(1)} %collective-permute-done.1.t2) | copy-start | bytes 3538948
  41.4 6.8 %copy-start.8 = (bf16[1536]{0:T(1024)(128)(2,1)S(1)}, bf16[1536]{0:T(1024)(128)(2,1)}, u32[]{:S(2)}) copy-start(bf16[1536]{0:T(1024)(128)(2,1)} %param.9) | copy-start | bytes 9220
  41.6 16.8 %all-to-all-start.1 = ((bf16[4,24,16,384]{3,2,1,0:T(8,128)(2,1)}), bf16[4,24,16,384]{3,2,1,0:T(8,128)(2,1)S(1)}, u32[]{:S(2)}, u32[]{:S(2)}) async-start(bf16[4,24,16,384]{3,2,1,0:T(8,128)(2,1)} %broadcast_in_dim.11), calls=%async_computation.1 | async-start | bytes 2359296 | tf_op jit(solution)/shard_map/all_to_all | solution.py:37
  45.6 4.3 %collective-permute-start.4 = (f32[2,384]{1,0:T(2,128)S(1)}, f32[2,384]{1,0:T(2,128)S(1)}, u32[]{:S(2)}, u32[]{:S(2)}) collective-permute-start(f32[2,384]{1,0:T(2,128)S(1)} %pad_maximum_fusion.4), channel_id=1, source_target_pairs={{0,12},{12,0},{1,13},{13,1},{2,14},{14,2},{3,15},{15,3},{4,16},{16... | collective-permute-start | bytes 9224 | tf_op jit(solution)/shard_map/ppermute | solution.py:128
  58.4 1.0 copy-start
  67.9 3.6 %copy-start.3 = (bf16[4,384,192]{2,1,0:T(8,128)(2,1)S(1)}, bf16[4,384,192]{2,1,0:T(8,128)(2,1)}, u32[]{:S(2)}) copy-start(bf16[4,384,192]{2,1,0:T(8,128)(2,1)} %get-tuple-element.16) | copy-start | bytes 1769476
  67.9 10.9 %all-to-all-start.2 = ((bf16[4,24,8,384]{3,2,1,0:T(8,128)(2,1)}), bf16[4,24,8,384]{3,2,1,0:T(8,128)(2,1)S(1)}, u32[]{:S(2)}, u32[]{:S(2)}) async-start(bf16[4,24,8,384]{3,2,1,0:T(8,128)(2,1)} %get-tuple-element.17), calls=%async_computation.2 | async-start | bytes 1179648 | tf_op jit(solution)/shard_map/all_to_all | solution.py:41
  71.6 29.3 %collective-permute-start.5 = (bf16[2,384,192]{2,1,0:T(8,128)(2,1)S(1)}, bf16[2,384,192]{2,1,0:T(8,128)(2,1)S(1)}, u32[]{:S(2)}, u32[]{:S(2)}) collective-permute-start(bf16[2,384,192]{2,1,0:T(8,128)(2,1)S(1)} %slice.52), channel_id=1, source_target_pairs={{0,12},{12,0},{1,13},{13,1},{2,14},{14,2},{3,15},{15,3},{4,16},{16... | collective-permute-start | bytes 884744 | tf_op jit(solution)/shard_map/ppermute | solution.py:157
  79.6 31.9 %all-to-all-start.3 = ((bf16[24,8,384]{2,1,0:T(8,128)(2,1)}), bf16[24,8,384]{2,1,0:T(8,128)(2,1)S(1)}, u32[]{:S(2)}, u32[]{:S(2)}) async-start(bf16[24,8,384]{2,1,0:T(8,128)(2,1)} %reduce_sum.30), calls=%async_computation.3 | async-start | bytes 294912 | tf_op jit(solution)/shard_map/all_to_all | solution.py:41
  101.1 6.0 %collective-permute-start.6 = (bf16[2,384,192]{2,1,0:T(8,128)(2,1)S(1)}, bf16[2,384,192]{2,1,0:T(8,128)(2,1)S(1)}, u32[]{:S(2)}, u32[]{:S(2)}) collective-permute-start(bf16[2,384,192]{2,1,0:T(8,128)(2,1)S(1)} %pad_maximum_fusion), channel_id=1, source_target_pairs={{0,24},{24,0},{1,25},{25,1},{2,26},{26,2},{3,27},{27,3},{4,28},{28... | collective-permute-start | bytes 884744 | tf_op jit(solution)/shard_map/ppermute | solution.py:159
  112.4 12.8 %all-to-all-start.4 = ((bf16[4,16,384]{2,1,0:T(8,128)(2,1)}), bf16[4,16,384]{2,1,0:T(8,128)(2,1)S(1)}, u32[]{:S(2)}, u32[]{:S(2)}) async-start(bf16[4,16,384]{2,1,0:T(8,128)(2,1)} %broadcast_in_dim.13), calls=%async_computation.4 | async-start | bytes 98304 | tf_op jit(solution)/shard_map/all_to_all | solution.py:37
  125.9 14.6 %all-to-all-start.5 = ((f32[8,16,384]{2,1,0:T(8,128)}), f32[8,16,384]{2,1,0:T(8,128)S(1)}, u32[]{:S(2)}, u32[]{:S(2)}) async-start(f32[8,16,384]{2,1,0:T(8,128)} %broadcast_in_dim.14), calls=%async_computation.5 | async-start | bytes 393216 | tf_op jit(solution)/shard_map/all_to_all | solution.py:37
  135.8 5.0 %copy-start.4 = (f32[64,768]{1,0:T(8,128)S(1)}, f32[64,768]{1,0:T(8,128)}, u32[]{:S(2)}) copy-start(f32[64,768]{1,0:T(8,128)} %param.11) | copy-start | bytes 589828
  135.8 5.0 %copy-start.5 = (f32[64,768]{1,0:T(8,128)S(1)}, f32[64,768]{1,0:T(8,128)}, u32[]{:S(2)}) copy-start(f32[64,768]{1,0:T(8,128)} %param.10) | copy-start | bytes 589828
  135.8 5.0 %copy-start.6 = (f32[64,768]{1,0:T(8,128)S(1)}, f32[64,768]{1,0:T(8,128)}, u32[]{:S(2)}) copy-start(f32[64,768]{1,0:T(8,128)} %param.12) | copy-start | bytes 589828
  135.8 5.0 %copy-start.7 = (f32[64,768]{1,0:T(8,128)S(1)}, f32[64,768]{1,0:T(8,128)}, u32[]{:S(2)}) copy-start(f32[64,768]{1,0:T(8,128)} %param.13) | copy-start | bytes 589828
